TPU v7x, 128 devices: a whole 4x4x4 slice. The times are simulated.
128 devices in a mesh: section: 4 (over x_hi, core), gx: 8 (over y, x_lo), gy: 4 (over z).
Axes of the slice: x: 4 (x_hi: 2, x_lo: 2; x = x_hi * 2 + x_lo), y: 4, z: 4, core: 2. Of those that a mesh axis runs over, the one named last changes fastest.
Arguments:
- voltage: float32 [8, 256, 1024], P(None, ('section', 'gx'), 'gy'), may hold values from -1.8 to 1.8
- capacity: float32 [8, 256, 1024], P(None, ('section', 'gx'), 'gy'), may hold values from 0.05 to 0.5
- node_class: int32 [8, 256, 1024], P(None, ('section', 'gx'), 'gy'), may hold values from 0 to 7
- via_sites: int32 [7, 256, 1024], P(None, ('section', 'gx'), 'gy'), may hold values 0 or 1
- ball_sites: int32 [256, 1024], P(('section', 'gx'), 'gy'), may hold values 0 or 1
- load_type: int32 [256, 1024], P(('section', 'gx'), 'gy'), may hold values from 0 to 15
- load_table: float32 [16, 5], replicated, may hold values from -4 to 4
Outputs:
- sections: float32 [5, 8, 256, 1024], P(None, None, ('section', 'gx'), 'gy')
- next_voltage: float32 [8, 256, 1024], P(None, ('section', 'gx'), 'gy')
Inputs may be any that keep to these rules, and one draw needn't show every extreme that they name: `node_class`: index into the table of 8 conductances. `load_type`: row of load_table.
All inputs are finite; a program needn't handle non-finite values. No bound on the sum of `via_sites` or of `ball_sites` on one device may be relied on, other than what follows from the above.
Results may differ from a plain program's by a relative error of at most 0.0003.
Values sent between devices are 32-bit elements; how exact they have to be, the bound alone decides.
No kernel may reach another device: no remote copies, remote signals or barrier semaphores. Data moves between devices by JAX's collectives and lax.ppermute only.
A program may use at most 128 MiB of HBM per device.

v0:
```python
import jax
import jax.numpy as jnp
from jax import lax
from jax.sharding import PartitionSpec as P

SECTIONS = 5
LEVELS = 3
SWEEPS = 2
COARSE_SWEEPS = 4
LOADS = 16


node_table = (0.35, 0.55, 0.8, 1.1, 1.5, 2.0, 2.7, 3.6)
via_conductance = 2.5
ball_conductance = 4.0
damping = 0.8
slab_partner = (0, 2, 1, 4, 3)


def extended(block, sides, width):
    for axis, dim in sides:
        count = lax.axis_size(axis)
        forward = [(i, i + 1) for i in range(count - 1)]
        backward = [(target, source) for source, target in forward]
        low = lax.ppermute(
            lax.slice_in_dim(block, block.shape[dim] - width, None, axis=dim), axis, forward
        )
        high = lax.ppermute(lax.slice_in_dim(block, 0, width, axis=dim), axis, backward)
        block = jnp.concatenate([low, block, high], axis=dim)
    return block


def swapped(value, axis, bit):
    mask = 2**bit
    pairs = [(source, source ^ mask) for source in range(lax.axis_size(axis))]
    return lax.ppermute(value, axis, pairs)


def pair_times(first, second):
    return (
        first[0] * second[0] - first[1] * second[1],
        first[0] * second[1] + first[1] * second[0],
    )


def pair_over(first, second):
    divisor = second[0] * second[0] + second[1] * second[1]
    return (
        (first[0] * second[0] + first[1] * second[1]) / divisor,
        (first[1] * second[0] - first[0] * second[1]) / divisor,
    )


def pair_minus(first, second):
    return (first[0] - second[0], first[1] - second[1])


def poly_value(coeffs, point):
    total = (0.0, 0.0)
    for c in reversed(coeffs):
        total = pair_times(total, point)
        total = (total[0] + c, total[1])
    return total


def poly_product(first, second):
    result = [0.0] * (len(first) + len(second) - 1)
    for i in range(len(first)):
        for j in range(len(second)):
            result[i + j] = result[i + j] + first[i] * second[j]
    return result


def poly_roots(coeffs):
    leading = coeffs[-1]
    scaled = [c / leading for c in coeffs]
    degree = len(coeffs) - 1
    guesses = []
    current = (1.0, 0.0)
    for k in range(degree):
        guesses.append(current)
        current = pair_times(current, (0.4, 0.9))
    for repeat_index in range(800):
        for k in range(degree):
            divisor = (1.0, 0.0)
            for j in range(degree):
                if j != k:
                    divisor = pair_times(divisor, pair_minus(guesses[k], guesses[j]))
            guesses[k] = pair_minus(guesses[k], pair_over(poly_value(scaled, guesses[k]), divisor))
    return guesses


def matrix_product(first, second):
    return [
        [
            sum((first[i][k] * second[k][j] for k in range(len(second))))
            for j in range(len(second[0]))
        ]
        for i in range(len(first))
    ]


def matrix_inverse(matrix):
    order = len(matrix)
    work = [list(matrix[i]) + [1.0 if i == j else 0.0 for j in range(order)] for i in range(order)]
    for column in range(order):
        pivot = column
        for i in range(column + 1, order):
            if abs(work[i][column]) > abs(work[pivot][column]):
                pivot = i
        work[column], work[pivot] = (work[pivot], work[column])
        factor = work[column][column]
        work[column] = [entry / factor for entry in work[column]]
        for i in range(order):
            if i != column:
                scale_row = work[i][column]
                work[i] = [work[i][j] - scale_row * work[column][j] for j in range(2 * order)]
    return [row[order:] for row in work]


def eigen_vector(matrix, value):
    order = len(matrix)
    size_inner = order - 1
    system = []
    for i in range(size_inner):
        row = []
        for j in range(order):
            entry = (matrix[i][j], 0.0)
            if i == j:
                entry = pair_minus(entry, value)
            row.append(entry)
        row[order - 1] = (-row[order - 1][0], -row[order - 1][1])
        system.append(row)
    for column in range(size_inner):
        pivot = column
        for i in range(column + 1, size_inner):
            left_size = system[i][column][0] ** 2 + system[i][column][1] ** 2
            right_size = system[pivot][column][0] ** 2 + system[pivot][column][1] ** 2
            if left_size > right_size:
                pivot = i
        system[column], system[pivot] = (system[pivot], system[column])
        for i in range(size_inner):
            if i != column:
                factor = pair_over(system[i][column], system[column][column])
                system[i] = [
                    pair_minus(system[i][j], pair_times(factor, system[column][j]))
                    for j in range(order)
                ]
    vector = [pair_over(system[i][order - 1], system[i][i]) for i in range(size_inner)]
    vector.append((1.0, 0.0))
    return vector


def radau_tables():
    section_count = 5
    generator = [1.0]
    for k in range(section_count - 1):
        generator = poly_product(generator, [0.0, 1.0])
    for k in range(section_count):
        generator = poly_product(generator, [-1.0, 1.0])
    for k in range(section_count - 1):
        generator = [j * generator[j] for j in range(1, len(generator))]
    abscissae = sorted((root[0] for root in poly_roots(generator)))
    vander = [[abscissae[i] ** j for j in range(section_count)] for i in range(section_count)]
    integrals = [
        [abscissae[i] ** (j + 1) / (j + 1) for j in range(section_count)]
        for i in range(section_count)
    ]
    butcher = matrix_product(integrals, matrix_inverse(vander))
    inverse = matrix_inverse(butcher)
    coeffs = [0.0] * (section_count + 1)
    coeffs[section_count] = 1.0
    current = [[0.0] * section_count for _ in range(section_count)]
    for k in range(1, section_count + 1):
        current = matrix_product(inverse, current)
        for i in range(section_count):
            current[i][i] = current[i][i] + coeffs[section_count - k + 1]
        applied = matrix_product(inverse, current)
        coeffs[section_count - k] = -sum((applied[i][i] for i in range(section_count))) / k
    eigen_values = poly_roots(coeffs)
    real_pick = 0
    for k in range(section_count):
        if abs(eigen_values[k][1]) < abs(eigen_values[real_pick][1]):
            real_pick = k
    upper_half = [k for k in range(section_count) if eigen_values[k][1] > 1e-09]
    upper_half = sorted(upper_half, key=lambda k: -eigen_values[k][0])
    columns = [[entry[0] for entry in eigen_vector(inverse, (eigen_values[real_pick][0], 0.0))]]
    for k in upper_half:
        vector = eigen_vector(inverse, eigen_values[k])
        columns.append([entry[0] for entry in vector])
        columns.append([entry[1] for entry in vector])
    transform = [[columns[j][i] for j in range(section_count)] for i in range(section_count)]
    inverse_transform = matrix_inverse(transform)
    blocks = matrix_product(matrix_product(inverse_transform, inverse), transform)
    diagonal = [blocks[k][k] for k in range(section_count)]
    coupling = [
        blocks[k][slab_partner[k]] if slab_partner[k] != k else 0.0 for k in range(section_count)
    ]
    return (transform, inverse_transform, diagonal, coupling)


def lookup(classes, values_table):
    result = jnp.zeros(classes.shape, jnp.float32)
    for k in range(len(values_table)):
        result = result + jnp.where(classes == k, jnp.float32(values_table[k]), jnp.float32(0.0))
    return result


def series(near_side, far_side):
    return 2.0 * near_side * far_side / (near_side + far_side)


def branch_set(conduct, padded, via_sites, ball_sites, capacity):
    lower_x = series(padded[:, :-2, 1:-1], conduct)
    upper_x = series(conduct, padded[:, 2:, 1:-1])
    lower_y = series(padded[:, 1:-1, :-2], conduct)
    upper_y = series(conduct, padded[:, 1:-1, 2:])
    vertical = jnp.where(via_sites == 1, jnp.float32(via_conductance), jnp.float32(0.0))
    ground = jnp.where(ball_sites == 1, jnp.float32(ball_conductance), jnp.float32(0.0))
    return (capacity, lower_x, upper_x, lower_y, upper_y, vertical, ground)


def layer_terms(vertical, ground, layers):
    zero_plane = jnp.zeros((1,) + vertical.shape[1:], jnp.float32)
    via_above = jnp.concatenate([vertical, zero_plane], axis=0)
    via_below = jnp.concatenate([zero_plane, vertical], axis=0)
    grounded = jnp.concatenate(
        [ground[None], jnp.zeros((layers - 1,) + ground.shape, jnp.float32)], axis=0
    )
    return (via_above, via_below, grounded)


def network(voltage, padded_voltage, branches):
    capacity, lower_x, upper_x, lower_y, upper_y, vertical, ground = branches
    via_above, via_below, grounded = layer_terms(vertical, ground, voltage.shape[0])
    branch_total = lower_x + upper_x + lower_y + upper_y + via_above + via_below + grounded
    zero_plane = jnp.zeros((1,) + voltage.shape[1:], jnp.float32)
    volt_above = jnp.concatenate([voltage[1:], zero_plane], axis=0)
    volt_below = jnp.concatenate([zero_plane, voltage[:-1]], axis=0)
    inflow = (
        upper_x * padded_voltage[:, 2:, 1:-1]
        + lower_x * padded_voltage[:, :-2, 1:-1]
        + upper_y * padded_voltage[:, 1:-1, 2:]
        + lower_y * padded_voltage[:, 1:-1, :-2]
        + via_above * volt_above
        + via_below * volt_below
    )
    return branch_total * voltage - inflow


def section_sources(load_type, load_table):
    surface = jnp.zeros((SECTIONS,) + load_type.shape, jnp.float32)
    for t in range(LOADS):
        surface = surface + jnp.where(
            (load_type == t)[None], load_table[t][:, None, None], jnp.float32(0.0)
        )
    return surface


def pair_rows(array):
    extent = array.shape
    return array.reshape(extent[:-2] + (extent[-2] // 2, 2, extent[-1])).sum(axis=-2)


def pair_cols(array):
    extent = array.shape
    return array.reshape(extent[:-1] + (extent[-1] // 2, 2)).sum(axis=-1)


def take_rows(array, offset):
    extent = array.shape
    return array.reshape(extent[:-2] + (extent[-2] // 2, 2, extent[-1]))[..., offset, :]


def take_cols(array, offset):
    extent = array.shape
    return array.reshape(extent[:-1] + (extent[-1] // 2, 2))[..., offset]


def block_sum(array):
    return pair_cols(pair_rows(array))


def coarsen(branches):
    capacity, lower_x, upper_x, lower_y, upper_y, vertical, ground = branches
    return (
        block_sum(capacity),
        pair_cols(take_rows(lower_x, 0)),
        pair_cols(take_rows(upper_x, 1)),
        pair_rows(take_cols(lower_y, 0)),
        pair_rows(take_cols(upper_y, 1)),
        block_sum(vertical),
        block_sum(ground),
    )


def level_operator(branches, shifts, couple, partner):
    capacity, lower_x, upper_x, lower_y, upper_y, vertical, ground = branches
    via_above, via_below, grounded = layer_terms(vertical, ground, capacity.shape[0])
    branch_total = lower_x + upper_x + lower_y + upper_y + via_above + via_below + grounded
    diagonal = shifts[:, None, None, None] * capacity + branch_total
    coupled = couple[:, None, None, None] * capacity
    diagonal_mate = jnp.stack([diagonal[p] for p in partner])
    coupled_mate = jnp.stack([coupled[p] for p in partner])
    determinant = diagonal * diagonal_mate - coupled * coupled_mate
    self_weight = diagonal_mate / determinant
    mate_weight = -coupled / determinant
    return (
        lower_x,
        upper_x,
        lower_y,
        upper_y,
        via_above,
        via_below,
        diagonal,
        coupled,
        self_weight,
        mate_weight,
        partner,
    )


def operate(iterate, operator, neighbours):
    (
        lower_x,
        upper_x,
        lower_y,
        upper_y,
        via_above,
        via_below,
        diagonal,
        coupled,
        self_weight,
        mate_weight,
        partner,
    ) = operator
    upper_rows, lower_rows, right_cols, left_cols = neighbours
    zero_plane = jnp.zeros_like(iterate[:, :1])
    from_above = jnp.concatenate([iterate[:, 1:], zero_plane], axis=1)
    from_below = jnp.concatenate([zero_plane, iterate[:, :-1]], axis=1)
    inflow = (
        upper_x * upper_rows
        + lower_x * lower_rows
        + upper_y * right_cols
        + lower_y * left_cols
        + via_above * from_above
        + via_below * from_below
    )
    partner_field = jnp.stack([iterate[p] for p in partner])
    return diagonal * iterate - inflow + coupled * partner_field


def relax(iterate, source, operator, neighbour_fn):
    partner = operator[-1]
    if iterate is None:
        residual = source
    else:
        residual = source - operate(iterate, operator, neighbour_fn(iterate))
    mate_values = jnp.stack([residual[p] for p in partner])
    update = operator[8] * residual + operator[9] * mate_values
    if iterate is None:
        return damping * update
    return iterate + damping * update


def vcycle(operators, level_index, iterate, source, neighbour_fn):
    operator = operators[level_index]
    if level_index == len(operators) - 1:
        for _ in range(COARSE_SWEEPS):
            iterate = relax(iterate, source, operator, neighbour_fn)
        return iterate
    for _ in range(SWEEPS):
        iterate = relax(iterate, source, operator, neighbour_fn)
    residual = source - operate(iterate, operator, neighbour_fn(iterate))
    coarse = vcycle(operators, level_index + 1, None, block_sum(residual), neighbour_fn)
    iterate = iterate + jnp.repeat(jnp.repeat(coarse, 2, axis=2), 2, axis=3)
    for _ in range(SWEEPS):
        iterate = relax(iterate, source, operator, neighbour_fn)
    return iterate


def solve(source, branches, shifts, couple, partner, neighbour_fn):
    operators = []
    for level_index in range(LEVELS):
        if level_index > 0:
            branches = coarsen(branches)
        operators.append(level_operator(branches, shifts, couple, partner))
    iterate = vcycle(operators, 0, None, source, neighbour_fn)
    iterate = vcycle(operators, 0, iterate, source, neighbour_fn)
    return iterate


def paired_faces(iterate):
    row_padded = extended(iterate, ((("section", "gx"), 2),), 1)
    leading = lax.axis_index("gy") // 2 == 0
    edge_column = jnp.where(leading, iterate[..., -1], iterate[..., 0])
    facing = swapped(edge_column, "gy", 1)
    blank_rim = jnp.zeros_like(facing)
    right_rim = jnp.where(leading, facing, blank_rim)
    left_rim = jnp.where(leading, blank_rim, facing)
    right_cols = jnp.concatenate([iterate[..., 1:], right_rim[..., None]], axis=-1)
    left_cols = jnp.concatenate([left_rim[..., None], iterate[..., :-1]], axis=-1)
    return (row_padded[:, :, 2:], row_padded[:, :, :-2], right_cols, left_cols)


def join_halves(left_half, own_array, their_array):
    return jnp.where(
        left_half,
        jnp.concatenate([own_array, their_array], axis=-1),
        jnp.concatenate([their_array, own_array], axis=-1),
    )


def local(voltage, capacity, node_class, via_sites, ball_sites, load_type, load_table):
    transform, inverse_transform, diagonal_np, coupling_np = radau_tables()
    conduct = lookup(node_class, node_table)
    stacked = jnp.stack([voltage, conduct])
    padded_both = extended(stacked, ((("section", "gx"), 2), ("gy", 3)), 1)
    branches = branch_set(conduct, padded_both[1], via_sites, ball_sites, capacity)
    leakage = network(voltage, padded_both[0], branches)
    surface = section_sources(load_type, load_table)
    forcing = jnp.concatenate(
        [
            jnp.broadcast_to(-leakage[:-1], (SECTIONS,) + leakage[:-1].shape),
            (surface - leakage[-1])[:, None],
        ],
        axis=1,
    )
    transformed = jnp.einsum(
        "jk,klrc->jlrc",
        jnp.asarray(inverse_transform, jnp.float32),
        forcing,
        precision=lax.Precision.HIGHEST,
    )
    left_half = lax.axis_index("gy") % 2 == 0
    own_complex = jnp.where(left_half, transformed[1:3], transformed[3:5])
    other_complex = jnp.where(left_half, transformed[3:5], transformed[1:3])
    outgoing = jnp.concatenate([transformed[:1], other_complex], axis=0)
    own_capacity, lower_x, upper_x, lower_y, upper_y, vertical, ground = branches
    received = swapped(
        (outgoing, own_capacity, lower_x, upper_x, lower_y, upper_y, vertical, ground), "gy", 0
    )
    paired = tuple(
        (
            join_halves(left_half, own_array, their_array)
            for own_array, their_array in zip(branches, received[1:])
        )
    )
    paired_source = join_halves(
        left_half, jnp.concatenate([transformed[:1], own_complex], axis=0), received[0]
    )
    shifts = jnp.where(
        left_half,
        jnp.asarray(
            [float(diagonal_np[0]), float(diagonal_np[1]), float(diagonal_np[2])], jnp.float32
        ),
        jnp.asarray(
            [float(diagonal_np[0]), float(diagonal_np[3]), float(diagonal_np[4])], jnp.float32
        ),
    )
    couple = jnp.where(
        left_half,
        jnp.asarray([0.0, float(coupling_np[1]), float(coupling_np[2])], jnp.float32),
        jnp.asarray([0.0, float(coupling_np[3]), float(coupling_np[4])], jnp.float32),
    )
    joint_field = solve(paired_source, paired, shifts, couple, (0, 2, 1), paired_faces)
    half_width = capacity.shape[-1]
    own_part = jnp.where(left_half, joint_field[..., :half_width], joint_field[..., half_width:])
    partner_part = jnp.where(
        left_half, joint_field[..., half_width:], joint_field[..., :half_width]
    )
    returned = swapped(partner_part[1:3], "gy", 0)
    solution = jnp.where(
        left_half,
        jnp.concatenate([own_part, returned], axis=0),
        jnp.concatenate([own_part[:1], returned, own_part[1:3]], axis=0),
    )
    sections = jnp.einsum(
        "jk,klrc->jlrc",
        jnp.asarray(transform, jnp.float32),
        solution,
        precision=lax.Precision.HIGHEST,
    )
    return (sections, voltage + sections[SECTIONS - 1])


def solution(mesh):
    return jax.shard_map(
        local,
        mesh=mesh,
        in_specs=(
            P(None, ("section", "gx"), "gy"),
            P(None, ("section", "gx"), "gy"),
            P(None, ("section", "gx"), "gy"),
            P(None, ("section", "gx"), "gy"),
            P(("section", "gx"), "gy"),
            P(("section", "gx"), "gy"),
            P(),
        ),
        out_specs=(P(None, None, ("section", "gx"), "gy"), P(None, ("section", "gx"), "gy")),
        check_vma=False,
    )
```

profile of v0, /device:TPU:1, one launch (start us, length us, event | category | flops | bytes accessed | tf_op | source)
XLA Modules:
  0.0 598.1 jit_solution(8353342889147651853)
XLA Ops:
  8.8 5.2 collective-permute-start.2
  28.4 3.7 collective-permute-done.4
  77.4 14.4 %fusion.99 = (f32[3,8,8,512]{3,0,2,1:T(4,128)S(1)}, f32[3,8,8,512]{3,0,2,1:T(4,128)S(1)}, f32[3,8,8,512]{3,0,2,1:T(4,128)S(1)}) fusion(f32[1,8,8,512]{3,0,2,1:T(1,128)S(1)} %get-tuple-element.214, f32[1,8,8,512]{3,0,2,1:T(1,128)S(1)} %get-tuple-element.213, f32[1,8,8,512]{3,0,2,1:T(1,128)S(1)} %get-tuple-element.212, ...), kind=kLoop, calls=%fused_computation.137 | loop fusion | flops 2359296 | bytes 3014681 | tf_op jit(solution)/shard_map/mul | solution.py:362
  99.0 7.3 %collective-permute-start.12 = (f32[3,8,1,512]{3,0,2,1:T(4,128)}, f32[3,8,1,512]{3,0,2,1:T(4,128)}, u32[]{:S(2)}, u32[]{:S(2)}) collective-permute-start(f32[3,8,1,512]{3,0,2,1:T(4,128)} %get-tuple-element.204), channel_id=1, source_target_pairs={{4,0},{8,4},{12,8},{16,12},{20,16},{24,20},{28,24},{32,28},{36,32}... | collective-permute-start | bytes 147464 | tf_op jit(solution)/shard_map/ppermute | solution.py:28
  127.7 3.7 collective-permute-start.15
  139.4 3.7 fusion.7
  146.6 7.0 %reduce_sum.263 = f32[3,8,4,256]{1,3,2,0:T(8,128)} reduce(f32[3,8,4,256,2]{1,4,3,2,0:T(2,128)} %bitcast.188, f32[]{:T(128)} %constant.139.clone.1), dimensions={4}, to_apply=%region_11.12 | reduce | flops 24576 | bytes 294916 | tf_op jit(solution)/shard_map/reduce_sum | solution.py:267
  159.6 3.7 collective-permute-start.18
  177.3 3.9 collective-permute-start.21
  184.7 3.9 collective-permute-done.22
  216.7 3.9 collective-permute-start.27
  238.8 3.8 collective-permute-done.31
  271.6 3.9 collective-permute-start.36
  279.0 3.9 collective-permute-done.37
  286.5 4.9 broadcast_in_dim.705
  291.5 5.4 copy.4449
  329.2 3.7 collective-permute-start.42
  354.4 3.7 collective-permute-start.45
  377.3 3.9 collective-permute-start.48
  402.6 3.7 collective-permute-start.51
  414.4 3.7 fusion.17
  421.6 7.1 %reduce_sum.277 = f32[3,8,4,256]{1,3,2,0:T(8,128)} reduce(f32[3,8,4,256,2]{1,4,3,2,0:T(2,128)} %bitcast.189, f32[]{:T(128)} %constant.139.clone.1), dimensions={4}, to_apply=%region_25.26 | reduce | flops 24576 | bytes 294916 | tf_op jit(solution)/shard_map/reduce_sum | solution.py:267
  432.4 4.0 collective-permute-start.54
  438.6 5.1 collective-permute-done.55
  471.7 3.7 collective-permute-done.61
  484.2 3.8 collective-permute-done.64
  494.3 3.8 collective-permute-done.67
  510.2 3.3 collective-permute-start.70
  527.4 3.5 collective-permute-done.73
  534.3 4.9 broadcast_in_dim.733
  539.2 4.7 copy.4501
  575.3 3.7 collective-permute-start.78
  (709 shorter events, 445.5 us)
Async XLA Ops:
  1.4 19.9 %collective-permute-start.10 = (f32[8,256]{1,0:T(8,128)S(1)}, f32[8,256]{1,0:T(8,128)S(1)}, u32[]{:S(2)}, u32[]{:S(2)}) collective-permute-start(f32[8,256]{1,0:T(8,128)S(1)} %get-tuple-element.443), channel_id=1, source_target_pairs={{0,1},{1,0},{2,3},{3,2},{4,5},{5,4},{6,7},{7,6},{8,9},{9,8},{10,11... | collective-permute-start | bytes 24584 | tf_op jit(solution)/shard_map/ppermute | solution.py:36
  5.7 16.3 %collective-permute-start.1 = (f32[2,8,1,256]{3,2,1,0:T(1,128)S(1)}, f32[2,8,1,256]{3,2,1,0:T(1,128)S(1)}, u32[]{:S(2)}, u32[]{:S(2)}) collective-permute-start(f32[2,8,1,256]{3,2,1,0:T(1,128)S(1)} %get-tuple-element.223), channel_id=1, source_target_pairs={{0,4},{4,8},{8,12},{12,16},{16,20},{20,24},{24,28},{28,32},{32,36}... | collective-permute-start | bytes 49160 | tf_op jit(solution)/shard_map/ppermute | solution.py:25
  8.8 13.1 %collective-permute-start.2 = (f32[2,8,1,256]{3,2,1,0:T(1,128)S(1)}, f32[2,8,1,256]{3,2,1,0:T(1,128)S(1)}, u32[]{:S(2)}, u32[]{:S(2)}) collective-permute-start(f32[2,8,1,256]{3,2,1,0:T(1,128)S(1)} %get-tuple-element.224), channel_id=1, source_target_pairs={{4,0},{8,4},{12,8},{16,12},{20,16},{24,20},{28,24},{32,28},{36,32}... | collective-permute-start | bytes 49160 | tf_op jit(solution)/shard_map/ppermute | solution.py:28
  14.9 27.2 %collective-permute-start.9 = (f32[7,8,256]{2,1,0:T(8,128)S(1)}, f32[7,8,256]{2,1,0:T(8,128)S(1)}, u32[]{:S(2)}, u32[]{:S(2)}) collective-permute-start(f32[7,8,256]{2,1,0:T(8,128)S(1)} %compare_select_fusion), channel_id=1, source_target_pairs={{0,1},{1,0},{2,3},{3,2},{4,5},{5,4},{6,7},{7,6},{8,9},{9,8},{10,11... | collective-permute-start | bytes 172040 | tf_op jit(solution)/shard_map/ppermute | solution.py:36
  14.9 33.3 %collective-permute-start = (f32[8,8,256]{2,1,0:T(8,128)}, f32[8,8,256]{2,1,0:T(8,128)S(1)}, u32[]{:S(2)}, u32[]{:S(2)}) collective-permute-start(f32[8,8,256]{2,1,0:T(8,128)} %param.14), channel_id=1, source_target_pairs={{0,1},{1,0},{2,3},{3,2},{4,5},{5,4},{6,7},{7,6},{8,9},{9,8},{10,11... | collective-permute-start | bytes 196616 | tf_op jit(solution)/shard_map/ppermute | solution.py:36
  34.4 29.9 %collective-permute-start.5 = (f32[8,8,256]{2,1,0:T(8,128)}, f32[8,8,256]{2,1,0:T(8,128)}, u32[]{:S(2)}, u32[]{:S(2)}) collective-permute-start(f32[8,8,256]{2,1,0:T(8,128)} %get-tuple-element.98), channel_id=1, source_target_pairs={{0,1},{1,0},{2,3},{3,2},{4,5},{5,4},{6,7},{7,6},{8,9},{9,8},{10,11... | collective-permute-start | bytes 196616 | tf_op jit(solution)/shard_map/ppermute | solution.py:36
  35.9 18.5 %collective-permute-start.8 = (f32[8,8,256]{2,1,0:T(8,128)S(1)}, f32[8,8,256]{2,1,0:T(8,128)S(1)}, u32[]{:S(2)}, u32[]{:S(2)}) collective-permute-start(f32[8,8,256]{2,1,0:T(8,128)S(1)} %get-tuple-element.99), channel_id=1, source_target_pairs={{0,1},{1,0},{2,3},{3,2},{4,5},{5,4},{6,7},{7,6},{8,9},{9,8},{10,11... | collective-permute-start | bytes 196616 | tf_op jit(solution)/shard_map/ppermute | solution.py:36
  38.9 24.5 %collective-permute-start.6 = (f32[8,8,256]{2,1,0:T(8,128)S(1)}, f32[8,8,256]{2,1,0:T(8,128)}, u32[]{:S(2)}, u32[]{:S(2)}) collective-permute-start(f32[8,8,256]{2,1,0:T(8,128)S(1)} %get-tuple-element.97), channel_id=1, source_target_pairs={{0,1},{1,0},{2,3},{3,2},{4,5},{5,4},{6,7},{7,6},{8,9},{9,8},{10,11... | collective-permute-start | bytes 196616 | tf_op jit(solution)/shard_map/ppermute | solution.py:36
  42.1 13.6 %collective-permute-start.7 = (f32[8,8,256]{2,1,0:T(8,128)S(1)}, f32[8,8,256]{2,1,0:T(8,128)S(1)}, u32[]{:S(2)}, u32[]{:S(2)}) collective-permute-start(f32[8,8,256]{2,1,0:T(8,128)S(1)} %get-tuple-element.100), channel_id=1, source_target_pairs={{0,1},{1,0},{2,3},{3,2},{4,5},{5,4},{6,7},{7,6},{8,9},{9,8},{10,11... | collective-permute-start | bytes 196616 | tf_op jit(solution)/shard_map/ppermute | solution.py:36
  48.2 28.6 %collective-permute-start.11 = (f32[3,8,8,256]{3,0,2,1:T(4,128)}, f32[3,8,8,256]{3,0,2,1:T(4,128)S(1)}, u32[]{:S(2)}, u32[]{:S(2)}) collective-permute-start(f32[3,8,8,256]{3,0,2,1:T(4,128)} %pad_maximum_fusion.25), channel_id=1, source_target_pairs={{0,1},{1,0},{2,3},{3,2},{4,5},{5,4},{6,7},{7,6},{8,9},{9,8},{10,11... | collective-permute-start | bytes 589832 | tf_op jit(solution)/shard_map/ppermute | solution.py:36
  97.7 10.4 %collective-permute-start.14 = (f32[3,8,8]{2,1,0:T(8,128)}, f32[3,8,8]{2,1,0:T(8,128)S(1)}, u32[]{:S(2)}, u32[]{:S(2)}) collective-permute-start(f32[3,8,8]{2,1,0:T(8,128)} %bitcast.231), channel_id=1, source_target_pairs={{0,2},{1,3},{2,0},{3,1},{4,6},{5,7},{6,4},{7,5},{8,10},{9,11},{10,... | collective-permute-start | bytes 2312 | tf_op jit(solution)/shard_map/ppermute | solution.py:36
  99.0 13.0 %collective-permute-start.12 = (f32[3,8,1,512]{3,0,2,1:T(4,128)}, f32[3,8,1,512]{3,0,2,1:T(4,128)}, u32[]{:S(2)}, u32[]{:S(2)}) collective-permute-start(f32[3,8,1,512]{3,0,2,1:T(4,128)} %get-tuple-element.204), channel_id=1, source_target_pairs={{4,0},{8,4},{12,8},{16,12},{20,16},{24,20},{28,24},{32,28},{36,32}... | collective-permute-start | bytes 147464 | tf_op jit(solution)/shard_map/ppermute | solution.py:28
  124.3 9.0 %collective-permute-start.17 = (f32[3,8,8]{2,1,0:T(8,128)}, f32[3,8,8]{2,1,0:T(8,128)S(1)}, u32[]{:S(2)}, u32[]{:S(2)}) collective-permute-start(f32[3,8,8]{2,1,0:T(8,128)} %bitcast.232), channel_id=1, source_target_pairs={{0,2},{1,3},{2,0},{3,1},{4,6},{5,7},{6,4},{7,5},{8,10},{9,11},{10,... | collective-permute-start | bytes 2312 | tf_op jit(solution)/shard_map/ppermute | solution.py:36
  127.7 9.4 %collective-permute-start.15 = (f32[3,8,1,512]{3,0,2,1:T(4,128)}, f32[3,8,1,512]{3,0,2,1:T(4,128)}, u32[]{:S(2)}, u32[]{:S(2)}) collective-permute-start(f32[3,8,1,512]{3,0,2,1:T(4,128)} %get-tuple-element.192), channel_id=1, source_target_pairs={{4,0},{8,4},{12,8},{16,12},{20,16},{24,20},{28,24},{32,28},{36,32}... | collective-permute-start | bytes 147464 | tf_op jit(solution)/shard_map/ppermute | solution.py:28
  159.6 9.2 %collective-permute-start.18 = (f32[3,8,1,256]{3,1,2,0:T(8,128)}, f32[3,8,1,256]{3,1,2,0:T(8,128)}, u32[]{:S(2)}, u32[]{:S(2)}) collective-permute-start(f32[3,8,1,256]{3,1,2,0:T(8,128)} %get-tuple-element.318), channel_id=1, source_target_pairs={{4,0},{8,4},{12,8},{16,12},{20,16},{24,20},{28,24},{32,28},{36,32}... | collective-permute-start | bytes 73736 | tf_op jit(solution)/shard_map/ppermute | solution.py:28
  174.6 8.6 %collective-permute-start.23 = (f32[3,8,4]{1,2,0:T(4,128)S(1)}, f32[3,8,4]{1,2,0:T(4,128)S(1)}, u32[]{:S(2)}, u32[]{:S(2)}) collective-permute-start(f32[3,8,4]{1,2,0:T(4,128)S(1)} %fusion.254), channel_id=1, source_target_pairs={{0,2},{1,3},{2,0},{3,1},{4,6},{5,7},{6,4},{7,5},{8,10},{9,11},{10,... | collective-permute-start | bytes 1160 | tf_op jit(solution)/shard_map/ppermute | solution.py:36
  200.1 8.7 %collective-permute-start.24 = (f32[3,8,1,128]{3,1,2,0:T(8,128)}, f32[3,8,1,128]{3,1,2,0:T(8,128)}, u32[]{:S(2)}, u32[]{:S(2)}) collective-permute-start(f32[3,8,1,128]{3,1,2,0:T(8,128)} %get-tuple-element.409), channel_id=1, source_target_pairs={{4,0},{8,4},{12,8},{16,12},{20,16},{24,20},{28,24},{32,28},{36,32}... | collective-permute-start | bytes 36872 | tf_op jit(solution)/shard_map/ppermute | solution.py:28
  214.0 8.6 %collective-permute-start.29 = (f32[3,8,2]{1,2,0:T(2,128)S(1)}, f32[3,8,2]{1,2,0:T(2,128)S(1)}, u32[]{:S(2)}, u32[]{:S(2)}) collective-permute-start(f32[3,8,2]{1,2,0:T(2,128)S(1)} %fusion.306), channel_id=1, source_target_pairs={{0,2},{1,3},{2,0},{3,1},{4,6},{5,7},{6,4},{7,5},{8,10},{9,11},{10,... | collective-permute-start | bytes 584 | tf_op jit(solution)/shard_map/ppermute | solution.py:36
  216.7 8.6 %collective-permute-start.27 = (f32[3,8,1,128]{3,1,2,0:T(8,128)}, f32[3,8,1,128]{3,1,2,0:T(8,128)}, u32[]{:S(2)}, u32[]{:S(2)}) collective-permute-start(f32[3,8,1,128]{3,1,2,0:T(8,128)} %get-tuple-element.397), channel_id=1, source_target_pairs={{4,0},{8,4},{12,8},{16,12},{20,16},{24,20},{28,24},{32,28},{36,32}... | collective-permute-start | bytes 36872 | tf_op jit(solution)/shard_map/ppermute | solution.py:28
  254.3 9.0 %collective-permute-start.35 = (f32[3,8,4]{1,2,0:T(4,128)S(1)}, f32[3,8,4]{1,2,0:T(4,128)S(1)}, u32[]{:S(2)}, u32[]{:S(2)}) collective-permute-start(f32[3,8,4]{1,2,0:T(4,128)S(1)} %fusion.253), channel_id=1, source_target_pairs={{0,2},{1,3},{2,0},{3,1},{4,6},{5,7},{6,4},{7,5},{8,10},{9,11},{10,... | collective-permute-start | bytes 1160 | tf_op jit(solution)/shard_map/ppermute | solution.py:36
  258.0 8.8 %collective-permute-start.33 = (f32[3,8,1,256]{3,1,2,0:T(8,128)}, f32[3,8,1,256]{3,1,2,0:T(8,128)}, u32[]{:S(2)}, u32[]{:S(2)}) collective-permute-start(f32[3,8,1,256]{3,1,2,0:T(8,128)} %get-tuple-element.297), channel_id=1, source_target_pairs={{4,0},{8,4},{12,8},{16,12},{20,16},{24,20},{28,24},{32,28},{36,32}... | collective-permute-start | bytes 73736 | tf_op jit(solution)/shard_map/ppermute | solution.py:28
  304.0 8.7 %collective-permute-start.41 = (f32[3,8,8]{2,1,0:T(8,128)}, f32[3,8,8]{2,1,0:T(8,128)S(1)}, u32[]{:S(2)}, u32[]{:S(2)}) collective-permute-start(f32[3,8,8]{2,1,0:T(8,128)} %bitcast.233), channel_id=1, source_target_pairs={{0,2},{1,3},{2,0},{3,1},{4,6},{5,7},{6,4},{7,5},{8,10},{9,11},{10,... | collective-permute-start | bytes 2312 | tf_op jit(solution)/shard_map/ppermute | solution.py:36
  307.4 9.0 %collective-permute-start.39 = (f32[3,8,1,512]{3,0,2,1:T(4,128)}, f32[3,8,1,512]{3,0,2,1:T(4,128)}, u32[]{:S(2)}, u32[]{:S(2)}) collective-permute-start(f32[3,8,1,512]{3,0,2,1:T(4,128)} %get-tuple-element.183), channel_id=1, source_target_pairs={{4,0},{8,4},{12,8},{16,12},{20,16},{24,20},{28,24},{32,28},{36,32}... | collective-permute-start | bytes 147464 | tf_op jit(solution)/shard_map/ppermute | solution.py:28
  329.2 9.4 %collective-permute-start.42 = (f32[3,8,1,512]{3,0,2,1:T(4,128)}, f32[3,8,1,512]{3,0,2,1:T(4,128)}, u32[]{:S(2)}, u32[]{:S(2)}) collective-permute-start(f32[3,8,1,512]{3,0,2,1:T(4,128)} %get-tuple-element.171), channel_id=1, source_target_pairs={{4,0},{8,4},{12,8},{16,12},{20,16},{24,20},{28,24},{32,28},{36,32}... | collective-permute-start | bytes 147464 | tf_op jit(solution)/shard_map/ppermute | solution.py:28
  351.0 9.2 %collective-permute-start.47 = (f32[3,8,8]{2,1,0:T(8,128)}, f32[3,8,8]{2,1,0:T(8,128)S(1)}, u32[]{:S(2)}, u32[]{:S(2)}) collective-permute-start(f32[3,8,8]{2,1,0:T(8,128)} %bitcast.235), channel_id=1, source_target_pairs={{0,2},{1,3},{2,0},{3,1},{4,6},{5,7},{6,4},{7,5},{8,10},{9,11},{10,... | collective-permute-start | bytes 2312 | tf_op jit(solution)/shard_map/ppermute | solution.py:36
  354.4 9.6 %collective-permute-start.45 = (f32[3,8,1,512]{3,0,2,1:T(4,128)}, f32[3,8,1,512]{3,0,2,1:T(4,128)}, u32[]{:S(2)}, u32[]{:S(2)}) collective-permute-start(f32[3,8,1,512]{3,0,2,1:T(4,128)} %get-tuple-element.159), channel_id=1, source_target_pairs={{4,0},{8,4},{12,8},{16,12},{20,16},{24,20},{28,24},{32,28},{36,32}... | collective-permute-start | bytes 147464 | tf_op jit(solution)/shard_map/ppermute | solution.py:28
  377.3 9.6 %collective-permute-start.48 = (f32[3,8,1,512]{3,0,2,1:T(4,128)}, f32[3,8,1,512]{3,0,2,1:T(4,128)}, u32[]{:S(2)}, u32[]{:S(2)}) collective-permute-start(f32[3,8,1,512]{3,0,2,1:T(4,128)} %get-tuple-element.147), channel_id=1, source_target_pairs={{4,0},{8,4},{12,8},{16,12},{20,16},{24,20},{28,24},{32,28},{36,32}... | collective-permute-start | bytes 147464 | tf_op jit(solution)/shard_map/ppermute | solution.py:28
  399.3 9.2 %collective-permute-start.53 = (f32[3,8,8]{2,1,0:T(8,128)}, f32[3,8,8]{2,1,0:T(8,128)S(1)}, u32[]{:S(2)}, u32[]{:S(2)}) collective-permute-start(f32[3,8,8]{2,1,0:T(8,128)} %bitcast.237), channel_id=1, source_target_pairs={{0,2},{1,3},{2,0},{3,1},{4,6},{5,7},{6,4},{7,5},{8,10},{9,11},{10,... | collective-permute-start | bytes 2312 | tf_op jit(solution)/shard_map/ppermute | solution.py:36
  402.6 9.6 %collective-permute-start.51 = (f32[3,8,1,512]{3,0,2,1:T(4,128)}, f32[3,8,1,512]{3,0,2,1:T(4,128)}, u32[]{:S(2)}, u32[]{:S(2)}) collective-permute-start(f32[3,8,1,512]{3,0,2,1:T(4,128)} %get-tuple-element.135), channel_id=1, source_target_pairs={{4,0},{8,4},{12,8},{16,12},{20,16},{24,20},{28,24},{32,28},{36,32}... | collective-permute-start | bytes 147464 | tf_op jit(solution)/shard_map/ppermute | solution.py:28
  550.0 8.7 %collective-permute-start.77 = (f32[3,8,8]{2,1,0:T(8,128)}, f32[3,8,8]{2,1,0:T(8,128)S(1)}, u32[]{:S(2)}, u32[]{:S(2)}) collective-permute-start(f32[3,8,8]{2,1,0:T(8,128)} %bitcast.238), channel_id=1, source_target_pairs={{0,2},{1,3},{2,0},{3,1},{4,6},{5,7},{6,4},{7,5},{8,10},{9,11},{10,... | collective-permute-start | bytes 2312 | tf_op jit(solution)/shard_map/ppermute | solution.py:36
  553.4 9.0 %collective-permute-start.75 = (f32[3,8,1,512]{3,0,2,1:T(4,128)}, f32[3,8,1,512]{3,0,2,1:T(4,128)}, u32[]{:S(2)}, u32[]{:S(2)}) collective-permute-start(f32[3,8,1,512]{3,0,2,1:T(4,128)} %get-tuple-element.126), channel_id=1, source_target_pairs={{4,0},{8,4},{12,8},{16,12},{20,16},{24,20},{28,24},{32,28},{36,32}... | collective-permute-start | bytes 147464 | tf_op jit(solution)/shard_map/ppermute | solution.py:28
  575.3 9.4 %collective-permute-start.78 = (f32[3,8,1,512]{3,0,2,1:T(4,128)}, f32[3,8,1,512]{3,0,2,1:T(4,128)}, u32[]{:S(2)}, u32[]{:S(2)}) collective-permute-start(f32[3,8,1,512]{3,0,2,1:T(4,128)} %get-tuple-element.114), channel_id=1, source_target_pairs={{4,0},{8,4},{12,8},{16,12},{20,16},{24,20},{28,24},{32,28},{36,32}... | collective-permute-start | bytes 147464 | tf_op jit(solution)/shard_map/ppermute | solution.py:28
  (134 other events, 3027.9 us)
where the time goes:
time: 610 us; the launch traced here: 598 us
  local copies, waits for them, and re-layouts  204 us (33%)
  starting transfers between devices  186 us (30%)
  other arithmetic  133 us (22%)
  waiting for transfers between devices  70.3 us (12%)
    ppermute x25, starting transfers between devices, extended(): lax.ppermute(lax.slice_in_dim(block, 0, width, axis=dim), axis, backward)  83.2 us
    ppermute x25, waiting for transfers between devices, extended(): lax.ppermute(lax.slice_in_dim(block, block.shape[dim] - width, None, axis...  63.8 us
    ppermute x25, starting transfers between devices, extended(): lax.ppermute(lax.slice_in_dim(block, block.shape[dim] - width, None, axis...  59.3 us
    ppermute x32, starting transfers between devices, swapped(): return lax.ppermute(value, axis, pairs)  43.6 us
    sub x19, other arithmetic, relax(): residual = source - operate(iterate, operator, neighbour_fn(iterate))  31.7 us
    broadcast_in_dim x23, local copies, waits for them, and re-layouts, paired_faces(): right_rim[..., None]  24.8 us
    reduce_sum x11, other arithmetic, pair_cols(): return array.reshape(extent[:-1] + (extent[-1] // 2, 2)).sum(axis=-1)  23.7 us
    broadcast_in_dim x23, local copies, waits for them, and re-layouts, paired_faces(): left_rim[..., None]  23.6 us
  transfers between devices with their start and end apart: 82, of which 25 were waited for; matrix products, arithmetic and copies ran while one was open for 19% of the time, Pallas kernels for 0%

commit v1 on v0

v1 whole, which is shorter than its diff:
```python
import jax
import jax.numpy as jnp
from jax import lax
from jax.experimental import pallas as pl
from jax.experimental.pallas import tpu as pltpu
from jax.sharding import PartitionSpec as P

SECTIONS = 5
LOADS = 16
LAYERS = 8
LANES = 128
EXT0 = 40
EXT1 = 20
EXT2 = 10
WIDE2 = 14

node_table = (0.35, 0.55, 0.8, 1.1, 1.5, 2.0, 2.7, 3.6)
via_conductance = 2.5
ball_conductance = 4.0
damping = 0.8
slab_partner = (0, 2, 1, 4, 3)


def pair_times(first, second):
    return (
        first[0] * second[0] - first[1] * second[1],
        first[0] * second[1] + first[1] * second[0],
    )


def pair_over(first, second):
    divisor = second[0] * second[0] + second[1] * second[1]
    return (
        (first[0] * second[0] + first[1] * second[1]) / divisor,
        (first[1] * second[0] - first[0] * second[1]) / divisor,
    )


def pair_minus(first, second):
    return (first[0] - second[0], first[1] - second[1])


def poly_value(coeffs, point):
    total = (0.0, 0.0)
    for c in reversed(coeffs):
        total = pair_times(total, point)
        total = (total[0] + c, total[1])
    return total


def poly_product(first, second):
    result = [0.0] * (len(first) + len(second) - 1)
    for i in range(len(first)):
        for j in range(len(second)):
            result[i + j] = result[i + j] + first[i] * second[j]
    return result


def poly_roots(coeffs):
    leading = coeffs[-1]
    scaled = [c / leading for c in coeffs]
    degree = len(coeffs) - 1
    guesses = []
    current = (1.0, 0.0)
    for k in range(degree):
        guesses.append(current)
        current = pair_times(current, (0.4, 0.9))
    for repeat_index in range(800):
        for k in range(degree):
            divisor = (1.0, 0.0)
            for j in range(degree):
                if j != k:
                    divisor = pair_times(divisor, pair_minus(guesses[k], guesses[j]))
            guesses[k] = pair_minus(guesses[k], pair_over(poly_value(scaled, guesses[k]), divisor))
    return guesses


def matrix_product(first, second):
    return [
        [
            sum((first[i][k] * second[k][j] for k in range(len(second))))
            for j in range(len(second[0]))
        ]
        for i in range(len(first))
    ]


def matrix_inverse(matrix):
    order = len(matrix)
    work = [list(matrix[i]) + [1.0 if i == j else 0.0 for j in range(order)] for i in range(order)]
    for column in range(order):
        pivot = column
        for i in range(column + 1, order):
            if abs(work[i][column]) > abs(work[pivot][column]):
                pivot = i
        work[column], work[pivot] = (work[pivot], work[column])
        factor = work[column][column]
        work[column] = [entry / factor for entry in work[column]]
        for i in range(order):
            if i != column:
                scale_row = work[i][column]
                work[i] = [work[i][j] - scale_row * work[column][j] for j in range(2 * order)]
    return [row[order:] for row in work]


def eigen_vector(matrix, value):
    order = len(matrix)
    size_inner = order - 1
    system = []
    for i in range(size_inner):
        row = []
        for j in range(order):
            entry = (matrix[i][j], 0.0)
            if i == j:
                entry = pair_minus(entry, value)
            row.append(entry)
        row[order - 1] = (-row[order - 1][0], -row[order - 1][1])
        system.append(row)
    for column in range(size_inner):
        pivot = column
        for i in range(column + 1, size_inner):
            left_size = system[i][column][0] ** 2 + system[i][column][1] ** 2
            right_size = system[pivot][column][0] ** 2 + system[pivot][column][1] ** 2
            if left_size > right_size:
                pivot = i
        system[column], system[pivot] = (system[pivot], system[column])
        for i in range(size_inner):
            if i != column:
                factor = pair_over(system[i][column], system[column][column])
                system[i] = [
                    pair_minus(system[i][j], pair_times(factor, system[column][j]))
                    for j in range(order)
                ]
    vector = [pair_over(system[i][order - 1], system[i][i]) for i in range(size_inner)]
    vector.append((1.0, 0.0))
    return vector


def radau_tables():
    section_count = 5
    generator = [1.0]
    for k in range(section_count - 1):
        generator = poly_product(generator, [0.0, 1.0])
    for k in range(section_count):
        generator = poly_product(generator, [-1.0, 1.0])
    for k in range(section_count - 1):
        generator = [j * generator[j] for j in range(1, len(generator))]
    abscissae = sorted((root[0] for root in poly_roots(generator)))
    vander = [[abscissae[i] ** j for j in range(section_count)] for i in range(section_count)]
    integrals = [
        [abscissae[i] ** (j + 1) / (j + 1) for j in range(section_count)]
        for i in range(section_count)
    ]
    butcher = matrix_product(integrals, matrix_inverse(vander))
    inverse = matrix_inverse(butcher)
    coeffs = [0.0] * (section_count + 1)
    coeffs[section_count] = 1.0
    current = [[0.0] * section_count for _ in range(section_count)]
    for k in range(1, section_count + 1):
        current = matrix_product(inverse, current)
        for i in range(section_count):
            current[i][i] = current[i][i] + coeffs[section_count - k + 1]
        applied = matrix_product(inverse, current)
        coeffs[section_count - k] = -sum((applied[i][i] for i in range(section_count))) / k
    eigen_values = poly_roots(coeffs)
    real_pick = 0
    for k in range(section_count):
        if abs(eigen_values[k][1]) < abs(eigen_values[real_pick][1]):
            real_pick = k
    upper_half = [k for k in range(section_count) if eigen_values[k][1] > 1e-09]
    upper_half = sorted(upper_half, key=lambda k: -eigen_values[k][0])
    columns = [[entry[0] for entry in eigen_vector(inverse, (eigen_values[real_pick][0], 0.0))]]
    for k in upper_half:
        vector = eigen_vector(inverse, eigen_values[k])
        columns.append([entry[0] for entry in vector])
        columns.append([entry[1] for entry in vector])
    transform = [[columns[j][i] for j in range(section_count)] for i in range(section_count)]
    inverse_transform = matrix_inverse(transform)
    blocks = matrix_product(matrix_product(inverse_transform, inverse), transform)
    diagonal = [blocks[k][k] for k in range(section_count)]
    coupling = [
        blocks[k][slab_partner[k]] if slab_partner[k] != k else 0.0 for k in range(section_count)
    ]
    return (transform, inverse_transform, diagonal, coupling)


TRANSFORM, INVERSE, DIAGONAL, COUPLING = radau_tables()
SHIFTS = (
    DIAGONAL[0],
    0.5 * (DIAGONAL[1] + DIAGONAL[2]),
    0.5 * (DIAGONAL[3] + DIAGONAL[4]),
)
COUPLES = (0.5 * (COUPLING[1] - COUPLING[2]), 0.5 * (COUPLING[3] - COUPLING[4]))
ROW_SUMS = tuple(sum(row) for row in INVERSE)


def from_right(value):
    return pltpu.roll(value, LANES - 1, 1)


def from_left(value):
    return pltpu.roll(value, 1, 1)


def from_above(value):
    return pltpu.roll(value, LAYERS - 1, 0)


def from_below(value):
    return pltpu.roll(value, 1, 0)


def lane_index():
    return lax.broadcasted_iota(jnp.int32, (LAYERS, LANES), 1)


def layer_index():
    return lax.broadcasted_iota(jnp.int32, (LAYERS, LANES), 0)


def unpacked(packs):
    lane = lane_index()
    last = jnp.where(
        lane < 32,
        pltpu.roll(packs[0], 32, 1),
        jnp.where(lane < 64, pltpu.roll(packs[1], 64, 1), pltpu.roll(packs[2], 96, 1)),
    )
    return [packs[0], packs[1], packs[2], last]


def packed(phases):
    lane = lane_index()
    return [
        jnp.where(lane < 96, phases[s], pltpu.roll(phases[3], 96 - 32 * s, 1)) for s in range(3)
    ]


def rows_loop(low, high, body):
    def step(i, carry):
        body(i)
        return carry

    lax.fori_loop(low, high, step, 0)


class Level:
    def __init__(self, phases, gx, gy, via, below, cap, total, weights):
        self.phases = phases
        self.gx, self.gy = gx, gy
        self.via, self.below = via, below
        self.cap, self.total, self.weights = cap, total, weights

    def sides(self, centre, p):
        right = centre[p + 1] if p < self.phases - 1 else from_right(centre[0])
        left = centre[p - 1] if p > 0 else from_left(centre[self.phases - 1])
        return right, left

    def inflow(self, coeffs, centre, p, upper, lower):
        gx_lower, gx_upper, gy_left, gy_right, via, below = coeffs
        right, left = self.sides(centre, p)
        here = centre[p]
        return (
            (gx_upper * upper + gx_lower * lower)
            + (gy_right * right + gy_left * left)
            + (via * from_above(here) + below * from_below(here))
        )

    def coeffs(self, i, p):
        return (
            self.gx[i, p],
            self.gx[i + 1, p],
            self.gy[i, p],
            self.gy[i, p + 1],
            self.via[i, p],
            self.below[i, p],
        )

    def set_total(self, i):
        bottom = layer_index() == 0
        for p in range(self.phases):
            grounded = self.below[i, p]
            below = jnp.where(bottom, 0.0, grounded)
            via = from_above(below)
            total = (
                (self.gx[i, p] + self.gx[i + 1, p])
                + (self.gy[i, p] + self.gy[i, p + 1])
                + (via + grounded)
            )
            self.below[i, p] = below
            self.via[i, p] = via
            self.total[i, p] = total
            cap = self.cap[i, p]
            self.weights[i, p * 5] = damping / (SHIFTS[0] * cap + total)
            for s in range(2):
                direct = SHIFTS[s + 1] * cap + total
                cross = COUPLES[s] * cap
                scale = damping / (direct * direct + cross * cross)
                self.weights[i, p * 5 + 1 + 2 * s] = direct * scale
                self.weights[i, p * 5 + 2 + 2 * s] = -(cross * scale)

    def weighted(self, i, p, values):
        w = [self.weights[i, p * 5 + m] for m in range(5)]
        out = [w[0] * values[0]]
        for s in range(2):
            first, second = values[1 + 2 * s], values[2 + 2 * s]
            out.append(w[1 + 2 * s] * first + w[2 + 2 * s] * second)
            out.append(w[1 + 2 * s] * second - w[2 + 2 * s] * first)
        return out

    def first_relax(self, target, source, low, high):
        def body(i):
            for p in range(self.phases):
                values = [source[i, k * self.phases + p] for k in range(SECTIONS)]
                for k, value in enumerate(self.weighted(i, p, values)):
                    target[i, k * self.phases + p] = value

        rows_loop(low, high, body)

    def gathered(self, iterate, source, i):
        count = self.phases
        centres = [[iterate[i, k * count + p] for p in range(count)] for k in range(SECTIONS)]
        sums = []
        for p in range(count):
            coeffs = self.coeffs(i, p)
            sums.append(
                [
                    source[i, k * count + p]
                    + self.inflow(
                        coeffs,
                        centres[k],
                        p,
                        iterate[i + 1, k * count + p],
                        iterate[i - 1, k * count + p],
                    )
                    for k in range(SECTIONS)
                ]
            )
        return centres, sums

    def relax(self, target, iterate, source, low, high):
        count = self.phases

        def body(i):
            centres, sums = self.gathered(iterate, source, i)
            for p in range(count):
                for k, value in enumerate(self.weighted(i, p, sums[p])):
                    target[i, k * count + p] = (1.0 - damping) * centres[k][p] + value

        rows_loop(low, high, body)

    def residual(self, iterate, source, i):
        centres, sums = self.gathered(iterate, source, i)
        result = []
        for p in range(self.phases):
            cap, total = self.cap[i, p], self.total[i, p]
            x = [centres[k][p] for k in range(SECTIONS)]
            out = [sums[p][0] - (SHIFTS[0] * cap + total) * x[0]]
            for s in range(2):
                direct = SHIFTS[s + 1] * cap + total
                cross = COUPLES[s] * cap
                a, b = 1 + 2 * s, 2 + 2 * s
                out.append(sums[p][a] - (direct * x[a] + cross * x[b]))
                out.append(sums[p][b] - (direct * x[b] - cross * x[a]))
            result.append(out)
        return result

    def restrict(self, target, iterate, source, low, high, shift=0):
        half = self.phases // 2

        def body(row):
            one = self.residual(iterate, source, 2 * row)
            two = self.residual(iterate, source, 2 * row + 1)
            for k in range(SECTIONS):
                for q in range(half):
                    target[row + shift, k * half + q] = (one[2 * q][k] + one[2 * q + 1][k]) + (
                        two[2 * q][k] + two[2 * q + 1][k]
                    )

        rows_loop(low, high, body)

    def correct(self, target, iterate, coarse, low, high, shift=0):
        count, half = self.phases, self.phases // 2

        def body(i):
            row = lax.shift_right_logical(i, 1) + shift
            for k in range(SECTIONS):
                for q in range(half):
                    value = coarse[row, k * half + q]
                    for p in (2 * q, 2 * q + 1):
                        target[i, k * count + p] = iterate[i, k * count + p] + value

        rows_loop(low, high, body)


def coarsen(fine, coarse, rows):
    half = coarse.phases

    def body(row):
        for q in range(half):
            for ref_out, ref_in in ((coarse.cap, fine.cap),):
                ref_out[row, q] = (ref_in[2 * row, 2 * q] + ref_in[2 * row, 2 * q + 1]) + (
                    ref_in[2 * row + 1, 2 * q] + ref_in[2 * row + 1, 2 * q + 1]
                )
        for q in range(half + 1):
            coarse.gy[row, q] = fine.gy[2 * row, 2 * q] + fine.gy[2 * row + 1, 2 * q]

    rows_loop(0, rows, body)

    def body_gx(row):
        for q in range(half):
            coarse.gx[row, q] = fine.gx[2 * row, 2 * q] + fine.gx[2 * row, 2 * q + 1]

    rows_loop(1, rows, body_gx)


def sum_below(fine_below, coarse_below, phases, rows):
    def body(row):
        for q in range(phases):
            coarse_below[row, q] = (
                fine_below[2 * row, 2 * q] + fine_below[2 * row, 2 * q + 1]
            ) + (fine_below[2 * row + 1, 2 * q] + fine_below[2 * row + 1, 2 * q + 1])

    rows_loop(0, rows, body)


def gather_kernel(voltage, capacity, node_class, via, ball, load, whole, left, right, work):
    classes = node_class[...]
    conduct = jnp.full(classes.shape, node_table[0], jnp.float32)
    for c in range(1, len(node_table)):
        conduct = jnp.where(classes == c, node_table[c], conduct)
    grounded = jnp.where(ball[...] == 1, ball_conductance, 0.0)
    upright = jnp.where(via[...] == 1, via_conductance, 0.0)
    for h in range(2):
        half = slice(h * 128, h * 128 + 128)
        work[0, h] = voltage[:, half]
        work[1, h] = capacity[:, half]
        work[2, h] = conduct[:, half]
        work[3, h, 0:8] = grounded[:, half]
        work[3, h, 8:64] = upright[:, half]
    for row in range(8):
        for a in range(4):
            at = (row * 4 + a) * 8
            for h in range(2):
                whole[at : at + 8, h * 128 : h * 128 + 128] = work[
                    a, h, pl.ds(row, 8, stride=8), :
                ]
    whole[256:264] = load[...].astype(jnp.float32)
    left[...] = whole[:, :64]
    right[...] = whole[:, 192:]


def three_parts(value):
    high = value.astype(jnp.bfloat16)
    rest = value - high.astype(jnp.float32)
    middle = rest.astype(jnp.bfloat16)
    low = (rest - middle.astype(jnp.float32)).astype(jnp.bfloat16)
    return high, middle, low


def selected(value, chooser):
    high, middle, low = (
        jnp.dot(part, chooser, preferred_element_type=jnp.float32) for part in three_parts(value)
    )
    return high + (middle + low)


def phase_kernel(whole, from_lower, from_upper, out):
    def chooser(first, count):
        shape = (count, 384)
        column = first + lax.broadcasted_iota(jnp.int32, shape, 0)
        slot = lax.broadcasted_iota(jnp.int32, shape, 1)
        s, lane = slot // 128, slot % 128
        wanted = jnp.where(lane < 96, 4 * lane + s, 4 * (32 * s + lane - 96) + 3)
        return jnp.where(column == wanted, 1.0, 0.0).astype(jnp.bfloat16)

    result = selected(whole[...], chooser(64, 256))
    result = result + selected(from_lower[...], chooser(0, 64))
    result = result + selected(from_upper[...], chooser(320, 64))
    for n in range(33):
        for s in range(3):
            out[n, s] = result[8 * n : 8 * n + 8, 128 * s : 128 * s + 128]


def setup_kernel(
    place, mixed_table, *refs
):
    blocks = refs[:5]
    (gx0, gy0, via0, below0, cap0, total0, weights0, f0, x0) = refs[5:14]
    (gx1, gy1, via1, below1, cap1, total1, weights1, f1, x1) = refs[14:23]
    (gx2, gy2, below2, cap2, f2, go_up, go_down) = refs[23:30]
    volt, conduct, surface, spare0, spare1 = refs[30:35]
    fine = Level(4, gx0, gy0, via0, below0, cap0, total0, weights0)
    middle = Level(2, gx1, gy1, via1, below1, cap1, total1, weights1)
    coarse = Level(1, gx2, gy2, None, below2, cap2, None, None)
    row_block, column_block = place[0], place[1]
    lane = lane_index()

    for b, block in enumerate(blocks):

        def spread(s, block=block, b=b):
            for a, ref in enumerate((volt, cap0, conduct, below0)):
                phases = unpacked([block[4 * s + a, t] for t in range(3)])
                for p in range(4):
                    ref[8 * b + s, p] = phases[p]

        rows_loop(0, 8, spread)
        loads = unpacked([block[32, t] for t in range(3)])
        for p in range(4):
            values = [jnp.zeros((8, LANES), jnp.float32) for _ in range(SECTIONS)]
            for t in range(LOADS):
                chosen = loads[p] == float(t)
                values = [
                    jnp.where(chosen, mixed_table[t, k], values[k]) for k in range(SECTIONS)
                ]
            for k in range(SECTIONS):
                surface[4 * k + p, 8 * b : 8 * b + 8] = values[k]

    def series(near, far):
        return 2.0 * near * far / (near + far)

    def set_gx(i):
        row = 8 * row_block - 16 + i
        inside = jnp.where((row == 0) | (row == 256), 0.0, 1.0).astype(jnp.float32)
        for p in range(4):
            gx0[i, p] = inside * series(conduct[i - 1, p], conduct[i, p])

    rows_loop(1, EXT0, set_gx)
    edge = ((lane == 16) & (column_block == 0)) | ((lane == 80) & (column_block == 3))

    def set_gy(i):
        here = [conduct[i, p] for p in range(4)]
        first = jnp.where(edge, 0.0, series(from_left(here[3]), here[0]))
        gy0[i, 0] = first
        for p in range(1, 4):
            gy0[i, p] = series(here[p - 1], here[p])
        gy0[i, 4] = from_right(first)

    rows_loop(0, EXT0, set_gy)
    coarsen(fine, middle, EXT1)
    sum_below(below0, below1, 2, EXT1)
    coarsen(middle, coarse, EXT2)
    sum_below(below1, below2, 1, EXT2)
    rows_loop(1, EXT0 - 1, fine.set_total)
    rows_loop(1, EXT1 - 1, middle.set_total)

    top = layer_index() == LAYERS - 1

    def set_source(i):
        centre = [volt[i, p] for p in range(4)]
        for p in range(4):
            leak = total0[i, p] * centre[p] - fine.inflow(
                fine.coeffs(i, p), centre, p, volt[i + 1, p], volt[i - 1, p]
            )
            values = []
            for k in range(SECTIONS):
                drawn = jnp.broadcast_to(surface[4 * k + p, pl.ds(i, 1), :], (LAYERS, LANES))
                values.append(jnp.where(top, drawn, 0.0) - ROW_SUMS[k] * leak)
                f0[i, 4 * k + p] = values[k]
            for k, value in enumerate(fine.weighted(i, p, values)):
                spare0[i, 4 * k + p] = value

    rows_loop(1, EXT0 - 1, set_source)
    fine.relax(x0, spare0, f0, 2, 38)
    fine.restrict(f1, x0, f0, 2, 18)
    middle.first_relax(spare1, f1, 2, 18)
    middle.relax(x1, spare1, f1, 3, 17)
    middle.restrict(f2, x1, f1, 2, 8)
    for target, first, outer in ((go_up, 2, 2), (go_down, 4, 6)):
        for j in range(4):
            for k in range(SECTIONS):
                target[5 * j + k] = f2[first + j, k]
        for j in range(2):
            target[20 + 3 * j] = gy2[outer + j, 0]
            target[21 + 3 * j] = below2[outer + j, 0]
            target[22 + 3 * j] = cap2[outer + j, 0]
        for j in range(3):
            target[26 + j] = gx2[outer + j, 0]


def middle_kernel(*refs):
    (gx0, gy0, via0, below0, cap0, total0, weights0, f0, x0) = refs[0:9]
    (gx1, gy1, via1, below1, cap1, total1, weights1, f1, x1) = refs[9:18]
    (gx2, gy2, below2, cap2, f2, from_lower, from_upper) = refs[18:25]
    (x0_out, f1_out, gxw, gyw, viaw, beloww, weightsw) = refs[25:32]
    (capw, totalw, fw, xa, xb, ya, yb, za) = refs[32:40]
    fine = Level(4, gx0, gy0, via0, below0, cap0, total0, weights0)
    middle = Level(2, gx1, gy1, via1, below1, cap1, total1, weights1)
    coarse = Level(1, gxw, gyw, viaw, beloww, capw, totalw, weightsw)
    for j in range(4):
        for k in range(SECTIONS):
            fw[j, k] = from_lower[5 * j + k]
            fw[10 + j, k] = from_upper[5 * j + k]
    for j in range(2):
        for near, source in ((j, from_lower), (12 + j, from_upper)):
            gyw[near, 0] = source[20 + 3 * j]
            gyw[near, 1] = from_right(source[20 + 3 * j])
            beloww[near, 0] = source[21 + 3 * j]
            capw[near, 0] = source[22 + 3 * j]
    for j in range(3):
        gxw[j, 0] = from_lower[26 + j]
        gxw[12 + j, 0] = from_upper[26 + j]
    for j in range(6):
        for k in range(SECTIONS):
            fw[4 + j, k] = f2[2 + j, k]
    for j in range(10):
        gyw[2 + j, 0] = gy2[j, 0]
        gyw[2 + j, 1] = gy2[j, 1]
        beloww[2 + j, 0] = below2[j, 0]
        capw[2 + j, 0] = cap2[j, 0]
    for j in range(1, 10):
        gxw[2 + j, 0] = gx2[j, 0]
    rows_loop(0, WIDE2, coarse.set_total)
    coarse.first_relax(xa, fw, 0, 14)
    coarse.relax(xb, xa, fw, 1, 13)
    coarse.relax(xa, xb, fw, 2, 12)
    coarse.relax(xb, xa, fw, 3, 11)
    middle.correct(ya, x1, xb, 3, 17, 2)
    middle.relax(yb, ya, f1, 4, 16)
    middle.relax(ya, yb, f1, 5, 15)
    fine.correct(za, x0, ya, 10, 30)
    fine.relax(x0_out, za, f0, 11, 29)
    fine.relax(za, x0_out, f0, 12, 28)
    fine.relax(x0_out, za, f0, 13, 27)
    fine.relax(za, x0_out, f0, 14, 26)
    fine.restrict(f1_out, za, f0, 8, 12, -8)

    def keep(i):
        for n in range(20):
            x0_out[i, n] = za[i, n]

    rows_loop(14, 26, keep)


def lower_kernel(*refs):
    (gx1, gy1, via1, below1, cap1, total1, weights1) = refs[0:7]
    own, from_lower, from_upper = refs[7:10]
    f1, x1, f2_out = refs[10:13]
    (xa,) = refs[13:14]
    middle = Level(2, gx1, gy1, via1, below1, cap1, total1, weights1)
    for j in range(4):
        for n in range(10):
            f1[4 + j, n] = from_lower[j, n]
            f1[8 + j, n] = own[j, n]
            f1[12 + j, n] = from_upper[j, n]
    middle.first_relax(xa, f1, 4, 16)
    middle.relax(x1, xa, f1, 5, 15)
    middle.restrict(f2_out, x1, f1, 3, 7, -3)


def finish_kernel(*refs):
    (gx0, gy0, via0, below0, weights0, f0, x0) = refs[0:7]
    (gx1, gy1, via1, below1, weights1, f1, x1) = refs[7:14]
    (gxw, gyw, viaw, beloww, weightsw, own, from_lower, from_upper, voltage) = refs[14:23]
    sections, next_voltage = refs[23:25]
    fw, xa, xb, ya, yb, za, zb, mixed, turn = refs[25:34]
    fine = Level(4, gx0, gy0, via0, below0, None, None, weights0)
    middle = Level(2, gx1, gy1, via1, below1, None, None, weights1)
    coarse = Level(1, gxw, gyw, viaw, beloww, None, None, weightsw)
    for j in range(4):
        for k in range(SECTIONS):
            fw[1 + j, k] = from_lower[j, k]
            fw[5 + j, k] = own[j, k]
            fw[9 + j, k] = from_upper[j, k]
    coarse.first_relax(xa, fw, 1, 13)
    coarse.relax(xb, xa, fw, 2, 12)
    coarse.relax(xa, xb, fw, 3, 11)
    coarse.relax(xb, xa, fw, 4, 10)
    middle.correct(ya, x1, xb, 5, 15, 2)
    middle.relax(yb, ya, f1, 6, 14)
    middle.relax(ya, yb, f1, 7, 13)
    fine.correct(za, x0, ya, 14, 26)
    fine.relax(zb, za, f0, 15, 25)
    fine.relax(za, zb, f0, 16, 24)

    def mix(row):
        for p in range(4):
            values = [za[16 + row, 4 * k + p] for k in range(SECTIONS)]
            for j in range(SECTIONS):
                total = TRANSFORM[j][0] * values[0]
                for k in range(1, SECTIONS):
                    total = total + TRANSFORM[j][k] * values[k]
                mixed[p, 8 * j + row] = total

    rows_loop(0, 8, mix)
    result = None
    for p in range(4):
        lane = lax.broadcasted_iota(jnp.int32, (LANES, 256), 0)
        column = lax.broadcasted_iota(jnp.int32, (LANES, 256), 1)
        chooser = jnp.where(column == 4 * (lane - 16) + p, 1.0, 0.0).astype(jnp.bfloat16)
        part = selected(mixed[p].reshape(320, LANES), chooser)
        result = part if result is None else result + part
    for j in range(SECTIONS):
        for row in range(8):
            at = (8 * j + row) * 8
            for h in range(2):
                turn[j, h, pl.ds(row, 8, stride=8), :] = result[
                    at : at + 8, h * 128 : h * 128 + 128
                ]
        for h in range(2):
            sections[j, :, h * 128 : h * 128 + 128] = turn[j, h]
    next_voltage[...] = voltage[...] + sections[SECTIONS - 1]


VMEM = pltpu.MemorySpace.VMEM
SMEM = pltpu.MemorySpace.SMEM


def vregs(*shape):
    return jax.ShapeDtypeStruct(shape + (LAYERS, LANES), jnp.float32)


def scratch(*shape):
    return pltpu.VMEM(shape + (LAYERS, LANES), jnp.float32)


def call(kernel, inputs, outs, scratches=(), scalars=0):
    return pl.pallas_call(
        kernel,
        out_shape=outs,
        in_specs=[pl.BlockSpec(memory_space=SMEM)] * scalars
        + [pl.BlockSpec(memory_space=VMEM)] * (len(inputs) - scalars),
        out_specs=[pl.BlockSpec(memory_space=VMEM)] * len(outs),
        scratch_shapes=list(scratches),
        compiler_params=pltpu.CompilerParams(vmem_limit_bytes=60 * 2**20),
    )(*inputs)


def turned(value, axis, count, shift):
    return lax.ppermute(value, axis, [(i, (i + shift) % count) for i in range(count)])


ROWS = ("section", "gx")


def local(voltage, capacity, node_class, via_sites, ball_sites, load_type, load_table):
    rows = lax.axis_size("section") * lax.axis_size("gx")
    columns = lax.axis_size("gy")
    volts = voltage.reshape(64, 256)
    whole, left, right = call(
        gather_kernel,
        (
            volts,
            capacity.reshape(64, 256),
            node_class.reshape(64, 256),
            via_sites.reshape(56, 256),
            ball_sites,
            load_type,
        ),
        [
            jax.ShapeDtypeStruct((264, 256), jnp.float32),
            jax.ShapeDtypeStruct((264, 64), jnp.float32),
            jax.ShapeDtypeStruct((264, 64), jnp.float32),
        ],
        [pltpu.VMEM((4, 2, 64, LANES), jnp.float32)],
    )
    from_lower = turned(right, "gy", columns, 1)
    from_upper = turned(left, "gy", columns, -1)
    mixed_table = jnp.einsum(
        "tk,jk->tj", load_table, jnp.asarray(INVERSE, jnp.float32), precision=lax.Precision.HIGHEST
    )
    place = jnp.stack(
        [
            lax.axis_index("section") * lax.axis_size("gx") + lax.axis_index("gx"),
            lax.axis_index("gy"),
        ]
    ).astype(jnp.int32)
    (block,) = call(phase_kernel, (whole, from_lower, from_upper), [vregs(33, 3)])
    blocks = [turned(block, ROWS, rows, s) if s else block for s in (2, 1, 0, -1, -2)]
    level0 = [
        vregs(EXT0, 4),
        vregs(EXT0, 5),
        vregs(EXT0, 4),
        vregs(EXT0, 4),
        vregs(EXT0, 4),
        vregs(EXT0, 4),
        vregs(EXT0, 20),
        vregs(EXT0, 20),
        vregs(EXT0, 20),
    ]
    level1 = [
        vregs(EXT1, 2),
        vregs(EXT1, 3),
        vregs(EXT1, 2),
        vregs(EXT1, 2),
        vregs(EXT1, 2),
        vregs(EXT1, 2),
        vregs(EXT1, 10),
        vregs(EXT1, 10),
        vregs(EXT1, 10),
    ]
    level2 = [vregs(EXT2, 1), vregs(EXT2, 2), vregs(EXT2, 1), vregs(EXT2, 1), vregs(EXT2, 5)]
    state = call(
        setup_kernel,
        (place, mixed_table, *blocks),
        level0 + level1 + level2 + [vregs(29), vregs(29)],
        [
            scratch(EXT0, 4),
            scratch(EXT0, 4),
            pltpu.VMEM((20, EXT0, LANES), jnp.float32),
            scratch(EXT0, 20),
            scratch(EXT1, 10),
        ],
        2,
    )
    fine, middle, coarse = state[0:9], state[9:18], state[18:23]
    go_up, go_down = state[23:25]
    lower = turned(go_up, ROWS, rows, 2)
    upper = turned(go_down, ROWS, rows, -2)
    x0, f1_own, gxw, gyw, viaw, beloww, weightsw = call(
        middle_kernel,
        (*fine, *middle, *coarse, lower, upper),
        [
            vregs(EXT0, 20),
            vregs(4, 10),
            vregs(WIDE2 + 1, 1),
            vregs(WIDE2, 2),
            vregs(WIDE2, 1),
            vregs(WIDE2, 1),
            vregs(WIDE2, 5),
        ],
        [
            scratch(WIDE2, 1),
            scratch(WIDE2, 1),
            scratch(WIDE2, 5),
            scratch(WIDE2, 5),
            scratch(WIDE2, 5),
            scratch(EXT1, 10),
            scratch(EXT1, 10),
            scratch(EXT0, 20),
        ],
    )
    lower = turned(f1_own, ROWS, rows, 1)
    upper = turned(f1_own, ROWS, rows, -1)
    f1, x1, f2_own = call(
        lower_kernel,
        (*middle[:7], f1_own, lower, upper),
        [vregs(EXT1, 10), vregs(EXT1, 10), vregs(4, 5)],
        [scratch(EXT1, 10)],
    )
    lower = turned(f2_own, ROWS, rows, 2)
    upper = turned(f2_own, ROWS, rows, -2)
    sections, next_voltage = call(
        finish_kernel,
        (
            *fine[:4],
            *fine[6:8],
            x0,
            *middle[:4],
            middle[6],
            f1,
            x1,
            gxw,
            gyw,
            viaw,
            beloww,
            weightsw,
            f2_own,
            lower,
            upper,
            volts,
        ),
        [
            jax.ShapeDtypeStruct((SECTIONS, 64, 256), jnp.float32),
            jax.ShapeDtypeStruct((64, 256), jnp.float32),
        ],
        [
            scratch(WIDE2, 5),
            scratch(WIDE2, 5),
            scratch(WIDE2, 5),
            scratch(EXT1, 10),
            scratch(EXT1, 10),
            scratch(EXT0, 20),
            scratch(EXT0, 20),
            scratch(4, 40),
            pltpu.VMEM((SECTIONS, 2, 64, LANES), jnp.float32),
        ],
    )
    return sections.reshape((SECTIONS,) + voltage.shape), next_voltage.reshape(voltage.shape)


def solution(mesh):
    return jax.shard_map(
        local,
        mesh=mesh,
        in_specs=(
            P(None, ("section", "gx"), "gy"),
            P(None, ("section", "gx"), "gy"),
            P(None, ("section", "gx"), "gy"),
            P(None, ("section", "gx"), "gy"),
            P(("section", "gx"), "gy"),
            P(("section", "gx"), "gy"),
            P(),
        ),
        out_specs=(P(None, None, ("section", "gx"), "gy"), P(None, ("section", "gx"), "gy")),
        check_vma=False,
    )
```

time: 610 us -> 140 us (0.23)
  the two profiles are of different devices: /device:TPU:1 before, /device:TPU:0 now
where the time goes in v1:
time: 140 us
  Pallas kernels  70.6 us (50%)
  waiting for transfers between devices  40.8 us (29%)
  starting transfers between devices  22.5 us (16%)
  local copies, waits for them, and re-layouts  3.45 us (2%)
  matrix products  1.48 us (1%)
    pallas_call x6, Pallas kernels, call(): pl.pallas_call(kernel, out_shape=outs, in_specs=[pl.BlockSpec(memory_spac...  70.6 us
    ppermute x12, waiting for transfers between devices, turned(): lax.ppermute(value, axis, [(i, (i + shift) % count) for i in range(count)])  40.8 us
    ppermute x12, starting transfers between devices, turned(): lax.ppermute(value, axis, [(i, (i + shift) % count) for i in range(count)])  22.5 us
    unnamed x26, local copies, waits for them, and re-layouts  3.45 us
  transfers between devices with their start and end apart: 12, of which 10 were waited for; matrix products, arithmetic and copies ran while one was open for 2% of the time, Pallas kernels for 0%

profile of v1, /device:TPU:0, one launch (start us, length us, event | category | flops | bytes accessed | tf_op | source)
XLA Modules:
  0.0 140.2 jit_solution(12023755250965772797)
XLA Ops:
  0.6 1.8 %shard_map.95 = (f32[264,256]{1,0:T(8,128)}, f32[264,64]{1,0:T(8,128)}, f32[264,64]{1,0:T(8,128)}) custom-call(f32[64,256]{1,0:T(8,128)} %bitcast.12, f32[64,256]{1,0:T(8,128)} %bitcast.14, s32[64,256]{1,0:T(8,128)} %bitcast.15, s32[56,256]{1,0:T(8,128)} %bitcast.16, s32[8,256]{1,0:T(8,128)} %ball.1, s32[8,256]{1,0:T(8,128)} %load.1), custom_call_target="tpu_custom_call" | custom-call | tf_op jit(solution)/shard_map/pallas_call | solution.py:717
  2.5 2.0 %collective-permute-start = (f32[264,64]{1,0:T(8,128)}, f32[264,64]{1,0:T(8,128)S(1)}, u32[]{:S(2)}, u32[]{:S(2)}) collective-permute-start(f32[264,64]{1,0:T(8,128)} %get-tuple-element.43), channel_id=1, source_target_pairs={{0,1},{1,2},{2,3},{3,0},{4,5},{5,6},{6,7},{7,4},{8,9},{9,10},{10,1... | collective-permute-start | bytes 202760 | tf_op jit(solution)/shard_map/ppermute | solution.py:729
  4.5 2.1 %collective-permute-start.1 = (f32[264,64]{1,0:T(8,128)}, f32[264,64]{1,0:T(8,128)S(1)}, u32[]{:S(2)}, u32[]{:S(2)}) collective-permute-start(f32[264,64]{1,0:T(8,128)} %get-tuple-element.44), channel_id=1, source_target_pairs={{0,3},{1,0},{2,1},{3,2},{4,7},{5,4},{6,5},{7,6},{8,11},{9,8},{10,9... | collective-permute-start | bytes 202760 | tf_op jit(solution)/shard_map/ppermute | solution.py:729
  6.6 3.8 %collective-permute-done.from_lower = f32[264,64]{1,0:T(8,128)S(1)} collective-permute-done((f32[264,64]{1,0:T(8,128)}, f32[264,64]{1,0:T(8,128)S(1)}, u32[]{:S(2)}, u32[]{:S(2)}) %collective-permute-start) | collective-permute-done | bytes 67616 | tf_op jit(solution)/shard_map/ppermute | solution.py:729
  10.4 0.6 copy-done.7
  11.1 2.7 %shard_map.96.refs_2_ = f32[33,3,8,128]{3,2,1,0:T(8,128)} custom-call(f32[264,256]{1,0:T(8,128)} %get-tuple-element.42.whole, f32[264,64]{1,0:T(8,128)} %copy-done.7, f32[264,64]{1,0:T(8,128)} %copy-done.8), custom_call_target="tpu_custom_call" | custom-call | tf_op jit(solution)/shard_map/pallas_call | solution.py:717
  13.8 4.4 %collective-permute-start.5 = (f32[33,3,8,128]{3,2,1,0:T(8,128)}, f32[33,3,8,128]{3,2,1,0:T(8,128)S(1)}, u32[]{:S(2)}, u32[]{:S(2)}) collective-permute-start(f32[33,3,8,128]{3,2,1,0:T(8,128)} %shard_map.96.refs_2_), channel_id=1, source_target_pairs={{0,120},{4,124},{8,0},{12,4},{16,8},{20,12},{24,16},{28,20},{32,24... | collective-permute-start | bytes 1216520 | tf_op jit(solution)/shard_map/ppermute | solution.py:729
  18.1 0.2 collective-permute-start.4
  18.3 1.8 %collective-permute-start.3 = (f32[33,3,8,128]{3,2,1,0:T(8,128)}, f32[33,3,8,128]{3,2,1,0:T(8,128)S(1)}, u32[]{:S(2)}, u32[]{:S(2)}) collective-permute-start(f32[33,3,8,128]{3,2,1,0:T(8,128)} %shard_map.96.refs_2_), channel_id=1, source_target_pairs={{0,4},{4,8},{8,12},{12,16},{16,20},{20,24},{24,28},{28,32},{32,36}... | collective-permute-start | bytes 1216520 | tf_op jit(solution)/shard_map/ppermute | solution.py:729
  20.2 0.7 pad_add_fusion.place
  20.9 1.5 %convolution_bitcast_fusion.mixed_table = f32[16,5]{1,0:T(8,128)} fusion(f32[5,5]{1,0:T(8,128)} %constant.17.clone, f32[16,5]{0,1:T(8,128)S(1)} %copy-done), kind=kOutput, calls=%fused_computation | convolution fusion | flops 4800 | bytes 740 | tf_op jit(solution)/shard_map/tk,jk->tj/dot_general | solution.py:758
  22.3 8.7 %collective-permute-done.5.refs_4_ = f32[33,3,8,128]{3,2,1,0:T(8,128)S(1)} collective-permute-done((f32[33,3,8,128]{3,2,1,0:T(8,128)}, f32[33,3,8,128]{3,2,1,0:T(8,128)S(1)}, u32[]{:S(2)}, u32[]{:S(2)}) %collective-permute-start.5) | collective-permute-done | bytes 405536 | tf_op jit(solution)/shard_map/ppermute | solution.py:729
  31.1 6.0 %collective-permute-done.4.refs_3_ = f32[33,3,8,128]{3,2,1,0:T(8,128)S(1)} collective-permute-done((f32[33,3,8,128]{3,2,1,0:T(8,128)}, f32[33,3,8,128]{3,2,1,0:T(8,128)S(1)}, u32[]{:S(2)}, u32[]{:S(2)}) %collective-permute-start.4) | collective-permute-done | bytes 405536 | tf_op jit(solution)/shard_map/ppermute | solution.py:729
  37.1 2.4 %collective-permute-done.3.refs_1_ = f32[33,3,8,128]{3,2,1,0:T(8,128)S(1)} collective-permute-done((f32[33,3,8,128]{3,2,1,0:T(8,128)}, f32[33,3,8,128]{3,2,1,0:T(8,128)S(1)}, u32[]{:S(2)}, u32[]{:S(2)}) %collective-permute-start.3) | collective-permute-done | bytes 405536 | tf_op jit(solution)/shard_map/ppermute | solution.py:729
  39.5 3.1 %collective-permute-done.2.refs_0_ = f32[33,3,8,128]{3,2,1,0:T(8,128)S(1)} collective-permute-done((f32[33,3,8,128]{3,2,1,0:T(8,128)}, f32[33,3,8,128]{3,2,1,0:T(8,128)S(1)}, u32[]{:S(2)}, u32[]{:S(2)}) %collective-permute-start.2) | collective-permute-done | bytes 405536 | tf_op jit(solution)/shard_map/ppermute | solution.py:729
  42.6 0.7 copy-done.4
  43.4 29.9 %shard_map.97 = (f32[40,4,8,128]{3,2,1,0:T(8,128)}, f32[40,5,8,128]{3,2,1,0:T(8,128)}, f32[40,4,8,128]{3,2,1,0:T(8,128)}, f32[40,4,8,128]{3,2,1,0:T(8,128)}, f32...) custom-call(s32[2]{0:T(128)} %pad_add_fusion.place, ...), custom_call_target="tpu_custom_call" | custom-call | tf_op jit(solution)/shard_map/pallas_call | solution.py:717
  73.3 1.1 collective-permute-start.6
  74.3 4.4 %collective-permute-start.7 = (f32[29,8,128]{2,1,0:T(8,128)}, f32[29,8,128]{2,1,0:T(8,128)S(1)}, u32[]{:S(2)}, u32[]{:S(2)}) collective-permute-start(f32[29,8,128]{2,1,0:T(8,128)} %get-tuple-element.69), channel_id=1, source_target_pairs={{0,120},{4,124},{8,0},{12,4},{16,8},{20,12},{24,16},{28,20},{32,24... | collective-permute-start | bytes 356360 | tf_op jit(solution)/shard_map/ppermute | solution.py:729
  78.7 2.7 %collective-permute-done.6.refs_23_ = f32[29,8,128]{2,1,0:T(8,128)S(1)} collective-permute-done((f32[29,8,128]{2,1,0:T(8,128)}, f32[29,8,128]{2,1,0:T(8,128)S(1)}, u32[]{:S(2)}, u32[]{:S(2)}) %collective-permute-start.6) | collective-permute-done | bytes 118816 | tf_op jit(solution)/shard_map/ppermute | solution.py:729
  81.4 0.7 copy-done.9
  82.1 19.3 %shard_map.98 = (f32[40,20,8,128]{3,2,1,0:T(8,128)}, f32[4,10,8,128]{3,2,1,0:T(8,128)}, f32[15,1,8,128]{3,2,1,0:T(8,128)}, f32[14,2,8,128]{3,2,1,0:T(8,128)}, f3...) custom-call(f32[40,4,8,128]{3,2,1,0:T(8,128)} %get-tuple-element.45.refs_0_, ...), custom_call_target="tpu_custom_call" | custom-call | tf_op jit(solution)/shard_map/pallas_call | solution.py:717
  101.4 4.5 %collective-permute-start.9 = (f32[4,10,8,128]{3,2,1,0:T(8,128)}, f32[4,10,8,128]{3,2,1,0:T(8,128)S(1)}, u32[]{:S(2)}, u32[]{:S(2)}) collective-permute-start(f32[4,10,8,128]{3,2,1,0:T(8,128)} %get-tuple-element.71.refs_7_), channel_id=1, source_target_pairs={{0,124},{4,0},{8,4},{12,8},{16,12},{20,16},{24,20},{28,24},{32,28}... | collective-permute-start | bytes 491528 | tf_op jit(solution)/shard_map/ppermute | solution.py:729
  105.9 3.1 %collective-permute-done.9.refs_9_ = f32[4,10,8,128]{3,2,1,0:T(8,128)S(1)} collective-permute-done((f32[4,10,8,128]{3,2,1,0:T(8,128)}, f32[4,10,8,128]{3,2,1,0:T(8,128)S(1)}, u32[]{:S(2)}, u32[]{:S(2)}) %collective-permute-start.9) | collective-permute-done | bytes 163872 | tf_op jit(solution)/shard_map/ppermute | solution.py:729
  109.1 5.1 %collective-permute-done.8.refs_8_ = f32[4,10,8,128]{3,2,1,0:T(8,128)S(1)} collective-permute-done((f32[4,10,8,128]{3,2,1,0:T(8,128)}, f32[4,10,8,128]{3,2,1,0:T(8,128)S(1)}, u32[]{:S(2)}, u32[]{:S(2)}) %collective-permute-start.8) | collective-permute-done | bytes 163872 | tf_op jit(solution)/shard_map/ppermute | solution.py:729
  114.2 0.7 copy-done.6
  114.9 4.3 %shard_map.99 = (f32[20,10,8,128]{3,2,1,0:T(8,128)}, f32[20,10,8,128]{3,2,1,0:T(8,128)}, f32[4,5,8,128]{3,2,1,0:T(8,128)}) custom-call(f32[20,2,8,128]{3,2,1,0:T(8,128)} %get-tuple-element.54.refs_9_.refs_0_.refs_7_, f32[20,3,8,128]{3,2,1,0:T(8,128)} %get-tuple-element.55.refs_10_.refs_1_.refs_8_, ...), custom_call_target="tpu_custom_call" | custom-call | tf_op jit(solution)/shard_map/pallas_call | solution.py:717
  119.2 2.0 %collective-permute-start.10 = (f32[4,5,8,128]{3,2,1,0:T(8,128)}, f32[4,5,8,128]{3,2,1,0:T(8,128)S(1)}, u32[]{:S(2)}, u32[]{:S(2)}) collective-permute-start(f32[4,5,8,128]{3,2,1,0:T(8,128)} %get-tuple-element.79.refs_19_), channel_id=1, source_target_pairs={{0,8},{4,12},{8,16},{12,20},{16,24},{20,28},{24,32},{28,36},{32,40... | collective-permute-start | bytes 245768 | tf_op jit(solution)/shard_map/ppermute | solution.py:729
  121.2 2.6 %collective-permute-done.11.refs_21_ = f32[4,5,8,128]{3,2,1,0:T(8,128)S(1)} collective-permute-done((f32[4,5,8,128]{3,2,1,0:T(8,128)}, f32[4,5,8,128]{3,2,1,0:T(8,128)S(1)}, u32[]{:S(2)}, u32[]{:S(2)}) %collective-permute-start.11) | collective-permute-done | bytes 81952 | tf_op jit(solution)/shard_map/ppermute | solution.py:729
  123.9 3.1 %collective-permute-done.10.refs_20_ = f32[4,5,8,128]{3,2,1,0:T(8,128)S(1)} collective-permute-done((f32[4,5,8,128]{3,2,1,0:T(8,128)}, f32[4,5,8,128]{3,2,1,0:T(8,128)S(1)}, u32[]{:S(2)}, u32[]{:S(2)}) %collective-permute-start.10) | collective-permute-done | bytes 81952 | tf_op jit(solution)/shard_map/ppermute | solution.py:729
  127.0 0.6 copy-done.12
  127.6 12.6 %shard_map.100 = (f32[5,64,256]{2,1,0:T(8,128)}, f32[64,256]{1,0:T(8,128)}) custom-call(f32[40,4,8,128]{3,2,1,0:T(8,128)} %get-tuple-element.45.refs_0_, f32[40,5,8,128]{3,2,1,0:T(8,128)} %get-tuple-element.46.refs_1_, f32[40,4,8,128]{3,2,1,0:T(8,128)} %get-tuple-element.47.refs_2_, f32[40,4,8,128]{3,2,1,0:T(8,128)} %get-tuple-element.48.refs_3_, ...), custom_call_target="tpu_custom_call" | custom-call | tf_op jit(solution)/shard_map/pallas_call | solution.py:717
  (26 shorter events, 0.2 us)
Async XLA Ops:
  0.6 20.2 %copy-start = (f32[16,5]{0,1:T(8,128)S(1)}, f32[16,5]{0,1:T(8,128)}, u32[]{:S(2)}) copy-start(f32[16,5]{0,1:T(8,128)} %param.14) | copy-start | bytes 964
  2.5 7.9 %collective-permute-start = (f32[264,64]{1,0:T(8,128)}, f32[264,64]{1,0:T(8,128)S(1)}, u32[]{:S(2)}, u32[]{:S(2)}) collective-permute-start(f32[264,64]{1,0:T(8,128)} %get-tuple-element.43), channel_id=1, source_target_pairs={{0,1},{1,2},{2,3},{3,0},{4,5},{5,6},{6,7},{7,4},{8,9},{9,10},{10,1... | collective-permute-start | bytes 202760 | tf_op jit(solution)/shard_map/ppermute | solution.py:729
  4.5 5.9 %collective-permute-start.1 = (f32[264,64]{1,0:T(8,128)}, f32[264,64]{1,0:T(8,128)S(1)}, u32[]{:S(2)}, u32[]{:S(2)}) collective-permute-start(f32[264,64]{1,0:T(8,128)} %get-tuple-element.44), channel_id=1, source_target_pairs={{0,3},{1,0},{2,1},{3,2},{4,7},{5,4},{6,5},{7,6},{8,11},{9,8},{10,9... | collective-permute-start | bytes 202760 | tf_op jit(solution)/shard_map/ppermute | solution.py:729
  10.4 0.7 copy-start.7
  10.4 0.7 copy-start.8
  13.8 17.3 %collective-permute-start.5 = (f32[33,3,8,128]{3,2,1,0:T(8,128)}, f32[33,3,8,128]{3,2,1,0:T(8,128)S(1)}, u32[]{:S(2)}, u32[]{:S(2)}) collective-permute-start(f32[33,3,8,128]{3,2,1,0:T(8,128)} %shard_map.96.refs_2_), channel_id=1, source_target_pairs={{0,120},{4,124},{8,0},{12,4},{16,8},{20,12},{24,16},{28,20},{32,24... | collective-permute-start | bytes 1216520 | tf_op jit(solution)/shard_map/ppermute | solution.py:729
  18.1 19.0 %collective-permute-start.4 = (f32[33,3,8,128]{3,2,1,0:T(8,128)}, f32[33,3,8,128]{3,2,1,0:T(8,128)S(1)}, u32[]{:S(2)}, u32[]{:S(2)}) collective-permute-start(f32[33,3,8,128]{3,2,1,0:T(8,128)} %shard_map.96.refs_2_), channel_id=1, source_target_pairs={{0,124},{4,0},{8,4},{12,8},{16,12},{20,16},{24,20},{28,24},{32,28}... | collective-permute-start | bytes 1216520 | tf_op jit(solution)/shard_map/ppermute | solution.py:729
  18.3 21.2 %collective-permute-start.3 = (f32[33,3,8,128]{3,2,1,0:T(8,128)}, f32[33,3,8,128]{3,2,1,0:T(8,128)S(1)}, u32[]{:S(2)}, u32[]{:S(2)}) collective-permute-start(f32[33,3,8,128]{3,2,1,0:T(8,128)} %shard_map.96.refs_2_), channel_id=1, source_target_pairs={{0,4},{4,8},{8,12},{12,16},{16,20},{20,24},{24,28},{28,32},{32,36}... | collective-permute-start | bytes 1216520 | tf_op jit(solution)/shard_map/ppermute | solution.py:729
  20.2 22.5 %collective-permute-start.2 = (f32[33,3,8,128]{3,2,1,0:T(8,128)}, f32[33,3,8,128]{3,2,1,0:T(8,128)S(1)}, u32[]{:S(2)}, u32[]{:S(2)}) collective-permute-start(f32[33,3,8,128]{3,2,1,0:T(8,128)} %shard_map.96.refs_2_), channel_id=1, source_target_pairs={{0,8},{4,12},{8,16},{12,20},{16,24},{20,28},{24,32},{28,36},{32,40... | collective-permute-start | bytes 1216520 | tf_op jit(solution)/shard_map/ppermute | solution.py:729
  31.1 11.6 %copy-start.1 = (f32[33,3,8,128]{3,2,1,0:T(8,128)}, f32[33,3,8,128]{3,2,1,0:T(8,128)S(1)}, u32[]{:S(2)}) copy-start(f32[33,3,8,128]{3,2,1,0:T(8,128)S(1)} %collective-permute-done.5.refs_4_) | copy-start | bytes 1216516
  37.1 5.5 %copy-start.2 = (f32[33,3,8,128]{3,2,1,0:T(8,128)}, f32[33,3,8,128]{3,2,1,0:T(8,128)S(1)}, u32[]{:S(2)}) copy-start(f32[33,3,8,128]{3,2,1,0:T(8,128)S(1)} %collective-permute-done.4.refs_3_) | copy-start | bytes 1216516
  39.5 3.1 %copy-start.3 = (f32[33,3,8,128]{3,2,1,0:T(8,128)}, f32[33,3,8,128]{3,2,1,0:T(8,128)S(1)}, u32[]{:S(2)}) copy-start(f32[33,3,8,128]{3,2,1,0:T(8,128)S(1)} %collective-permute-done.3.refs_1_) | copy-start | bytes 1216516
  42.6 0.8 copy-start.4
  73.3 8.2 %collective-permute-start.6 = (f32[29,8,128]{2,1,0:T(8,128)}, f32[29,8,128]{2,1,0:T(8,128)S(1)}, u32[]{:S(2)}, u32[]{:S(2)}) collective-permute-start(f32[29,8,128]{2,1,0:T(8,128)} %get-tuple-element.68), channel_id=1, source_target_pairs={{0,8},{4,12},{8,16},{12,20},{16,24},{20,28},{24,32},{28,36},{32,40... | collective-permute-start | bytes 356360 | tf_op jit(solution)/shard_map/ppermute | solution.py:729
  74.3 7.1 %collective-permute-start.7 = (f32[29,8,128]{2,1,0:T(8,128)}, f32[29,8,128]{2,1,0:T(8,128)S(1)}, u32[]{:S(2)}, u32[]{:S(2)}) collective-permute-start(f32[29,8,128]{2,1,0:T(8,128)} %get-tuple-element.69), channel_id=1, source_target_pairs={{0,120},{4,124},{8,0},{12,4},{16,8},{20,12},{24,16},{28,20},{32,24... | collective-permute-start | bytes 356360 | tf_op jit(solution)/shard_map/ppermute | solution.py:729
  81.4 0.7 copy-start.9
  81.4 0.7 copy-start.10
  101.4 7.7 %collective-permute-start.9 = (f32[4,10,8,128]{3,2,1,0:T(8,128)}, f32[4,10,8,128]{3,2,1,0:T(8,128)S(1)}, u32[]{:S(2)}, u32[]{:S(2)}) collective-permute-start(f32[4,10,8,128]{3,2,1,0:T(8,128)} %get-tuple-element.71.refs_7_), channel_id=1, source_target_pairs={{0,124},{4,0},{8,4},{12,8},{16,12},{20,16},{24,20},{28,24},{32,28}... | collective-permute-start | bytes 491528 | tf_op jit(solution)/shard_map/ppermute | solution.py:729
  105.9 8.3 %collective-permute-start.8 = (f32[4,10,8,128]{3,2,1,0:T(8,128)}, f32[4,10,8,128]{3,2,1,0:T(8,128)S(1)}, u32[]{:S(2)}, u32[]{:S(2)}) collective-permute-start(f32[4,10,8,128]{3,2,1,0:T(8,128)} %get-tuple-element.71.refs_7_), channel_id=1, source_target_pairs={{0,4},{4,8},{8,12},{12,16},{16,20},{20,24},{24,28},{28,32},{32,36}... | collective-permute-start | bytes 491528 | tf_op jit(solution)/shard_map/ppermute | solution.py:729
  109.1 5.1 %copy-start.5 = (f32[4,10,8,128]{3,2,1,0:T(8,128)}, f32[4,10,8,128]{3,2,1,0:T(8,128)S(1)}, u32[]{:S(2)}) copy-start(f32[4,10,8,128]{3,2,1,0:T(8,128)S(1)} %collective-permute-done.9.refs_9_) | copy-start | bytes 491524
  114.2 0.7 copy-start.6
  119.2 4.7 %collective-permute-start.11 = (f32[4,5,8,128]{3,2,1,0:T(8,128)}, f32[4,5,8,128]{3,2,1,0:T(8,128)S(1)}, u32[]{:S(2)}, u32[]{:S(2)}) collective-permute-start(f32[4,5,8,128]{3,2,1,0:T(8,128)} %get-tuple-element.79.refs_19_), channel_id=1, source_target_pairs={{0,120},{4,124},{8,0},{12,4},{16,8},{20,12},{24,16},{28,20},{32,24... | collective-permute-start | bytes 245768 | tf_op jit(solution)/shard_map/ppermute | solution.py:729
  119.2 7.7 %collective-permute-start.10 = (f32[4,5,8,128]{3,2,1,0:T(8,128)}, f32[4,5,8,128]{3,2,1,0:T(8,128)S(1)}, u32[]{:S(2)}, u32[]{:S(2)}) collective-permute-start(f32[4,5,8,128]{3,2,1,0:T(8,128)} %get-tuple-element.79.refs_19_), channel_id=1, source_target_pairs={{0,8},{4,12},{8,16},{12,20},{16,24},{20,28},{24,32},{28,36},{32,40... | collective-permute-start | bytes 245768 | tf_op jit(solution)/shard_map/ppermute | solution.py:729
  123.9 3.1 %copy-start.11 = (f32[4,5,8,128]{3,2,1,0:T(8,128)}, f32[4,5,8,128]{3,2,1,0:T(8,128)S(1)}, u32[]{:S(2)}) copy-start(f32[4,5,8,128]{3,2,1,0:T(8,128)S(1)} %collective-permute-done.11.refs_21_) | copy-start | bytes 245764
  127.0 0.6 copy-start.12

commit v2 on v1

--- a/solution.py
+++ b/solution.py
@@ -235,17 +235,26 @@
     ]
 
 
-def rows_loop(low, high, body):
-    def step(i, carry):
+def rows_loop(low, high, body, unroll=2):
+    steps = (high - low) // unroll
+
+    def step(n, carry):
+        for j in range(unroll):
+            body(low + n * unroll + j)
+        return carry
+
+    if steps > 1:
+        lax.fori_loop(0, steps, step, 0)
+    elif steps == 1:
+        step(0, 0)
+    for i in range(low + steps * unroll, high):
         body(i)
-        return carry
-
-    lax.fori_loop(low, high, step, 0)
 
 
 class Level:
     def __init__(self, phases, gx, gy, via, below, cap, total, weights):
         self.phases = phases
+        self.unroll = 8 // phases
         self.gx, self.gy = gx, gy
         self.via, self.below = via, below
         self.cap, self.total, self.weights = cap, total, weights
@@ -314,7 +323,7 @@
                 for k, value in enumerate(self.weighted(i, p, values)):
                     target[i, k * self.phases + p] = value
 
-        rows_loop(low, high, body)
+        rows_loop(low, high, body, self.unroll)
 
     def gathered(self, iterate, source, i):
         count = self.phases
@@ -346,7 +355,7 @@
                 for k, value in enumerate(self.weighted(i, p, sums[p])):
                     target[i, k * count + p] = (1.0 - damping) * centres[k][p] + value
 
-        rows_loop(low, high, body)
+        rows_loop(low, high, body, self.unroll)
 
     def residual(self, iterate, source, i):
         centres, sums = self.gathered(iterate, source, i)
@@ -376,7 +385,7 @@
                         two[2 * q][k] + two[2 * q + 1][k]
                     )
 
-        rows_loop(low, high, body)
+        rows_loop(low, high, body, self.unroll // 2)
 
     def correct(self, target, iterate, coarse, low, high, shift=0):
         count, half = self.phases, self.phases // 2
@@ -389,7 +398,7 @@
                     for p in (2 * q, 2 * q + 1):
                         target[i, k * count + p] = iterate[i, k * count + p] + value
 
-        rows_loop(low, high, body)
+        rows_loop(low, high, body, self.unroll)
 
 
 def coarsen(fine, coarse, rows):
@@ -423,7 +432,17 @@
     rows_loop(0, rows, body)
 
 
-def gather_kernel(voltage, capacity, node_class, via, ball, load, whole, left, right, work):
+def gather_kernel(*refs):
+    whole, left, right, work = refs[6:10]
+    voltage, capacity, node_class, via, ball, load = refs[10:16]
+    copies = [
+        pltpu.make_async_copy(source, target, refs[16].at[n])
+        for n, (source, target) in enumerate(zip(refs[:6], refs[10:16]))
+    ]
+    for copy in copies:
+        copy.start()
+    for copy in copies:
+        copy.wait()
     classes = node_class[...]
     conduct = jnp.full(classes.shape, node_table[0], jnp.float32)
     for c in range(1, len(node_table)):
@@ -706,22 +725,27 @@
 
 
 def vregs(*shape):
-    return jax.ShapeDtypeStruct(shape + (LAYERS, LANES), jnp.float32)
+    return pltpu.VMEM(shape + (LAYERS, LANES), jnp.float32)
 
 
 def scratch(*shape):
     return pltpu.VMEM(shape + (LAYERS, LANES), jnp.float32)
 
 
-def call(kernel, inputs, outs, scratches=(), scalars=0):
+def call(kernel, inputs, outs, scratches=(), scalars=0, outside=False):
+    space = pltpu.MemorySpace.HBM if outside else VMEM
+    inputs = [
+        value if n < scalars else pltpu.with_memory_space_constraint(value, space)
+        for n, value in enumerate(inputs)
+    ]
     return pl.pallas_call(
         kernel,
         out_shape=outs,
         in_specs=[pl.BlockSpec(memory_space=SMEM)] * scalars
-        + [pl.BlockSpec(memory_space=VMEM)] * (len(inputs) - scalars),
+        + [pl.BlockSpec(memory_space=space)] * (len(inputs) - scalars),
         out_specs=[pl.BlockSpec(memory_space=VMEM)] * len(outs),
         scratch_shapes=list(scratches),
-        compiler_params=pltpu.CompilerParams(vmem_limit_bytes=60 * 2**20),
+        compiler_params=pltpu.CompilerParams(vmem_limit_bytes=12 * 2**20),
     )(*inputs)
 
 
@@ -747,11 +771,21 @@
             load_type,
         ),
         [
-            jax.ShapeDtypeStruct((264, 256), jnp.float32),
-            jax.ShapeDtypeStruct((264, 64), jnp.float32),
-            jax.ShapeDtypeStruct((264, 64), jnp.float32),
+            pltpu.VMEM((264, 256), jnp.float32),
+            pltpu.VMEM((264, 64), jnp.float32),
+            pltpu.VMEM((264, 64), jnp.float32),
         ],
-        [pltpu.VMEM((4, 2, 64, LANES), jnp.float32)],
+        [
+            pltpu.VMEM((4, 2, 64, LANES), jnp.float32),
+            pltpu.VMEM((64, 256), jnp.float32),
+            pltpu.VMEM((64, 256), jnp.float32),
+            pltpu.VMEM((64, 256), jnp.int32),
+            pltpu.VMEM((56, 256), jnp.int32),
+            pltpu.VMEM((8, 256), jnp.int32),
+            pltpu.VMEM((8, 256), jnp.int32),
+            pltpu.SemaphoreType.DMA((6,)),
+        ],
+        outside=True,
     )
     from_lower = turned(right, "gy", columns, 1)
     from_upper = turned(left, "gy", columns, -1)

time: 140 us -> 92.4 us (0.66)
  Pallas kernels: 70.6 us -> 27.5 us
  local copies, waits for them, and re-layouts: 3.45 us -> 0.01 us
    pallas_call x6, Pallas kernels: 70.6 us -> 27.5 us  [call(): pl.pallas_call(kernel, out_shape=outs, in_specs=[pl.BlockSpec(memory_spac...]
    unnamed x26 -> x4, local copies, waits for them, and re-layouts: 3.45 us -> 0.01 us
  transfers between devices with their start and end apart: 12 -> 12, of which waited for: 10 -> 10; matrix products, arithmetic and copies ran while one was open for 2% -> 1% of each run, Pallas kernels for 0% -> 0%
where the time goes in v2:
time: 92.4 us; the launch traced here: 92.2 us
  waiting for transfers between devices  40.9 us (44%)
  Pallas kernels  27.5 us (30%)
  starting transfers between devices  22.1 us (24%)
    ppermute x12, waiting for transfers between devices, turned(): lax.ppermute(value, axis, [(i, (i + shift) % count) for i in range(count)])  40.9 us
    pallas_call x6, Pallas kernels, call(): pl.pallas_call(kernel, out_shape=outs, in_specs=[pl.BlockSpec(memory_spac...  27.5 us
    ppermute x12, starting transfers between devices, turned(): lax.ppermute(value, axis, [(i, (i + shift) % count) for i in range(count)])  22.1 us
  transfers between devices with their start and end apart: 12, of which 10 were waited for; matrix products, arithmetic and copies ran while one was open for 1% of the time, Pallas kernels for 0%

profile of v2, /device:TPU:0, one launch (start us, length us, event | category | flops | bytes accessed | tf_op | source)
XLA Modules:
  0.0 92.2 jit_solution(6875623534721432303)
XLA Ops:
  0.6 0.0 copy-start
  0.6 1.2 %shard_map.95 = (f32[264,256]{1,0:T(8,128)S(1)}, f32[264,64]{1,0:T(8,128)S(1)}, f32[264,64]{1,0:T(8,128)S(1)}) custom-call(f32[64,256]{1,0:T(8,128)} %bitcast.12, f32[64,256]{1,0:T(8,128)} %bitcast.14, s32[64,256]{1,0:T(8,128)} %bitcast.15, s32[56,256]{1,0:T(8,128)} %bitcast.16, s32[8,256]{1,0:T(8,128)} %refs_4_.1, s32[8,256]{1,0:T(8,128)} %refs_5_.1), custom_call_target="tpu_custom_call" | custom-call | tf_op jit(solution)/shard_map/pallas_call | solution.py:741
  1.8 2.1 %collective-permute-start = (f32[264,64]{1,0:T(8,128)S(1)}, f32[264,64]{1,0:T(8,128)S(1)}, u32[]{:S(2)}, u32[]{:S(2)}) collective-permute-start(f32[264,64]{1,0:T(8,128)S(1)} %get-tuple-element.43), channel_id=1, source_target_pairs={{0,1},{1,2},{2,3},{3,0},{4,5},{5,6},{6,7},{7,4},{8,9},{9,10},{10,1... | collective-permute-start | bytes 202760 | tf_op jit(solution)/shard_map/ppermute | solution.py:753
  3.9 2.2 %collective-permute-start.1 = (f32[264,64]{1,0:T(8,128)S(1)}, f32[264,64]{1,0:T(8,128)S(1)}, u32[]{:S(2)}, u32[]{:S(2)}) collective-permute-start(f32[264,64]{1,0:T(8,128)S(1)} %get-tuple-element.44), channel_id=1, source_target_pairs={{0,3},{1,0},{2,1},{3,2},{4,7},{5,4},{6,5},{7,6},{8,11},{9,8},{10,9... | collective-permute-start | bytes 202760 | tf_op jit(solution)/shard_map/ppermute | solution.py:753
  6.1 3.5 %collective-permute-done.from_lower = f32[264,64]{1,0:T(8,128)S(1)} collective-permute-done((f32[264,64]{1,0:T(8,128)S(1)}, f32[264,64]{1,0:T(8,128)S(1)}, u32[]{:S(2)}, u32[]{:S(2)}) %collective-permute-start) | collective-permute-done | bytes 67616 | tf_op jit(solution)/shard_map/ppermute | solution.py:753
  9.6 0.0 collective-permute-done.1.from_upper
  9.6 0.8 shard_map.96.refs_2_
  10.4 4.4 %collective-permute-start.5 = (f32[33,3,8,128]{3,2,1,0:T(8,128)S(1)}, f32[33,3,8,128]{3,2,1,0:T(8,128)S(1)}, u32[]{:S(2)}, u32[]{:S(2)}) collective-permute-start(f32[33,3,8,128]{3,2,1,0:T(8,128)S(1)} %shard_map.96.refs_2_), channel_id=1, source_target_pairs={{0,120},{4,124},{8,0},{12,4},{16,8},{20,12},{24,16},{28,20},{32,24... | collective-permute-start | bytes 1216520 | tf_op jit(solution)/shard_map/ppermute | solution.py:753
  14.8 0.2 collective-permute-start.4
  15.1 1.8 %collective-permute-start.3 = (f32[33,3,8,128]{3,2,1,0:T(8,128)S(1)}, f32[33,3,8,128]{3,2,1,0:T(8,128)S(1)}, u32[]{:S(2)}, u32[]{:S(2)}) collective-permute-start(f32[33,3,8,128]{3,2,1,0:T(8,128)S(1)} %shard_map.96.refs_2_), channel_id=1, source_target_pairs={{0,4},{4,8},{8,12},{12,16},{16,20},{20,24},{24,28},{28,32},{32,36}... | collective-permute-start | bytes 1216520 | tf_op jit(solution)/shard_map/ppermute | solution.py:753
  16.9 0.0 collective-permute-start.2
  16.9 0.1 pad_add_fusion.place
  17.0 0.9 convolution_bitcast_fusion.mixed_table
  17.9 9.6 %collective-permute-done.5.refs_4_ = f32[33,3,8,128]{3,2,1,0:T(8,128)S(1)} collective-permute-done((f32[33,3,8,128]{3,2,1,0:T(8,128)S(1)}, f32[33,3,8,128]{3,2,1,0:T(8,128)S(1)}, u32[]{:S(2)}, u32[]{:S(2)}) %collective-permute-start.5) | collective-permute-done | bytes 405536 | tf_op jit(solution)/shard_map/ppermute | solution.py:753
  27.5 6.1 %collective-permute-done.4.refs_3_ = f32[33,3,8,128]{3,2,1,0:T(8,128)S(1)} collective-permute-done((f32[33,3,8,128]{3,2,1,0:T(8,128)S(1)}, f32[33,3,8,128]{3,2,1,0:T(8,128)S(1)}, u32[]{:S(2)}, u32[]{:S(2)}) %collective-permute-start.4) | collective-permute-done | bytes 405536 | tf_op jit(solution)/shard_map/ppermute | solution.py:753
  33.6 2.3 %collective-permute-done.3.refs_1_ = f32[33,3,8,128]{3,2,1,0:T(8,128)S(1)} collective-permute-done((f32[33,3,8,128]{3,2,1,0:T(8,128)S(1)}, f32[33,3,8,128]{3,2,1,0:T(8,128)S(1)}, u32[]{:S(2)}, u32[]{:S(2)}) %collective-permute-start.3) | collective-permute-done | bytes 405536 | tf_op jit(solution)/shard_map/ppermute | solution.py:753
  35.9 3.2 %collective-permute-done.2.refs_0_ = f32[33,3,8,128]{3,2,1,0:T(8,128)S(1)} collective-permute-done((f32[33,3,8,128]{3,2,1,0:T(8,128)S(1)}, f32[33,3,8,128]{3,2,1,0:T(8,128)S(1)}, u32[]{:S(2)}, u32[]{:S(2)}) %collective-permute-start.2) | collective-permute-done | bytes 405536 | tf_op jit(solution)/shard_map/ppermute | solution.py:753
  39.1 14.8 %shard_map.97 = (f32[40,4,8,128]{3,2,1,0:T(8,128)S(1)}, f32[40,5,8,128]{3,2,1,0:T(8,128)S(1)}, f32[40,4,8,128]{3,2,1,0:T(8,128)S(1)}, f32[40,4,8,128]{3,2,1,0:T(...) custom-call(s32[2]{0:T(128)S(1)} %pad_add_fusion.place, ...), custom_call_target="tpu_custom_call" | custom-call | tf_op jit(solution)/shard_map/pallas_call | solution.py:741
  53.9 0.3 collective-permute-start.6
  54.3 5.1 %collective-permute-start.7 = (f32[29,8,128]{2,1,0:T(8,128)S(1)}, f32[29,8,128]{2,1,0:T(8,128)S(1)}, u32[]{:S(2)}, u32[]{:S(2)}) collective-permute-start(f32[29,8,128]{2,1,0:T(8,128)S(1)} %get-tuple-element.69), channel_id=1, source_target_pairs={{0,120},{4,124},{8,0},{12,4},{16,8},{20,12},{24,16},{28,20},{32,24... | collective-permute-start | bytes 356360 | tf_op jit(solution)/shard_map/ppermute | solution.py:753
  59.4 2.5 %collective-permute-done.6.refs_23_ = f32[29,8,128]{2,1,0:T(8,128)S(1)} collective-permute-done((f32[29,8,128]{2,1,0:T(8,128)S(1)}, f32[29,8,128]{2,1,0:T(8,128)S(1)}, u32[]{:S(2)}, u32[]{:S(2)}) %collective-permute-start.6) | collective-permute-done | bytes 118816 | tf_op jit(solution)/shard_map/ppermute | solution.py:753
  61.9 0.0 collective-permute-done.7.refs_24_
  61.9 6.2 %shard_map.98 = (f32[40,20,8,128]{3,2,1,0:T(8,128)S(1)}, f32[4,10,8,128]{3,2,1,0:T(8,128)S(1)}, f32[15,1,8,128]{3,2,1,0:T(8,128)S(1)}, f32[14,2,8,128]{3,2,1,0:T...) custom-call(f32[40,4,8,128]{3,2,1,0:T(8,128)S(1)} %get-tuple-element.45.ref, ...), custom_call_target="tpu_custom_call" | custom-call | tf_op jit(solution)/shard_map/pallas_call | solution.py:741
  68.1 3.8 %collective-permute-start.9 = (f32[4,10,8,128]{3,2,1,0:T(8,128)S(1)}, f32[4,10,8,128]{3,2,1,0:T(8,128)S(1)}, u32[]{:S(2)}, u32[]{:S(2)}) collective-permute-start(f32[4,10,8,128]{3,2,1,0:T(8,128)S(1)} %get-tuple-element.71.refs_7_), channel_id=1, source_target_pairs={{0,124},{4,0},{8,4},{12,8},{16,12},{20,16},{24,20},{28,24},{32,28}... | collective-permute-start | bytes 491528 | tf_op jit(solution)/shard_map/ppermute | solution.py:753
  71.9 2.8 %collective-permute-done.9.refs_9_ = f32[4,10,8,128]{3,2,1,0:T(8,128)S(1)} collective-permute-done((f32[4,10,8,128]{3,2,1,0:T(8,128)S(1)}, f32[4,10,8,128]{3,2,1,0:T(8,128)S(1)}, u32[]{:S(2)}, u32[]{:S(2)}) %collective-permute-start.9) | collective-permute-done | bytes 163872 | tf_op jit(solution)/shard_map/ppermute | solution.py:753
  74.7 5.2 %collective-permute-done.8.refs_8_ = f32[4,10,8,128]{3,2,1,0:T(8,128)S(1)} collective-permute-done((f32[4,10,8,128]{3,2,1,0:T(8,128)S(1)}, f32[4,10,8,128]{3,2,1,0:T(8,128)S(1)}, u32[]{:S(2)}, u32[]{:S(2)}) %collective-permute-start.8) | collective-permute-done | bytes 163872 | tf_op jit(solution)/shard_map/ppermute | solution.py:753
  79.9 0.7 shard_map.99
  80.7 0.1 collective-permute-start.11
  80.8 2.0 %collective-permute-start.10 = (f32[4,5,8,128]{3,2,1,0:T(8,128)S(1)}, f32[4,5,8,128]{3,2,1,0:T(8,128)S(1)}, u32[]{:S(2)}, u32[]{:S(2)}) collective-permute-start(f32[4,5,8,128]{3,2,1,0:T(8,128)S(1)} %get-tuple-element.79.refs_19_), channel_id=1, source_target_pairs={{0,8},{4,12},{8,16},{12,20},{16,24},{20,28},{24,32},{28,36},{32,40... | collective-permute-start | bytes 245768 | tf_op jit(solution)/shard_map/ppermute | solution.py:753
  82.8 2.4 %collective-permute-done.11.refs_21_ = f32[4,5,8,128]{3,2,1,0:T(8,128)S(1)} collective-permute-done((f32[4,5,8,128]{3,2,1,0:T(8,128)S(1)}, f32[4,5,8,128]{3,2,1,0:T(8,128)S(1)}, u32[]{:S(2)}, u32[]{:S(2)}) %collective-permute-start.11) | collective-permute-done | bytes 81952 | tf_op jit(solution)/shard_map/ppermute | solution.py:753
  85.2 3.1 %collective-permute-done.10.refs_20_ = f32[4,5,8,128]{3,2,1,0:T(8,128)S(1)} collective-permute-done((f32[4,5,8,128]{3,2,1,0:T(8,128)S(1)}, f32[4,5,8,128]{3,2,1,0:T(8,128)S(1)}, u32[]{:S(2)}, u32[]{:S(2)}) %collective-permute-start.10) | collective-permute-done | bytes 81952 | tf_op jit(solution)/shard_map/ppermute | solution.py:753
  88.3 3.8 %shard_map.100 = (f32[5,64,256]{2,1,0:T(8,128)}, f32[64,256]{1,0:T(8,128)}) custom-call(f32[40,4,8,128]{3,2,1,0:T(8,128)S(1)} %get-tuple-element.45.refs_0_, f32[40,5,8,128]{3,2,1,0:T(8,128)S(1)} %get-tuple-element.46.refs_1_, f32[40,4,8,128]{3,2,1,0:T(8,128)S(1)} %get-tuple-element.47.refs_2_, f32[40,4,8,128]{3,2,1,0:T(8,128)S(1)} %get-tuple-element.48.refs_3_, ...), custom_call_target="tpu_custom_call" | custom-call | tf_op jit(solution)/shard_map/pallas_call | solution.py:741
  (4 shorter events, 0.0 us)
Async XLA Ops:
  0.6 16.4 %copy-start = (f32[16,5]{0,1:T(8,128)S(1)}, f32[16,5]{0,1:T(8,128)}, u32[]{:S(2)}) copy-start(f32[16,5]{0,1:T(8,128)} %param.14) | copy-start | bytes 964
  1.8 7.8 %collective-permute-start = (f32[264,64]{1,0:T(8,128)S(1)}, f32[264,64]{1,0:T(8,128)S(1)}, u32[]{:S(2)}, u32[]{:S(2)}) collective-permute-start(f32[264,64]{1,0:T(8,128)S(1)} %get-tuple-element.43), channel_id=1, source_target_pairs={{0,1},{1,2},{2,3},{3,0},{4,5},{5,6},{6,7},{7,4},{8,9},{9,10},{10,1... | collective-permute-start | bytes 202760 | tf_op jit(solution)/shard_map/ppermute | solution.py:753
  3.9 5.7 %collective-permute-start.1 = (f32[264,64]{1,0:T(8,128)S(1)}, f32[264,64]{1,0:T(8,128)S(1)}, u32[]{:S(2)}, u32[]{:S(2)}) collective-permute-start(f32[264,64]{1,0:T(8,128)S(1)} %get-tuple-element.44), channel_id=1, source_target_pairs={{0,3},{1,0},{2,1},{3,2},{4,7},{5,4},{6,5},{7,6},{8,11},{9,8},{10,9... | collective-permute-start | bytes 202760 | tf_op jit(solution)/shard_map/ppermute | solution.py:753
  10.4 17.0 %collective-permute-start.5 = (f32[33,3,8,128]{3,2,1,0:T(8,128)S(1)}, f32[33,3,8,128]{3,2,1,0:T(8,128)S(1)}, u32[]{:S(2)}, u32[]{:S(2)}) collective-permute-start(f32[33,3,8,128]{3,2,1,0:T(8,128)S(1)} %shard_map.96.refs_2_), channel_id=1, source_target_pairs={{0,120},{4,124},{8,0},{12,4},{16,8},{20,12},{24,16},{28,20},{32,24... | collective-permute-start | bytes 1216520 | tf_op jit(solution)/shard_map/ppermute | solution.py:753
  14.8 18.7 %collective-permute-start.4 = (f32[33,3,8,128]{3,2,1,0:T(8,128)S(1)}, f32[33,3,8,128]{3,2,1,0:T(8,128)S(1)}, u32[]{:S(2)}, u32[]{:S(2)}) collective-permute-start(f32[33,3,8,128]{3,2,1,0:T(8,128)S(1)} %shard_map.96.refs_2_), channel_id=1, source_target_pairs={{0,124},{4,0},{8,4},{12,8},{16,12},{20,16},{24,20},{28,24},{32,28}... | collective-permute-start | bytes 1216520 | tf_op jit(solution)/shard_map/ppermute | solution.py:753
  15.1 20.8 %collective-permute-start.3 = (f32[33,3,8,128]{3,2,1,0:T(8,128)S(1)}, f32[33,3,8,128]{3,2,1,0:T(8,128)S(1)}, u32[]{:S(2)}, u32[]{:S(2)}) collective-permute-start(f32[33,3,8,128]{3,2,1,0:T(8,128)S(1)} %shard_map.96.refs_2_), channel_id=1, source_target_pairs={{0,4},{4,8},{8,12},{12,16},{16,20},{20,24},{24,28},{28,32},{32,36}... | collective-permute-start | bytes 1216520 | tf_op jit(solution)/shard_map/ppermute | solution.py:753
  16.9 22.3 %collective-permute-start.2 = (f32[33,3,8,128]{3,2,1,0:T(8,128)S(1)}, f32[33,3,8,128]{3,2,1,0:T(8,128)S(1)}, u32[]{:S(2)}, u32[]{:S(2)}) collective-permute-start(f32[33,3,8,128]{3,2,1,0:T(8,128)S(1)} %shard_map.96.refs_2_), channel_id=1, source_target_pairs={{0,8},{4,12},{8,16},{12,20},{16,24},{20,28},{24,32},{28,36},{32,40... | collective-permute-start | bytes 1216520 | tf_op jit(solution)/shard_map/ppermute | solution.py:753
  53.9 8.0 %collective-permute-start.6 = (f32[29,8,128]{2,1,0:T(8,128)S(1)}, f32[29,8,128]{2,1,0:T(8,128)S(1)}, u32[]{:S(2)}, u32[]{:S(2)}) collective-permute-start(f32[29,8,128]{2,1,0:T(8,128)S(1)} %get-tuple-element.68), channel_id=1, source_target_pairs={{0,8},{4,12},{8,16},{12,20},{16,24},{20,28},{24,32},{28,36},{32,40... | collective-permute-start | bytes 356360 | tf_op jit(solution)/shard_map/ppermute | solution.py:753
  54.3 7.6 %collective-permute-start.7 = (f32[29,8,128]{2,1,0:T(8,128)S(1)}, f32[29,8,128]{2,1,0:T(8,128)S(1)}, u32[]{:S(2)}, u32[]{:S(2)}) collective-permute-start(f32[29,8,128]{2,1,0:T(8,128)S(1)} %get-tuple-element.69), channel_id=1, source_target_pairs={{0,120},{4,124},{8,0},{12,4},{16,8},{20,12},{24,16},{28,20},{32,24... | collective-permute-start | bytes 356360 | tf_op jit(solution)/shard_map/ppermute | solution.py:753
  61.9 26.4 %copy-start.1 = (f32[8,8,256]{2,1,0:T(8,128)S(1)}, f32[8,8,256]{2,1,0:T(8,128)}, u32[]{:S(2)}) copy-start(f32[8,8,256]{2,1,0:T(8,128)} %param.8) | copy-start | bytes 196612
  68.1 6.7 %collective-permute-start.9 = (f32[4,10,8,128]{3,2,1,0:T(8,128)S(1)}, f32[4,10,8,128]{3,2,1,0:T(8,128)S(1)}, u32[]{:S(2)}, u32[]{:S(2)}) collective-permute-start(f32[4,10,8,128]{3,2,1,0:T(8,128)S(1)} %get-tuple-element.71.refs_7_), channel_id=1, source_target_pairs={{0,124},{4,0},{8,4},{12,8},{16,12},{20,16},{24,20},{28,24},{32,28}... | collective-permute-start | bytes 491528 | tf_op jit(solution)/shard_map/ppermute | solution.py:753
  71.9 8.1 %collective-permute-start.8 = (f32[4,10,8,128]{3,2,1,0:T(8,128)S(1)}, f32[4,10,8,128]{3,2,1,0:T(8,128)S(1)}, u32[]{:S(2)}, u32[]{:S(2)}) collective-permute-start(f32[4,10,8,128]{3,2,1,0:T(8,128)S(1)} %get-tuple-element.71.refs_7_), channel_id=1, source_target_pairs={{0,4},{4,8},{8,12},{12,16},{16,20},{20,24},{24,28},{28,32},{32,36}... | collective-permute-start | bytes 491528 | tf_op jit(solution)/shard_map/ppermute | solution.py:753
  80.7 4.5 %collective-permute-start.11 = (f32[4,5,8,128]{3,2,1,0:T(8,128)S(1)}, f32[4,5,8,128]{3,2,1,0:T(8,128)S(1)}, u32[]{:S(2)}, u32[]{:S(2)}) collective-permute-start(f32[4,5,8,128]{3,2,1,0:T(8,128)S(1)} %get-tuple-element.79.refs_19_), channel_id=1, source_target_pairs={{0,120},{4,124},{8,0},{12,4},{16,8},{20,12},{24,16},{28,20},{32,24... | collective-permute-start | bytes 245768 | tf_op jit(solution)/shard_map/ppermute | solution.py:753
  80.8 7.6 %collective-permute-start.10 = (f32[4,5,8,128]{3,2,1,0:T(8,128)S(1)}, f32[4,5,8,128]{3,2,1,0:T(8,128)S(1)}, u32[]{:S(2)}, u32[]{:S(2)}) collective-permute-start(f32[4,5,8,128]{3,2,1,0:T(8,128)S(1)} %get-tuple-element.79.refs_19_), channel_id=1, source_target_pairs={{0,8},{4,12},{8,16},{12,20},{16,24},{20,28},{24,32},{28,36},{32,40... | collective-permute-start | bytes 245768 | tf_op jit(solution)/shard_map/ppermute | solution.py:753

commit v3 on v2

--- a/solution.py
+++ b/solution.py
@@ -218,21 +218,34 @@
     return lax.broadcasted_iota(jnp.int32, (LAYERS, LANES), 0)
 
 
+def spread(first, second, rim):
+    own = lane_index() < 64
+    inner = (first, pltpu.roll(first, 64, 1), second, pltpu.roll(second, 64, 1))
+    outer = (rim, pltpu.roll(rim, 96, 1), pltpu.roll(rim, 64, 1), pltpu.roll(rim, 32, 1))
+    return [jnp.where(own, near, far) for near, far in zip(inner, outer)]
+
+
+def packed(values):
+    lane = lane_index()
+    dead = (lane >= 80) & (lane < 112)
+    one, two, three, last = values
+    tail = jnp.where(lane < 96, pltpu.roll(last, 96, 1), pltpu.roll(last, 32, 1))
+    return [
+        jnp.where(dead, pltpu.roll(last, 80, 1), one),
+        jnp.where(dead, pltpu.roll(last, 48, 1), two),
+        jnp.where(dead, tail, three),
+    ]
+
+
 def unpacked(packs):
     lane = lane_index()
+    one, two, three = packs
     last = jnp.where(
-        lane < 32,
-        pltpu.roll(packs[0], 32, 1),
-        jnp.where(lane < 64, pltpu.roll(packs[1], 64, 1), pltpu.roll(packs[2], 96, 1)),
-    )
-    return [packs[0], packs[1], packs[2], last]
-
-
-def packed(phases):
-    lane = lane_index()
-    return [
-        jnp.where(lane < 96, phases[s], pltpu.roll(phases[3], 96 - 32 * s, 1)) for s in range(3)
-    ]
+        lane < 64,
+        jnp.where(lane < 32, pltpu.roll(one, 48, 1), pltpu.roll(two, 80, 1)),
+        jnp.where(lane < 96, pltpu.roll(three, 96, 1), pltpu.roll(three, 32, 1)),
+    )
+    return [one, two, three, last]
 
 
 def rows_loop(low, high, body, unroll=2):
@@ -413,27 +426,28 @@
         for q in range(half + 1):
             coarse.gy[row, q] = fine.gy[2 * row, 2 * q] + fine.gy[2 * row + 1, 2 * q]
 
-    rows_loop(0, rows, body)
+    rows_loop(0, rows, body, 4)
 
     def body_gx(row):
         for q in range(half):
             coarse.gx[row, q] = fine.gx[2 * row, 2 * q] + fine.gx[2 * row, 2 * q + 1]
 
-    rows_loop(1, rows, body_gx)
-
-
-def sum_below(fine_below, coarse_below, phases, rows):
+    rows_loop(1, rows, body_gx, 4)
+
+
+def sum_below(fine_below, coarse_below, phases, low, high):
     def body(row):
         for q in range(phases):
             coarse_below[row, q] = (
                 fine_below[2 * row, 2 * q] + fine_below[2 * row, 2 * q + 1]
             ) + (fine_below[2 * row + 1, 2 * q] + fine_below[2 * row + 1, 2 * q + 1])
 
-    rows_loop(0, rows, body)
+    rows_loop(low, high, body, 4)
 
 
 def gather_kernel(*refs):
-    whole, left, right, work = refs[6:10]
+    own, left, right, work = refs[6:10]
+    whole = refs[17]
     voltage, capacity, node_class, via, ball, load = refs[10:16]
     copies = [
         pltpu.make_async_copy(source, target, refs[16].at[n])
@@ -466,6 +480,13 @@
     whole[256:264] = load[...].astype(jnp.float32)
     left[...] = whole[:, :64]
     right[...] = whole[:, 192:]
+    column = lax.broadcasted_iota(jnp.int32, (256, 256), 0)
+    slot = lax.broadcasted_iota(jnp.int32, (256, 256), 1)
+    wanted = 4 * (slot % 64) + slot // 64
+    result = selected(whole[...], jnp.where(column == wanted, 1.0, 0.0).astype(jnp.bfloat16))
+    for n in range(33):
+        for h in range(2):
+            own[n, h] = result[8 * n : 8 * n + 8, 128 * h : 128 * h + 128]
 
 
 def three_parts(value):
@@ -483,47 +504,81 @@
     return high + (middle + low)
 
 
-def phase_kernel(whole, from_lower, from_upper, out):
-    def chooser(first, count):
-        shape = (count, 384)
-        column = first + lax.broadcasted_iota(jnp.int32, shape, 0)
-        slot = lax.broadcasted_iota(jnp.int32, shape, 1)
-        s, lane = slot // 128, slot % 128
-        wanted = jnp.where(lane < 96, 4 * lane + s, 4 * (32 * s + lane - 96) + 3)
-        return jnp.where(column == wanted, 1.0, 0.0).astype(jnp.bfloat16)
-
-    result = selected(whole[...], chooser(64, 256))
-    result = result + selected(from_lower[...], chooser(0, 64))
-    result = result + selected(from_upper[...], chooser(320, 64))
+def rim_kernel(own, from_lower, from_upper, whole):
+    column = lax.broadcasted_iota(jnp.int32, (64, LANES), 0)
+    slot = lax.broadcasted_iota(jnp.int32, (64, LANES), 1)
+    group, place = slot // 32, slot % 32
+    below = (place >= 16) & (column == 4 * (place - 16) + (group + 1) % 4)
+    above = (place < 16) & (column == 4 * place + (group + 2) % 4)
+    result = selected(from_lower[...], jnp.where(below, 1.0, 0.0).astype(jnp.bfloat16))
+    result = result + selected(
+        from_upper[...], jnp.where(above, 1.0, 0.0).astype(jnp.bfloat16)
+    )
     for n in range(33):
-        for s in range(3):
-            out[n, s] = result[8 * n : 8 * n + 8, 128 * s : 128 * s + 128]
-
-
-def setup_kernel(
-    place, mixed_table, *refs
-):
-    blocks = refs[:5]
-    (gx0, gy0, via0, below0, cap0, total0, weights0, f0, x0) = refs[5:14]
-    (gx1, gy1, via1, below1, cap1, total1, weights1, f1, x1) = refs[14:23]
-    (gx2, gy2, below2, cap2, f2, go_up, go_down) = refs[23:30]
-    volt, conduct, surface, spare0, spare1 = refs[30:35]
+        whole[n, 2] = result[8 * n : 8 * n + 8]
+        for h in range(2):
+            whole[n, h] = own[n, h]
+
+
+def edge_kernel(near_lower, near_upper, go_right, go_left):
+    lane = lane_index()
+    group = lane // 32
+    late = lane % 32 >= 16
+
+    def chosen(one, two, three, four):
+        return jnp.where(
+            group < 2, jnp.where(group == 0, one, two), jnp.where(group == 2, three, four)
+        )
+
+    def body(n):
+        rights, lefts = [], []
+        for block in (near_lower, near_upper):
+            first, second = block[n, 0], block[n, 1]
+            first_far, first_near = pltpu.roll(first, 64, 1), pltpu.roll(first, 32, 1)
+            second_far = pltpu.roll(second, 96, 1)
+            rights.append(chosen(first_near, second, second_far, first_far))
+            lefts.append(chosen(second, second_far, first_far, first_near))
+        go_right[n] = jnp.where(late, rights[0], pltpu.roll(rights[1], 112, 1))
+        go_left[n] = jnp.where(late, pltpu.roll(lefts[1], 16, 1), lefts[0])
+
+    rows_loop(0, 33, body, 11)
+
+
+def prepare(place, mixed_table, state, f1, blocks, gx_rows, total_rows, relax_rows, sum_rows):
+    (gx0, gy0, via0, below0, cap0, total0, weights0, f0, x0) = state[:9]
+    below1, volt, conduct, surface, spare = state[9:14]
     fine = Level(4, gx0, gy0, via0, below0, cap0, total0, weights0)
-    middle = Level(2, gx1, gy1, via1, below1, cap1, total1, weights1)
-    coarse = Level(1, gx2, gy2, None, below2, cap2, None, None)
     row_block, column_block = place[0], place[1]
     lane = lane_index()
-
-    for b, block in enumerate(blocks):
-
-        def spread(s, block=block, b=b):
+    edge = ((lane == 0) & (column_block == 0)) | ((lane == 64) & (column_block == 3))
+    joined = jnp.where(edge, 0.0, 2.0)
+    top = layer_index() == LAYERS - 1
+
+    def series(near, far):
+        return 2.0 * near * far / (near + far)
+
+    def set_gy(i):
+        here = [conduct[i, p] for p in range(4)]
+        before = from_left(here[3])
+        first = joined * before * here[0] / (before + here[0])
+        gy0[i, 0] = first
+        for p in range(1, 4):
+            gy0[i, p] = series(here[p - 1], here[p])
+
+    def turn_gy(i):
+        gy0[i, 4] = from_right(gy0[i, 0])
+
+    for b, block, rim in blocks:
+
+        def place_row(s, block=block, rim=rim, b=b):
             for a, ref in enumerate((volt, cap0, conduct, below0)):
-                phases = unpacked([block[4 * s + a, t] for t in range(3)])
+                n = 4 * s + a
+                phases = spread(block[n, 0], block[n, 1], rim(n))
                 for p in range(4):
                     ref[8 * b + s, p] = phases[p]
 
-        rows_loop(0, 8, spread)
-        loads = unpacked([block[32, t] for t in range(3)])
+        rows_loop(0, 8, place_row, 4)
+        loads = spread(block[32, 0], block[32, 1], rim(32))
         for p in range(4):
             values = [jnp.zeros((8, LANES), jnp.float32) for _ in range(SECTIONS)]
             for t in range(LOADS):
@@ -533,36 +588,15 @@
                 ]
             for k in range(SECTIONS):
                 surface[4 * k + p, 8 * b : 8 * b + 8] = values[k]
-
-    def series(near, far):
-        return 2.0 * near * far / (near + far)
+        rows_loop(8 * b, 8 * b + 8, set_gy, 8)
+        rows_loop(8 * b, 8 * b + 8, turn_gy, 8)
+        sum_below(below0, below1, 2, 4 * b, 4 * b + 4)
 
     def set_gx(i):
         row = 8 * row_block - 16 + i
         inside = jnp.where((row == 0) | (row == 256), 0.0, 1.0).astype(jnp.float32)
         for p in range(4):
             gx0[i, p] = inside * series(conduct[i - 1, p], conduct[i, p])
-
-    rows_loop(1, EXT0, set_gx)
-    edge = ((lane == 16) & (column_block == 0)) | ((lane == 80) & (column_block == 3))
-
-    def set_gy(i):
-        here = [conduct[i, p] for p in range(4)]
-        first = jnp.where(edge, 0.0, series(from_left(here[3]), here[0]))
-        gy0[i, 0] = first
-        for p in range(1, 4):
-            gy0[i, p] = series(here[p - 1], here[p])
-        gy0[i, 4] = from_right(first)
-
-    rows_loop(0, EXT0, set_gy)
-    coarsen(fine, middle, EXT1)
-    sum_below(below0, below1, 2, EXT1)
-    coarsen(middle, coarse, EXT2)
-    sum_below(below1, below2, 1, EXT2)
-    rows_loop(1, EXT0 - 1, fine.set_total)
-    rows_loop(1, EXT1 - 1, middle.set_total)
-
-    top = layer_index() == LAYERS - 1
 
     def set_source(i):
         centre = [volt[i, p] for p in range(4)]
@@ -576,11 +610,85 @@
                 values.append(jnp.where(top, drawn, 0.0) - ROW_SUMS[k] * leak)
                 f0[i, 4 * k + p] = values[k]
             for k, value in enumerate(fine.weighted(i, p, values)):
-                spare0[i, 4 * k + p] = value
-
-    rows_loop(1, EXT0 - 1, set_source)
-    fine.relax(x0, spare0, f0, 2, 38)
-    fine.restrict(f1, x0, f0, 2, 18)
+                spare[i, 4 * k + p] = value
+
+    for low, high in gx_rows:
+        rows_loop(low, high, set_gx, 4)
+    for low, high in total_rows:
+        rows_loop(low, high, fine.set_total)
+        rows_loop(low, high, set_source)
+    for low, high in relax_rows:
+        fine.relax(x0, spare, f0, low, high)
+    for low, high in sum_rows:
+        fine.restrict(f1, x0, f0, low, high)
+
+
+STATE = 14
+
+
+def own_kernel(place, mixed_table, whole, *refs):
+    prepare(
+        place,
+        mixed_table,
+        refs,
+        None,
+        ((2, whole, lambda n: whole[n, 2]),),
+        ((17, 24),),
+        ((17, 23),),
+        ((18, 22),),
+        (),
+    )
+
+
+def near_kernel(place, mixed_table, near_lower, near_upper, edge_left, edge_right, *refs):
+    refs = refs[STATE:]
+    late = lane_index() % 32 >= 16
+
+    def rim_lower(n):
+        return jnp.where(late, edge_left[n], edge_right[n])
+
+    def rim_upper(n):
+        return jnp.where(
+            late, pltpu.roll(edge_left[n], 16, 1), pltpu.roll(edge_right[n], 112, 1)
+        )
+
+    prepare(
+        place,
+        mixed_table,
+        refs[:STATE],
+        refs[STATE],
+        ((1, near_lower, rim_lower), (3, near_upper, rim_upper)),
+        ((9, 17), (24, 32)),
+        ((9, 17), (23, 31)),
+        ((10, 18), (22, 30)),
+        ((6, 14),),
+    )
+
+
+def setup_kernel(place, mixed_table, far_lower, far_upper, *refs):
+    refs = refs[STATE + 1 :]
+    state, f1 = refs[:STATE], refs[STATE]
+    gx1, gy1, via1, cap1, total1, weights1, x1 = refs[STATE + 1 : STATE + 8]
+    gx2, gy2, below2, cap2, f2, go_up, go_down, spare1 = refs[STATE + 8 :]
+    below1 = state[9]
+    prepare(
+        place,
+        mixed_table,
+        state,
+        f1,
+        ((0, far_lower, lambda n: far_lower[n, 2]), (4, far_upper, lambda n: far_upper[n, 2])),
+        ((1, 9), (32, 40)),
+        ((1, 9), (31, 39)),
+        ((2, 10), (30, 38)),
+        ((2, 6), (14, 18)),
+    )
+    fine = Level(4, *state[:7])
+    middle = Level(2, gx1, gy1, via1, below1, cap1, total1, weights1)
+    coarse = Level(1, gx2, gy2, None, below2, cap2, None, None)
+    coarsen(fine, middle, EXT1)
+    coarsen(middle, coarse, EXT2)
+    sum_below(below1, below2, 1, 0, EXT2)
+    rows_loop(1, EXT1 - 1, middle.set_total)
     middle.first_relax(spare1, f1, 2, 18)
     middle.relax(x1, spare1, f1, 3, 17)
     middle.restrict(f2, x1, f1, 2, 8)
@@ -600,8 +708,8 @@
     (gx0, gy0, via0, below0, cap0, total0, weights0, f0, x0) = refs[0:9]
     (gx1, gy1, via1, below1, cap1, total1, weights1, f1, x1) = refs[9:18]
     (gx2, gy2, below2, cap2, f2, from_lower, from_upper) = refs[18:25]
-    (x0_out, f1_out, gxw, gyw, viaw, beloww, weightsw) = refs[25:32]
-    (capw, totalw, fw, xa, xb, ya, yb, za) = refs[32:40]
+    (x0_out, f1_out, go_side, gxw, gyw, viaw, beloww, weightsw) = refs[25:33]
+    (capw, totalw, fw, xa, xb, ya, yb, za, f1_own) = refs[33:42]
     fine = Level(4, gx0, gy0, via0, below0, cap0, total0, weights0)
     middle = Level(2, gx1, gy1, via1, below1, cap1, total1, weights1)
     coarse = Level(1, gxw, gyw, viaw, beloww, capw, totalw, weightsw)
@@ -641,7 +749,14 @@
     fine.relax(za, x0_out, f0, 12, 28)
     fine.relax(x0_out, za, f0, 13, 27)
     fine.relax(za, x0_out, f0, 14, 26)
-    fine.restrict(f1_out, za, f0, 8, 12, -8)
+    fine.restrict(f1_own, za, f0, 8, 12, -8)
+    for j in range(4):
+        for n in range(10):
+            f1_out[10 * j + n] = f1_own[j, n]
+    for j in range(10):
+        packs = packed([f1_own[n // 10, n % 10] for n in range(4 * j, 4 * j + 4)])
+        for t in range(3):
+            go_side[3 * j + t] = packs[t]
 
     def keep(i):
         for n in range(20):
@@ -656,11 +771,14 @@
     f1, x1, f2_out = refs[10:13]
     (xa,) = refs[13:14]
     middle = Level(2, gx1, gy1, via1, below1, cap1, total1, weights1)
-    for j in range(4):
-        for n in range(10):
-            f1[4 + j, n] = from_lower[j, n]
-            f1[8 + j, n] = own[j, n]
-            f1[12 + j, n] = from_upper[j, n]
+    for j in range(10):
+        for first, source in ((4, from_lower), (12, from_upper)):
+            values = unpacked([source[3 * j + t] for t in range(3)])
+            for t in range(4):
+                n = 4 * j + t
+                f1[first + n // 10, n % 10] = values[t]
+        for n in range(4 * j, 4 * j + 4):
+            f1[8 + n // 10, n % 10] = own[n]
     middle.first_relax(xa, f1, 4, 16)
     middle.relax(x1, xa, f1, 5, 15)
     middle.restrict(f2_out, x1, f1, 3, 7, -3)
@@ -705,7 +823,7 @@
     for p in range(4):
         lane = lax.broadcasted_iota(jnp.int32, (LANES, 256), 0)
         column = lax.broadcasted_iota(jnp.int32, (LANES, 256), 1)
-        chooser = jnp.where(column == 4 * (lane - 16) + p, 1.0, 0.0).astype(jnp.bfloat16)
+        chooser = jnp.where((lane < 64) & (column == 4 * lane + p), 1.0, 0.0).astype(jnp.bfloat16)
         part = selected(mixed[p].reshape(320, LANES), chooser)
         result = part if result is None else result + part
     for j in range(SECTIONS):
@@ -732,7 +850,7 @@
     return pltpu.VMEM(shape + (LAYERS, LANES), jnp.float32)
 
 
-def call(kernel, inputs, outs, scratches=(), scalars=0, outside=False):
+def call(kernel, inputs, outs, scratches=(), scalars=0, outside=False, aliases=()):
     space = pltpu.MemorySpace.HBM if outside else VMEM
     inputs = [
         value if n < scalars else pltpu.with_memory_space_constraint(value, space)
@@ -745,6 +863,7 @@
         + [pl.BlockSpec(memory_space=space)] * (len(inputs) - scalars),
         out_specs=[pl.BlockSpec(memory_space=VMEM)] * len(outs),
         scratch_shapes=list(scratches),
+        input_output_aliases=dict(aliases),
         compiler_params=pltpu.CompilerParams(vmem_limit_bytes=12 * 2**20),
     )(*inputs)
 
@@ -760,7 +879,7 @@
     rows = lax.axis_size("section") * lax.axis_size("gx")
     columns = lax.axis_size("gy")
     volts = voltage.reshape(64, 256)
-    whole, left, right = call(
+    own, left, right = call(
         gather_kernel,
         (
             volts,
@@ -771,7 +890,7 @@
             load_type,
         ),
         [
-            pltpu.VMEM((264, 256), jnp.float32),
+            vregs(33, 2),
             pltpu.VMEM((264, 64), jnp.float32),
             pltpu.VMEM((264, 64), jnp.float32),
         ],
@@ -784,9 +903,11 @@
             pltpu.VMEM((8, 256), jnp.int32),
             pltpu.VMEM((8, 256), jnp.int32),
             pltpu.SemaphoreType.DMA((6,)),
+            pltpu.VMEM((264, 256), jnp.float32),
         ],
         outside=True,
     )
+    near_lower, near_upper = (turned(own, ROWS, rows, s) for s in (1, -1))
     from_lower = turned(right, "gy", columns, 1)
     from_upper = turned(left, "gy", columns, -1)
     mixed_table = jnp.einsum(
@@ -798,9 +919,12 @@
             lax.axis_index("gy"),
         ]
     ).astype(jnp.int32)
-    (block,) = call(phase_kernel, (whole, from_lower, from_upper), [vregs(33, 3)])
-    blocks = [turned(block, ROWS, rows, s) if s else block for s in (2, 1, 0, -1, -2)]
-    level0 = [
+    (whole,) = call(rim_kernel, (own, from_lower, from_upper), [vregs(33, 3)])
+    far_lower, far_upper = (turned(whole, ROWS, rows, s) for s in (2, -2))
+    go_right, go_left = call(edge_kernel, (near_lower, near_upper), [vregs(33), vregs(33)])
+    edge_left = turned(go_right, "gy", columns, 1)
+    edge_right = turned(go_left, "gy", columns, -1)
+    state_shapes = [
         vregs(EXT0, 4),
         vregs(EXT0, 5),
         vregs(EXT0, 4),
@@ -810,42 +934,60 @@
         vregs(EXT0, 20),
         vregs(EXT0, 20),
         vregs(EXT0, 20),
+        vregs(EXT1, 2),
+        vregs(EXT0, 4),
+        vregs(EXT0, 4),
+        pltpu.VMEM((20, EXT0, LANES), jnp.float32),
+        vregs(EXT0, 20),
     ]
-    level1 = [
-        vregs(EXT1, 2),
-        vregs(EXT1, 3),
-        vregs(EXT1, 2),
-        vregs(EXT1, 2),
-        vregs(EXT1, 2),
-        vregs(EXT1, 2),
-        vregs(EXT1, 10),
-        vregs(EXT1, 10),
-        vregs(EXT1, 10),
-    ]
-    level2 = [vregs(EXT2, 1), vregs(EXT2, 2), vregs(EXT2, 1), vregs(EXT2, 1), vregs(EXT2, 5)]
+    state = call(own_kernel, (place, mixed_table, whole), state_shapes, (), 2)
+    state = call(
+        near_kernel,
+        (place, mixed_table, near_lower, near_upper, edge_left, edge_right, *state),
+        [*state_shapes, vregs(EXT1, 10)],
+        (),
+        2,
+        aliases=[(6 + n, n) for n in range(STATE)],
+    )
     state = call(
         setup_kernel,
-        (place, mixed_table, *blocks),
-        level0 + level1 + level2 + [vregs(29), vregs(29)],
+        (place, mixed_table, far_lower, far_upper, *state),
         [
-            scratch(EXT0, 4),
-            scratch(EXT0, 4),
-            pltpu.VMEM((20, EXT0, LANES), jnp.float32),
-            scratch(EXT0, 20),
-            scratch(EXT1, 10),
+            *state_shapes,
+            vregs(EXT1, 10),
+            vregs(EXT1, 2),
+            vregs(EXT1, 3),
+            vregs(EXT1, 2),
+            vregs(EXT1, 2),
+            vregs(EXT1, 2),
+            vregs(EXT1, 10),
+            vregs(EXT1, 10),
+            vregs(EXT2, 1),
+            vregs(EXT2, 2),
+            vregs(EXT2, 1),
+            vregs(EXT2, 1),
+            vregs(EXT2, 5),
+            vregs(29),
+            vregs(29),
         ],
+        [scratch(EXT1, 10)],
         2,
-    )
-    fine, middle, coarse = state[0:9], state[9:18], state[18:23]
-    go_up, go_down = state[23:25]
+        aliases=[(4 + n, n) for n in range(STATE + 1)],
+    )
+    fine, below1, f1 = state[:9], state[9], state[STATE]
+    gx1, gy1, via1, cap1, total1, weights1, x1 = state[STATE + 1 : STATE + 8]
+    middle = (gx1, gy1, via1, below1, cap1, total1, weights1, f1, x1)
+    coarse = state[STATE + 8 : STATE + 13]
+    go_up, go_down = state[STATE + 13 :]
     lower = turned(go_up, ROWS, rows, 2)
     upper = turned(go_down, ROWS, rows, -2)
-    x0, f1_own, gxw, gyw, viaw, beloww, weightsw = call(
+    x0, f1_own, go_side, gxw, gyw, viaw, beloww, weightsw = call(
         middle_kernel,
         (*fine, *middle, *coarse, lower, upper),
         [
             vregs(EXT0, 20),
-            vregs(4, 10),
+            vregs(40),
+            vregs(30),
             vregs(WIDE2 + 1, 1),
             vregs(WIDE2, 2),
             vregs(WIDE2, 1),
@@ -861,10 +1003,11 @@
             scratch(EXT1, 10),
             scratch(EXT1, 10),
             scratch(EXT0, 20),
+            scratch(4, 10),
         ],
     )
-    lower = turned(f1_own, ROWS, rows, 1)
-    upper = turned(f1_own, ROWS, rows, -1)
+    lower = turned(go_side, ROWS, rows, 1)
+    upper = turned(go_side, ROWS, rows, -1)
     f1, x1, f2_own = call(
         lower_kernel,
         (*middle[:7], f1_own, lower, upper),

time: 92.4 us -> 78.1 us (0.85)
  waiting for transfers between devices: 40.9 us -> 21.7 us
  starting transfers between devices: 22.1 us -> 28.1 us
  Pallas kernels: 27.5 us -> 26.4 us
    ppermute x12 -> x14, waiting for transfers between devices: 40.9 us -> 21.7 us  [turned(): lax.ppermute(value, axis, [(i, (i + shift) % count) for i in range(count)])]
    ppermute x12 -> x14, starting transfers between devices: 22.1 us -> 28.1 us  [turned(): lax.ppermute(value, axis, [(i, (i + shift) % count) for i in range(count)])]
    pallas_call x6 -> x9, Pallas kernels: 27.5 us -> 26.4 us  [call(): pl.pallas_call(kernel, out_shape=outs, in_specs=[pl.BlockSpec(memory_spac...]
  transfers between devices with their start and end apart: 12 -> 14, of which waited for: 10 -> 8; matrix products, arithmetic and copies ran while one was open for 1% -> 1% of each run, Pallas kernels for 0% -> 10%
where the time goes in v3:
time: 78.1 us; the launch traced here: 77.9 us
  starting transfers between devices  28.1 us (36%)
  Pallas kernels  26.4 us (34%)
  waiting for transfers between devices  21.7 us (28%)
  matrix products  0.88 us (1%)
    ppermute x14, starting transfers between devices, turned(): lax.ppermute(value, axis, [(i, (i + shift) % count) for i in range(count)])  28.1 us
    pallas_call x9, Pallas kernels, call(): pl.pallas_call(kernel, out_shape=outs, in_specs=[pl.BlockSpec(memory_spac...  26.4 us
    ppermute x14, waiting for transfers between devices, turned(): lax.ppermute(value, axis, [(i, (i + shift) % count) for i in range(count)])  21.7 us
  transfers between devices with their start and end apart: 14, of which 8 were waited for; matrix products, arithmetic and copies ran while one was open for 1% of the time, Pallas kernels for 10%

profile of v3, /device:TPU:0, one launch (start us, length us, event | category | flops | bytes accessed | tf_op | source)
XLA Modules:
  0.0 77.9 jit_solution(7765004728822860136)
XLA Ops:
  0.6 0.0 copy-start
  0.6 1.3 %shard_map.95 = (f32[33,2,8,128]{3,2,1,0:T(8,128)S(1)}, f32[264,64]{1,0:T(8,128)S(1)}, f32[264,64]{1,0:T(8,128)S(1)}) custom-call(f32[64,256]{1,0:T(8,128)} %bitcast.12, f32[64,256]{1,0:T(8,128)} %bitcast.14, s32[64,256]{1,0:T(8,128)} %bitcast.15, s32[56,256]{1,0:T(8,128)} %bitcast.16, s32[8,256]{1,0:T(8,128)} %refs_4_.1, s32[8,256]{1,0:T(8,128)} %refs_5_.1), custom_call_target="tpu_custom_call" | custom-call | tf_op jit(solution)/shard_map/pallas_call | solution.py:859
  2.0 4.8 %collective-permute-start.5 = (f32[33,2,8,128]{3,2,1,0:T(8,128)S(1)}, f32[33,2,8,128]{3,2,1,0:T(8,128)S(1)}, u32[]{:S(2)}, u32[]{:S(2)}) collective-permute-start(f32[33,2,8,128]{3,2,1,0:T(8,128)S(1)} %get-tuple-element.74.own), channel_id=1, source_target_pairs={{0,124},{4,0},{8,4},{12,8},{16,12},{20,16},{24,20},{28,24},{32,28}... | collective-permute-start | bytes 811016 | tf_op jit(solution)/shard_map/ppermute | solution.py:872
  6.8 1.9 %collective-permute-start = (f32[264,64]{1,0:T(8,128)S(1)}, f32[264,64]{1,0:T(8,128)S(1)}, u32[]{:S(2)}, u32[]{:S(2)}) collective-permute-start(f32[264,64]{1,0:T(8,128)S(1)} %get-tuple-element.75), channel_id=1, source_target_pairs={{0,1},{1,2},{2,3},{3,0},{4,5},{5,6},{6,7},{7,4},{8,9},{9,10},{10,1... | collective-permute-start | bytes 202760 | tf_op jit(solution)/shard_map/ppermute | solution.py:872
  8.7 2.1 %collective-permute-start.1 = (f32[264,64]{1,0:T(8,128)S(1)}, f32[264,64]{1,0:T(8,128)S(1)}, u32[]{:S(2)}, u32[]{:S(2)}) collective-permute-start(f32[264,64]{1,0:T(8,128)S(1)} %get-tuple-element.76), channel_id=1, source_target_pairs={{0,3},{1,0},{2,1},{3,2},{4,7},{5,4},{6,5},{7,6},{8,11},{9,8},{10,9... | collective-permute-start | bytes 202760 | tf_op jit(solution)/shard_map/ppermute | solution.py:872
  10.8 3.2 %collective-permute-done.from_lower = f32[264,64]{1,0:T(8,128)S(1)} collective-permute-done((f32[264,64]{1,0:T(8,128)S(1)}, f32[264,64]{1,0:T(8,128)S(1)}, u32[]{:S(2)}, u32[]{:S(2)}) %collective-permute-start) | collective-permute-done | bytes 67616 | tf_op jit(solution)/shard_map/ppermute | solution.py:872
  14.0 0.4 shard_map.96.whole
  14.4 0.8 collective-permute-start.3
  15.1 1.3 %collective-permute-start.2 = (f32[33,3,8,128]{3,2,1,0:T(8,128)S(1)}, f32[33,3,8,128]{3,2,1,0:T(8,128)S(1)}, u32[]{:S(2)}, u32[]{:S(2)}) collective-permute-start(f32[33,3,8,128]{3,2,1,0:T(8,128)S(1)} %shard_map.96.whole), channel_id=1, source_target_pairs={{0,8},{4,12},{8,16},{12,20},{16,24},{20,28},{24,32},{28,36},{32,40... | collective-permute-start | bytes 1216520 | tf_op jit(solution)/shard_map/ppermute | solution.py:872
  16.5 1.7 %collective-permute-done.4.near_lower = f32[33,2,8,128]{3,2,1,0:T(8,128)S(1)} collective-permute-done((f32[33,2,8,128]{3,2,1,0:T(8,128)S(1)}, f32[33,2,8,128]{3,2,1,0:T(8,128)S(1)}, u32[]{:S(2)}, u32[]{:S(2)}) %collective-permute-start.4) | collective-permute-done | bytes 270368 | tf_op jit(solution)/shard_map/ppermute | solution.py:872
  18.2 0.5 shard_map.97
  18.7 2.0 %collective-permute-start.6 = (f32[33,8,128]{2,1,0:T(8,128)S(1)}, f32[33,8,128]{2,1,0:T(8,128)S(1)}, u32[]{:S(2)}, u32[]{:S(2)}) collective-permute-start(f32[33,8,128]{2,1,0:T(8,128)S(1)} %get-tuple-element.77), channel_id=1, source_target_pairs={{0,1},{1,2},{2,3},{3,0},{4,5},{5,6},{6,7},{7,4},{8,9},{9,10},{10,1... | collective-permute-start | bytes 405512 | tf_op jit(solution)/shard_map/ppermute | solution.py:872
  20.7 2.2 %collective-permute-start.7 = (f32[33,8,128]{2,1,0:T(8,128)S(1)}, f32[33,8,128]{2,1,0:T(8,128)S(1)}, u32[]{:S(2)}, u32[]{:S(2)}) collective-permute-start(f32[33,8,128]{2,1,0:T(8,128)S(1)} %get-tuple-element.78), channel_id=1, source_target_pairs={{0,3},{1,0},{2,1},{3,2},{4,7},{5,4},{6,5},{7,6},{8,11},{9,8},{10,9... | collective-permute-start | bytes 405512 | tf_op jit(solution)/shard_map/ppermute | solution.py:872
  22.9 0.9 %convolution_bitcast_fusion.mixed_table = f32[16,5]{1,0:T(8,128)S(1)} fusion(f32[5,5]{1,0:T(8,128)} %constant.17.clone, f32[16,5]{0,1:T(8,128)S(1)} %copy-done), kind=kOutput, calls=%fused_computation | convolution fusion | flops 4800 | bytes 740 | tf_op jit(solution)/shard_map/tk,jk->tj/dot_general | solution.py:913
  23.8 0.1 pad_add_fusion.place
  23.9 1.8 %shard_map.98 = (f32[40,4,8,128]{3,2,1,0:T(8,128)S(1)}, f32[40,5,8,128]{3,2,1,0:T(8,128)S(1)}, f32[40,4,8,128]{3,2,1,0:T(8,128)S(1)}, f32[40,4,8,128]{3,2,1,0:T(...) custom-call(s32[2]{0:T(128)S(1)} %pad_add_fusion.place, ...), custom_call_target="tpu_custom_call" | custom-call | tf_op jit(solution)/shard_map/pallas_call | solution.py:859
  25.7 1.1 %collective-permute-done.6.edge_left = f32[33,8,128]{2,1,0:T(8,128)S(1)} collective-permute-done((f32[33,8,128]{2,1,0:T(8,128)S(1)}, f32[33,8,128]{2,1,0:T(8,128)S(1)}, u32[]{:S(2)}, u32[]{:S(2)}) %collective-permute-start.6) | collective-permute-done | bytes 135200 | tf_op jit(solution)/shard_map/ppermute | solution.py:872
  26.8 5.0 %shard_map.99 = (f32[40,4,8,128]{3,2,1,0:T(8,128)S(1)}, f32[40,5,8,128]{3,2,1,0:T(8,128)S(1)}, f32[40,4,8,128]{3,2,1,0:T(8,128)S(1)}, f32[40,4,8,128]{3,2,1,0:T(...) custom-call(s32[2]{0:T(128)S(1)} %pad_add_fusion.place, ...), custom_call_target="tpu_custom_call", output_to_operand_aliasing={{0}: (6, {}), {1}: (7, {}), {2}: (8, {}), {3}: (9, {}), {4}... | custom-call | tf_op jit(solution)/shard_map/pallas_call | solution.py:859
  31.9 6.3 %shard_map.100 = (f32[40,4,8,128]{3,2,1,0:T(8,128)S(1)}, f32[40,5,8,128]{3,2,1,0:T(8,128)S(1)}, f32[40,4,8,128]{3,2,1,0:T(8,128)S(1)}, f32[40,4,8,128]{3,2,1,0:T...) custom-call(s32[2]{0:T(128)S(1)} %pad_add_fusion.place, ...), custom_call_target="tpu_custom_call", output_to_operand_aliasing={{0}: (4, {}), {1}: (5, {}), {2}: (6, {}), {3}: (7, {}), {4}... | custom-call | tf_op jit(solution)/shard_map/pallas_call | solution.py:859
  38.2 0.1 collective-permute-start.8
  38.3 5.3 %collective-permute-start.9 = (f32[29,8,128]{2,1,0:T(8,128)S(1)}, f32[29,8,128]{2,1,0:T(8,128)S(1)}, u32[]{:S(2)}, u32[]{:S(2)}) collective-permute-start(f32[29,8,128]{2,1,0:T(8,128)S(1)} %get-tuple-element.132), channel_id=1, source_target_pairs={{0,120},{4,124},{8,0},{12,4},{16,8},{20,12},{24,16},{28,20},{32,24... | collective-permute-start | bytes 356360 | tf_op jit(solution)/shard_map/ppermute | solution.py:872
  43.7 2.5 %collective-permute-done.8.refs_23_ = f32[29,8,128]{2,1,0:T(8,128)S(1)} collective-permute-done((f32[29,8,128]{2,1,0:T(8,128)S(1)}, f32[29,8,128]{2,1,0:T(8,128)S(1)}, u32[]{:S(2)}, u32[]{:S(2)}) %collective-permute-start.8) | collective-permute-done | bytes 118816 | tf_op jit(solution)/shard_map/ppermute | solution.py:872
  46.2 6.3 %shard_map.101 = (f32[40,20,8,128]{3,2,1,0:T(8,128)S(1)}, f32[40,8,128]{2,1,0:T(8,128)S(1)}, f32[30,8,128]{2,1,0:T(8,128)S(1)}, f32[15,1,8,128]{3,2,1,0:T(8,128)...) custom-call(f32[40,4,8,128]{3,2,1,0:T(8,128)S(1)} %get-tuple-element, ...), custom_call_target="tpu_custom_call" | custom-call | tf_op jit(solution)/shard_map/pallas_call | solution.py:859
  52.5 5.5 %collective-permute-start.11 = (f32[30,8,128]{2,1,0:T(8,128)S(1)}, f32[30,8,128]{2,1,0:T(8,128)S(1)}, u32[]{:S(2)}, u32[]{:S(2)}) collective-permute-start(f32[30,8,128]{2,1,0:T(8,128)S(1)} %get-tuple-element.135), channel_id=1, source_target_pairs={{0,124},{4,0},{8,4},{12,8},{16,12},{20,16},{24,20},{28,24},{32,28}... | collective-permute-start | bytes 368648 | tf_op jit(solution)/shard_map/ppermute | solution.py:872
  58.0 2.4 %collective-permute-done.11.refs_9_ = f32[30,8,128]{2,1,0:T(8,128)S(1)} collective-permute-done((f32[30,8,128]{2,1,0:T(8,128)S(1)}, f32[30,8,128]{2,1,0:T(8,128)S(1)}, u32[]{:S(2)}, u32[]{:S(2)}) %collective-permute-start.11) | collective-permute-done | bytes 122912 | tf_op jit(solution)/shard_map/ppermute | solution.py:872
  60.4 5.2 %collective-permute-done.10.refs_8_ = f32[30,8,128]{2,1,0:T(8,128)S(1)} collective-permute-done((f32[30,8,128]{2,1,0:T(8,128)S(1)}, f32[30,8,128]{2,1,0:T(8,128)S(1)}, u32[]{:S(2)}, u32[]{:S(2)}) %collective-permute-start.10) | collective-permute-done | bytes 122912 | tf_op jit(solution)/shard_map/ppermute | solution.py:872
  65.6 0.8 %shard_map.102 = (f32[20,10,8,128]{3,2,1,0:T(8,128)S(1)}, f32[20,10,8,128]{3,2,1,0:T(8,128)S(1)}, f32[4,5,8,128]{3,2,1,0:T(8,128)S(1)}) custom-call(f32[20,2,8,128]{3,2,1,0:T(8,128)S(1)} %get-tuple-element.117.refs_9_.refs_0_.refs_7_, f32[20,3,8,128]{3,2,1,0:T(8,128)S(1)} %get-tuple-element.118.refs_10_.refs_1_.refs_8_, ...), custom_call_target="tpu_custom_call" | custom-call | tf_op jit(solution)/shard_map/pallas_call | solution.py:859
  66.4 0.1 collective-permute-start.13
  66.5 2.0 %collective-permute-start.12 = (f32[4,5,8,128]{3,2,1,0:T(8,128)S(1)}, f32[4,5,8,128]{3,2,1,0:T(8,128)S(1)}, u32[]{:S(2)}, u32[]{:S(2)}) collective-permute-start(f32[4,5,8,128]{3,2,1,0:T(8,128)S(1)} %get-tuple-element.143.refs_19_), channel_id=1, source_target_pairs={{0,8},{4,12},{8,16},{12,20},{16,24},{20,28},{24,32},{28,36},{32,40... | collective-permute-start | bytes 245768 | tf_op jit(solution)/shard_map/ppermute | solution.py:872
  68.5 2.4 %collective-permute-done.13.refs_21_ = f32[4,5,8,128]{3,2,1,0:T(8,128)S(1)} collective-permute-done((f32[4,5,8,128]{3,2,1,0:T(8,128)S(1)}, f32[4,5,8,128]{3,2,1,0:T(8,128)S(1)}, u32[]{:S(2)}, u32[]{:S(2)}) %collective-permute-start.13) | collective-permute-done | bytes 81952 | tf_op jit(solution)/shard_map/ppermute | solution.py:872
  70.9 3.1 %collective-permute-done.12.refs_20_ = f32[4,5,8,128]{3,2,1,0:T(8,128)S(1)} collective-permute-done((f32[4,5,8,128]{3,2,1,0:T(8,128)S(1)}, f32[4,5,8,128]{3,2,1,0:T(8,128)S(1)}, u32[]{:S(2)}, u32[]{:S(2)}) %collective-permute-start.12) | collective-permute-done | bytes 81952 | tf_op jit(solution)/shard_map/ppermute | solution.py:872
  74.1 3.8 %shard_map.103 = (f32[5,64,256]{2,1,0:T(8,128)}, f32[64,256]{1,0:T(8,128)}) custom-call(f32[40,4,8,128]{3,2,1,0:T(8,128)S(1)} %get-tuple-element.108.refs_0_, f32[40,5,8,128]{3,2,1,0:T(8,128)S(1)} %get-tuple-element.109.refs_1_, f32[40,4,8,128]{3,2,1,0:T(8,128)S(1)} %get-tuple-element.110.refs_2_, f32[40,4,8,128]{3,2,1,0:T(8,128)S(1)} %get-tuple-element.111.refs_3_, ...), custom_call_target="tpu_custom_call" | custom-call | tf_op jit(solution)/shard_map/pallas_call | solution.py:859
  (11 shorter events, 0.0 us)
Async XLA Ops:
  0.6 22.3 %copy-start = (f32[16,5]{0,1:T(8,128)S(1)}, f32[16,5]{0,1:T(8,128)}, u32[]{:S(2)}) copy-start(f32[16,5]{0,1:T(8,128)} %param.14) | copy-start | bytes 964
  2.0 14.5 %collective-permute-start.5 = (f32[33,2,8,128]{3,2,1,0:T(8,128)S(1)}, f32[33,2,8,128]{3,2,1,0:T(8,128)S(1)}, u32[]{:S(2)}, u32[]{:S(2)}) collective-permute-start(f32[33,2,8,128]{3,2,1,0:T(8,128)S(1)} %get-tuple-element.74.own), channel_id=1, source_target_pairs={{0,124},{4,0},{8,4},{12,8},{16,12},{20,16},{24,20},{28,24},{32,28}... | collective-permute-start | bytes 811016 | tf_op jit(solution)/shard_map/ppermute | solution.py:872
  6.8 11.4 %collective-permute-start.4 = (f32[33,2,8,128]{3,2,1,0:T(8,128)S(1)}, f32[33,2,8,128]{3,2,1,0:T(8,128)S(1)}, u32[]{:S(2)}, u32[]{:S(2)}) collective-permute-start(f32[33,2,8,128]{3,2,1,0:T(8,128)S(1)} %get-tuple-element.74.own), channel_id=1, source_target_pairs={{0,4},{4,8},{8,12},{12,16},{16,20},{20,24},{24,28},{28,32},{32,36}... | collective-permute-start | bytes 811016 | tf_op jit(solution)/shard_map/ppermute | solution.py:872
  6.8 7.2 %collective-permute-start = (f32[264,64]{1,0:T(8,128)S(1)}, f32[264,64]{1,0:T(8,128)S(1)}, u32[]{:S(2)}, u32[]{:S(2)}) collective-permute-start(f32[264,64]{1,0:T(8,128)S(1)} %get-tuple-element.75), channel_id=1, source_target_pairs={{0,1},{1,2},{2,3},{3,0},{4,5},{5,6},{6,7},{7,4},{8,9},{9,10},{10,1... | collective-permute-start | bytes 202760 | tf_op jit(solution)/shard_map/ppermute | solution.py:872
  8.7 5.3 %collective-permute-start.1 = (f32[264,64]{1,0:T(8,128)S(1)}, f32[264,64]{1,0:T(8,128)S(1)}, u32[]{:S(2)}, u32[]{:S(2)}) collective-permute-start(f32[264,64]{1,0:T(8,128)S(1)} %get-tuple-element.76), channel_id=1, source_target_pairs={{0,3},{1,0},{2,1},{3,2},{4,7},{5,4},{6,5},{7,6},{8,11},{9,8},{10,9... | collective-permute-start | bytes 202760 | tf_op jit(solution)/shard_map/ppermute | solution.py:872
  14.4 17.5 %collective-permute-start.3 = (f32[33,3,8,128]{3,2,1,0:T(8,128)S(1)}, f32[33,3,8,128]{3,2,1,0:T(8,128)S(1)}, u32[]{:S(2)}, u32[]{:S(2)}) collective-permute-start(f32[33,3,8,128]{3,2,1,0:T(8,128)S(1)} %shard_map.96.whole), channel_id=1, source_target_pairs={{0,120},{4,124},{8,0},{12,4},{16,8},{20,12},{24,16},{28,20},{32,24... | collective-permute-start | bytes 1216520 | tf_op jit(solution)/shard_map/ppermute | solution.py:872
  15.1 16.7 %collective-permute-start.2 = (f32[33,3,8,128]{3,2,1,0:T(8,128)S(1)}, f32[33,3,8,128]{3,2,1,0:T(8,128)S(1)}, u32[]{:S(2)}, u32[]{:S(2)}) collective-permute-start(f32[33,3,8,128]{3,2,1,0:T(8,128)S(1)} %shard_map.96.whole), channel_id=1, source_target_pairs={{0,8},{4,12},{8,16},{12,20},{16,24},{20,28},{24,32},{28,36},{32,40... | collective-permute-start | bytes 1216520 | tf_op jit(solution)/shard_map/ppermute | solution.py:872
  18.7 8.1 %collective-permute-start.6 = (f32[33,8,128]{2,1,0:T(8,128)S(1)}, f32[33,8,128]{2,1,0:T(8,128)S(1)}, u32[]{:S(2)}, u32[]{:S(2)}) collective-permute-start(f32[33,8,128]{2,1,0:T(8,128)S(1)} %get-tuple-element.77), channel_id=1, source_target_pairs={{0,1},{1,2},{2,3},{3,0},{4,5},{5,6},{6,7},{7,4},{8,9},{9,10},{10,1... | collective-permute-start | bytes 405512 | tf_op jit(solution)/shard_map/ppermute | solution.py:872
  20.7 6.1 %collective-permute-start.7 = (f32[33,8,128]{2,1,0:T(8,128)S(1)}, f32[33,8,128]{2,1,0:T(8,128)S(1)}, u32[]{:S(2)}, u32[]{:S(2)}) collective-permute-start(f32[33,8,128]{2,1,0:T(8,128)S(1)} %get-tuple-element.78), channel_id=1, source_target_pairs={{0,3},{1,0},{2,1},{3,2},{4,7},{5,4},{6,5},{7,6},{8,11},{9,8},{10,9... | collective-permute-start | bytes 405512 | tf_op jit(solution)/shard_map/ppermute | solution.py:872
  38.2 8.0 %collective-permute-start.8 = (f32[29,8,128]{2,1,0:T(8,128)S(1)}, f32[29,8,128]{2,1,0:T(8,128)S(1)}, u32[]{:S(2)}, u32[]{:S(2)}) collective-permute-start(f32[29,8,128]{2,1,0:T(8,128)S(1)} %get-tuple-element.131), channel_id=1, source_target_pairs={{0,8},{4,12},{8,16},{12,20},{16,24},{20,28},{24,32},{28,36},{32,40... | collective-permute-start | bytes 356360 | tf_op jit(solution)/shard_map/ppermute | solution.py:872
  38.3 7.9 %collective-permute-start.9 = (f32[29,8,128]{2,1,0:T(8,128)S(1)}, f32[29,8,128]{2,1,0:T(8,128)S(1)}, u32[]{:S(2)}, u32[]{:S(2)}) collective-permute-start(f32[29,8,128]{2,1,0:T(8,128)S(1)} %get-tuple-element.132), channel_id=1, source_target_pairs={{0,120},{4,124},{8,0},{12,4},{16,8},{20,12},{24,16},{28,20},{32,24... | collective-permute-start | bytes 356360 | tf_op jit(solution)/shard_map/ppermute | solution.py:872
  46.2 27.9 %copy-start.1 = (f32[8,8,256]{2,1,0:T(8,128)S(1)}, f32[8,8,256]{2,1,0:T(8,128)}, u32[]{:S(2)}) copy-start(f32[8,8,256]{2,1,0:T(8,128)} %param.8) | copy-start | bytes 196612
  52.5 7.9 %collective-permute-start.11 = (f32[30,8,128]{2,1,0:T(8,128)S(1)}, f32[30,8,128]{2,1,0:T(8,128)S(1)}, u32[]{:S(2)}, u32[]{:S(2)}) collective-permute-start(f32[30,8,128]{2,1,0:T(8,128)S(1)} %get-tuple-element.135), channel_id=1, source_target_pairs={{0,124},{4,0},{8,4},{12,8},{16,12},{20,16},{24,20},{28,24},{32,28}... | collective-permute-start | bytes 368648 | tf_op jit(solution)/shard_map/ppermute | solution.py:872
  57.9 7.6 %collective-permute-start.10 = (f32[30,8,128]{2,1,0:T(8,128)S(1)}, f32[30,8,128]{2,1,0:T(8,128)S(1)}, u32[]{:S(2)}, u32[]{:S(2)}) collective-permute-start(f32[30,8,128]{2,1,0:T(8,128)S(1)} %get-tuple-element.135), channel_id=1, source_target_pairs={{0,4},{4,8},{8,12},{12,16},{16,20},{20,24},{24,28},{28,32},{32,36}... | collective-permute-start | bytes 368648 | tf_op jit(solution)/shard_map/ppermute | solution.py:872
  66.4 4.5 %collective-permute-start.13 = (f32[4,5,8,128]{3,2,1,0:T(8,128)S(1)}, f32[4,5,8,128]{3,2,1,0:T(8,128)S(1)}, u32[]{:S(2)}, u32[]{:S(2)}) collective-permute-start(f32[4,5,8,128]{3,2,1,0:T(8,128)S(1)} %get-tuple-element.143.refs_19_), channel_id=1, source_target_pairs={{0,120},{4,124},{8,0},{12,4},{16,8},{20,12},{24,16},{28,20},{32,24... | collective-permute-start | bytes 245768 | tf_op jit(solution)/shard_map/ppermute | solution.py:872
  66.5 7.6 %collective-permute-start.12 = (f32[4,5,8,128]{3,2,1,0:T(8,128)S(1)}, f32[4,5,8,128]{3,2,1,0:T(8,128)S(1)}, u32[]{:S(2)}, u32[]{:S(2)}) collective-permute-start(f32[4,5,8,128]{3,2,1,0:T(8,128)S(1)} %get-tuple-element.143.refs_19_), channel_id=1, source_target_pairs={{0,8},{4,12},{8,16},{12,20},{16,24},{20,28},{24,32},{28,36},{32,40... | collective-permute-start | bytes 245768 | tf_op jit(solution)/shard_map/ppermute | solution.py:872

commit v4 on v3

--- a/solution.py
+++ b/solution.py
@@ -264,6 +264,19 @@
         body(i)
 
 
+class Sides:
+    def __init__(self, place, distance, first, second):
+        block = jnp.full((LAYERS, LANES), place[0], jnp.int32)
+        self.odd = (block & distance) != 0
+        self.first, self.second = first, second
+
+    def lower(self, *at):
+        return jnp.where(self.odd, self.first[at], self.second[at])
+
+    def upper(self, *at):
+        return jnp.where(self.odd, self.second[at], self.first[at])
+
+
 class Level:
     def __init__(self, phases, gx, gy, via, below, cap, total, weights):
         self.phases = phases
@@ -520,10 +533,11 @@
             whole[n, h] = own[n, h]
 
 
-def edge_kernel(near_lower, near_upper, go_right, go_left):
+def edge_kernel(place, near0, near1, go_right, go_left):
     lane = lane_index()
     group = lane // 32
     late = lane % 32 >= 16
+    near = Sides(place, 1, near0, near1)
 
     def chosen(one, two, three, four):
         return jnp.where(
@@ -532,8 +546,8 @@
 
     def body(n):
         rights, lefts = [], []
-        for block in (near_lower, near_upper):
-            first, second = block[n, 0], block[n, 1]
+        for block in (near.lower, near.upper):
+            first, second = block(n, 0), block(n, 1)
             first_far, first_near = pltpu.roll(first, 64, 1), pltpu.roll(first, 32, 1)
             second_far = pltpu.roll(second, 96, 1)
             rights.append(chosen(first_near, second, second_far, first_far))
@@ -573,12 +587,12 @@
         def place_row(s, block=block, rim=rim, b=b):
             for a, ref in enumerate((volt, cap0, conduct, below0)):
                 n = 4 * s + a
-                phases = spread(block[n, 0], block[n, 1], rim(n))
+                phases = spread(block(n, 0), block(n, 1), rim(n))
                 for p in range(4):
                     ref[8 * b + s, p] = phases[p]
 
         rows_loop(0, 8, place_row, 4)
-        loads = spread(block[32, 0], block[32, 1], rim(32))
+        loads = spread(block(32, 0), block(32, 1), rim(32))
         for p in range(4):
             values = [jnp.zeros((8, LANES), jnp.float32) for _ in range(SECTIONS)]
             for t in range(LOADS):
@@ -632,7 +646,7 @@
         mixed_table,
         refs,
         None,
-        ((2, whole, lambda n: whole[n, 2]),),
+        ((2, lambda n, h: whole[n, h], lambda n: whole[n, 2]),),
         ((17, 24),),
         ((17, 23),),
         ((18, 22),),
@@ -640,9 +654,10 @@
     )
 
 
-def near_kernel(place, mixed_table, near_lower, near_upper, edge_left, edge_right, *refs):
+def near_kernel(place, mixed_table, near0, near1, edge_left, edge_right, *refs):
     refs = refs[STATE:]
     late = lane_index() % 32 >= 16
+    near = Sides(place, 1, near0, near1)
 
     def rim_lower(n):
         return jnp.where(late, edge_left[n], edge_right[n])
@@ -657,7 +672,7 @@
         mixed_table,
         refs[:STATE],
         refs[STATE],
-        ((1, near_lower, rim_lower), (3, near_upper, rim_upper)),
+        ((1, near.lower, rim_lower), (3, near.upper, rim_upper)),
         ((9, 17), (24, 32)),
         ((9, 17), (23, 31)),
         ((10, 18), (22, 30)),
@@ -665,18 +680,22 @@
     )
 
 
-def setup_kernel(place, mixed_table, far_lower, far_upper, *refs):
+def setup_kernel(place, mixed_table, far0, far1, *refs):
     refs = refs[STATE + 1 :]
     state, f1 = refs[:STATE], refs[STATE]
     gx1, gy1, via1, cap1, total1, weights1, x1 = refs[STATE + 1 : STATE + 8]
-    gx2, gy2, below2, cap2, f2, go_up, go_down, spare1 = refs[STATE + 8 :]
+    gx2, gy2, below2, cap2, f2, go0, go1, spare1 = refs[STATE + 8 :]
+    far = Sides(place, 2, far0, far1)
     below1 = state[9]
     prepare(
         place,
         mixed_table,
         state,
         f1,
-        ((0, far_lower, lambda n: far_lower[n, 2]), (4, far_upper, lambda n: far_upper[n, 2])),
+        (
+            (0, far.lower, lambda n: far.lower(n, 2)),
+            (4, far.upper, lambda n: far.upper(n, 2)),
+        ),
         ((1, 9), (32, 40)),
         ((1, 9), (31, 39)),
         ((2, 10), (30, 38)),
@@ -692,22 +711,25 @@
     middle.first_relax(spare1, f1, 2, 18)
     middle.relax(x1, spare1, f1, 3, 17)
     middle.restrict(f2, x1, f1, 2, 8)
-    for target, first, outer in ((go_up, 2, 2), (go_down, 4, 6)):
+    ups, downs = [], []
+    for target, first, outer in ((ups, 2, 2), (downs, 4, 6)):
         for j in range(4):
             for k in range(SECTIONS):
-                target[5 * j + k] = f2[first + j, k]
+                target.append(f2[first + j, k])
         for j in range(2):
-            target[20 + 3 * j] = gy2[outer + j, 0]
-            target[21 + 3 * j] = below2[outer + j, 0]
-            target[22 + 3 * j] = cap2[outer + j, 0]
+            target.extend((gy2[outer + j, 0], below2[outer + j, 0], cap2[outer + j, 0]))
         for j in range(3):
-            target[26 + j] = gx2[outer + j, 0]
-
-
-def middle_kernel(*refs):
+            target.append(gx2[outer + j, 0])
+    for n, (up, down) in enumerate(zip(ups, downs)):
+        go0[n] = jnp.where(far.odd, down, up)
+        go1[n] = jnp.where(far.odd, up, down)
+
+
+def middle_kernel(place, *refs):
     (gx0, gy0, via0, below0, cap0, total0, weights0, f0, x0) = refs[0:9]
     (gx1, gy1, via1, below1, cap1, total1, weights1, f1, x1) = refs[9:18]
-    (gx2, gy2, below2, cap2, f2, from_lower, from_upper) = refs[18:25]
+    (gx2, gy2, below2, cap2, f2, got0, got1) = refs[18:25]
+    got = Sides(place, 2, got0, got1)
     (x0_out, f1_out, go_side, gxw, gyw, viaw, beloww, weightsw) = refs[25:33]
     (capw, totalw, fw, xa, xb, ya, yb, za, f1_own) = refs[33:42]
     fine = Level(4, gx0, gy0, via0, below0, cap0, total0, weights0)
@@ -715,17 +737,17 @@
     coarse = Level(1, gxw, gyw, viaw, beloww, capw, totalw, weightsw)
     for j in range(4):
         for k in range(SECTIONS):
-            fw[j, k] = from_lower[5 * j + k]
-            fw[10 + j, k] = from_upper[5 * j + k]
+            fw[j, k] = got.lower(5 * j + k)
+            fw[10 + j, k] = got.upper(5 * j + k)
     for j in range(2):
-        for near, source in ((j, from_lower), (12 + j, from_upper)):
-            gyw[near, 0] = source[20 + 3 * j]
-            gyw[near, 1] = from_right(source[20 + 3 * j])
-            beloww[near, 0] = source[21 + 3 * j]
-            capw[near, 0] = source[22 + 3 * j]
+        for near, source in ((j, got.lower), (12 + j, got.upper)):
+            gyw[near, 0] = source(20 + 3 * j)
+            gyw[near, 1] = from_right(source(20 + 3 * j))
+            beloww[near, 0] = source(21 + 3 * j)
+            capw[near, 0] = source(22 + 3 * j)
     for j in range(3):
-        gxw[j, 0] = from_lower[26 + j]
-        gxw[12 + j, 0] = from_upper[26 + j]
+        gxw[j, 0] = got.lower(26 + j)
+        gxw[12 + j, 0] = got.upper(26 + j)
     for j in range(6):
         for k in range(SECTIONS):
             fw[4 + j, k] = f2[2 + j, k]
@@ -744,12 +766,12 @@
     middle.correct(ya, x1, xb, 3, 17, 2)
     middle.relax(yb, ya, f1, 4, 16)
     middle.relax(ya, yb, f1, 5, 15)
-    fine.correct(za, x0, ya, 10, 30)
-    fine.relax(x0_out, za, f0, 11, 29)
-    fine.relax(za, x0_out, f0, 12, 28)
-    fine.relax(x0_out, za, f0, 13, 27)
-    fine.relax(za, x0_out, f0, 14, 26)
-    fine.restrict(f1_own, za, f0, 8, 12, -8)
+    fine.correct(x0_out, x0, ya, 10, 30)
+    fine.relax(za, x0_out, f0, 11, 29)
+    fine.relax(x0_out, za, f0, 12, 28)
+    fine.relax(za, x0_out, f0, 13, 27)
+    fine.relax(x0_out, za, f0, 14, 26)
+    fine.restrict(f1_own, x0_out, f0, 8, 12, -8)
     for j in range(4):
         for n in range(10):
             f1_out[10 * j + n] = f1_own[j, n]
@@ -758,22 +780,17 @@
         for t in range(3):
             go_side[3 * j + t] = packs[t]
 
-    def keep(i):
-        for n in range(20):
-            x0_out[i, n] = za[i, n]
-
-    rows_loop(14, 26, keep)
-
-
-def lower_kernel(*refs):
+
+def lower_kernel(place, *refs):
     (gx1, gy1, via1, below1, cap1, total1, weights1) = refs[0:7]
-    own, from_lower, from_upper = refs[7:10]
+    own, got0, got1 = refs[7:10]
+    got = Sides(place, 1, got0, got1)
     f1, x1, f2_out = refs[10:13]
     (xa,) = refs[13:14]
     middle = Level(2, gx1, gy1, via1, below1, cap1, total1, weights1)
     for j in range(10):
-        for first, source in ((4, from_lower), (12, from_upper)):
-            values = unpacked([source[3 * j + t] for t in range(3)])
+        for first, source in ((4, got.lower), (12, got.upper)):
+            values = unpacked([source(3 * j + t) for t in range(3)])
             for t in range(4):
                 n = 4 * j + t
                 f1[first + n // 10, n % 10] = values[t]
@@ -784,10 +801,11 @@
     middle.restrict(f2_out, x1, f1, 3, 7, -3)
 
 
-def finish_kernel(*refs):
+def finish_kernel(place, *refs):
     (gx0, gy0, via0, below0, weights0, f0, x0) = refs[0:7]
     (gx1, gy1, via1, below1, weights1, f1, x1) = refs[7:14]
-    (gxw, gyw, viaw, beloww, weightsw, own, from_lower, from_upper, voltage) = refs[14:23]
+    (gxw, gyw, viaw, beloww, weightsw, own, got0, got1, voltage) = refs[14:23]
+    got = Sides(place, 2, got0, got1)
     sections, next_voltage = refs[23:25]
     fw, xa, xb, ya, yb, za, zb, mixed, turn = refs[25:34]
     fine = Level(4, gx0, gy0, via0, below0, None, None, weights0)
@@ -795,9 +813,13 @@
     coarse = Level(1, gxw, gyw, viaw, beloww, None, None, weightsw)
     for j in range(4):
         for k in range(SECTIONS):
-            fw[1 + j, k] = from_lower[j, k]
+            fw[1 + j, k] = got.lower(j, k)
             fw[5 + j, k] = own[j, k]
-            fw[9 + j, k] = from_upper[j, k]
+            fw[9 + j, k] = got.upper(j, k)
+    block = jnp.full((LAYERS, LANES), place[0], jnp.int32)
+    for k in range(SECTIONS):
+        fw[4, k] = jnp.where(block == 1, got.lower(1, k), fw[4, k])
+        fw[9, k] = jnp.where(block == 30, got.upper(2, k), fw[9, k])
     coarse.first_relax(xa, fw, 1, 13)
     coarse.relax(xb, xa, fw, 2, 12)
     coarse.relax(xa, xb, fw, 3, 11)
@@ -872,11 +894,26 @@
     return lax.ppermute(value, axis, [(i, (i + shift) % count) for i in range(count)])
 
 
-ROWS = ("section", "gx")
+def paired(value, distance):
+    rows = lax.axis_size("section") * lax.axis_size("gx")
+    columns = lax.axis_size("gy")
+    values = value if isinstance(value, tuple) else (value, value)
+    result = []
+    for which in range(2):
+        pairs = []
+        for row in range(rows):
+            up = (row // distance) % 2 == which
+            other = row + distance if up else row - distance
+            for column in range(columns):
+                target = (other, column)
+                if not 0 <= other < rows:
+                    target = (row, column ^ 1) if distance == 1 else (row ^ 1, column)
+                pairs.append((row * columns + column, target[0] * columns + target[1]))
+        result.append(lax.ppermute(values[which], ("section", "gx", "gy"), pairs))
+    return result
 
 
 def local(voltage, capacity, node_class, via_sites, ball_sites, load_type, load_table):
-    rows = lax.axis_size("section") * lax.axis_size("gx")
     columns = lax.axis_size("gy")
     volts = voltage.reshape(64, 256)
     own, left, right = call(
@@ -907,21 +944,21 @@
         ],
         outside=True,
     )
-    near_lower, near_upper = (turned(own, ROWS, rows, s) for s in (1, -1))
-    from_lower = turned(right, "gy", columns, 1)
-    from_upper = turned(left, "gy", columns, -1)
-    mixed_table = jnp.einsum(
-        "tk,jk->tj", load_table, jnp.asarray(INVERSE, jnp.float32), precision=lax.Precision.HIGHEST
-    )
     place = jnp.stack(
         [
             lax.axis_index("section") * lax.axis_size("gx") + lax.axis_index("gx"),
             lax.axis_index("gy"),
         ]
     ).astype(jnp.int32)
+    near = paired(own, 1)
+    from_lower = turned(right, "gy", columns, 1)
+    from_upper = turned(left, "gy", columns, -1)
+    mixed_table = jnp.einsum(
+        "tk,jk->tj", load_table, jnp.asarray(INVERSE, jnp.float32), precision=lax.Precision.HIGHEST
+    )
     (whole,) = call(rim_kernel, (own, from_lower, from_upper), [vregs(33, 3)])
-    far_lower, far_upper = (turned(whole, ROWS, rows, s) for s in (2, -2))
-    go_right, go_left = call(edge_kernel, (near_lower, near_upper), [vregs(33), vregs(33)])
+    far = paired(whole, 2)
+    go_right, go_left = call(edge_kernel, (place, *near), [vregs(33), vregs(33)], (), 1)
     edge_left = turned(go_right, "gy", columns, 1)
     edge_right = turned(go_left, "gy", columns, -1)
     state_shapes = [
@@ -943,7 +980,7 @@
     state = call(own_kernel, (place, mixed_table, whole), state_shapes, (), 2)
     state = call(
         near_kernel,
-        (place, mixed_table, near_lower, near_upper, edge_left, edge_right, *state),
+        (place, mixed_table, *near, edge_left, edge_right, *state),
         [*state_shapes, vregs(EXT1, 10)],
         (),
         2,
@@ -951,7 +988,7 @@
     )
     state = call(
         setup_kernel,
-        (place, mixed_table, far_lower, far_upper, *state),
+        (place, mixed_table, *far, *state),
         [
             *state_shapes,
             vregs(EXT1, 10),
@@ -978,12 +1015,10 @@
     gx1, gy1, via1, cap1, total1, weights1, x1 = state[STATE + 1 : STATE + 8]
     middle = (gx1, gy1, via1, below1, cap1, total1, weights1, f1, x1)
     coarse = state[STATE + 8 : STATE + 13]
-    go_up, go_down = state[STATE + 13 :]
-    lower = turned(go_up, ROWS, rows, 2)
-    upper = turned(go_down, ROWS, rows, -2)
+    got = paired(tuple(state[STATE + 13 :]), 2)
     x0, f1_own, go_side, gxw, gyw, viaw, beloww, weightsw = call(
         middle_kernel,
-        (*fine, *middle, *coarse, lower, upper),
+        (place, *fine, *middle, *coarse, *got),
         [
             vregs(EXT0, 20),
             vregs(40),
@@ -1005,20 +1040,21 @@
             scratch(EXT0, 20),
             scratch(4, 10),
         ],
-    )
-    lower = turned(go_side, ROWS, rows, 1)
-    upper = turned(go_side, ROWS, rows, -1)
+        1,
+    )
+    got = paired(go_side, 1)
     f1, x1, f2_own = call(
         lower_kernel,
-        (*middle[:7], f1_own, lower, upper),
+        (place, *middle[:7], f1_own, *got),
         [vregs(EXT1, 10), vregs(EXT1, 10), vregs(4, 5)],
         [scratch(EXT1, 10)],
-    )
-    lower = turned(f2_own, ROWS, rows, 2)
-    upper = turned(f2_own, ROWS, rows, -2)
+        1,
+    )
+    got = paired(f2_own, 2)
     sections, next_voltage = call(
         finish_kernel,
         (
+            place,
             *fine[:4],
             *fine[6:8],
             x0,
@@ -1032,8 +1068,7 @@
             beloww,
             weightsw,
             f2_own,
-            lower,
-            upper,
+            *got,
             volts,
         ),
         [
@@ -1051,6 +1086,7 @@
             scratch(4, 40),
             pltpu.VMEM((SECTIONS, 2, 64, LANES), jnp.float32),
         ],
+        1,
     )
     return sections.reshape((SECTIONS,) + voltage.shape), next_voltage.reshape(voltage.shape)
 

time: 78.1 us -> 73 us (0.935)
  the two profiles are of different devices: /device:TPU:0 before, /device:TPU:1 now
where the time goes in v4:
time: 73 us; the launch traced here: 71.8 us
  starting transfers between devices  28.6 us (39%)
  Pallas kernels  28.5 us (39%)
  waiting for transfers between devices  12.9 us (18%)
  matrix products  0.88 us (1%)
  between operations  0.73 us (1%)
    pallas_call x9, Pallas kernels, call(): pl.pallas_call(kernel, out_shape=outs, in_specs=[pl.BlockSpec(memory_spac...  28.5 us
    ppermute x10, starting transfers between devices, paired(): result.append(lax.ppermute(values[which], ('section', 'gx', 'gy'), pairs))  20.9 us
    ppermute x10, waiting for transfers between devices, paired(): result.append(lax.ppermute(values[which], ('section', 'gx', 'gy'), pairs))  9.34 us
    ppermute x4, starting transfers between devices, turned(): lax.ppermute(value, axis, [(i, (i + shift) % count) for i in range(count)])  7.67 us
    ppermute x4, waiting for transfers between devices, turned(): lax.ppermute(value, axis, [(i, (i + shift) % count) for i in range(count)])  3.6 us
  transfers between devices with their start and end apart: 14, of which 8 were waited for; matrix products, arithmetic and copies ran while one was open for 1% of the time, Pallas kernels for 12%

profile of v4, /device:TPU:1, one launch (start us, length us, event | category | flops | bytes accessed | tf_op | source)
XLA Modules:
  0.0 71.8 jit_solution(2518865615930999171)
XLA Ops:
  0.6 0.0 copy-start
  0.6 1.3 %shard_map.95 = (f32[33,2,8,128]{3,2,1,0:T(8,128)S(1)}, f32[264,64]{1,0:T(8,128)S(1)}, f32[264,64]{1,0:T(8,128)S(1)}) custom-call(f32[64,256]{1,0:T(8,128)} %bitcast.12, f32[64,256]{1,0:T(8,128)} %bitcast.14, s32[64,256]{1,0:T(8,128)} %bitcast.15, s32[56,256]{1,0:T(8,128)} %bitcast.16, s32[8,256]{1,0:T(8,128)} %refs_4_.1, s32[8,256]{1,0:T(8,128)} %refs_5_.1), custom_call_target="tpu_custom_call" | custom-call | tf_op jit(solution)/shard_map/pallas_call | solution.py:881
  2.0 5.1 %collective-permute-start.5 = (f32[33,2,8,128]{3,2,1,0:T(8,128)S(1)}, f32[33,2,8,128]{3,2,1,0:T(8,128)S(1)}, u32[]{:S(2)}, u32[]{:S(2)}) collective-permute-start(f32[33,2,8,128]{3,2,1,0:T(8,128)S(1)} %get-tuple-element.74.own), channel_id=1, source_target_pairs={{0,1},{1,0},{2,3},{3,2},{4,8},{5,9},{6,10},{7,11},{8,4},{9,5},{10,... | collective-permute-start | bytes 811016 | tf_op jit(solution)/shard_map/ppermute | solution.py:912
  7.1 0.0 collective-permute-start.4
  7.1 1.6 %collective-permute-start = (f32[264,64]{1,0:T(8,128)S(1)}, f32[264,64]{1,0:T(8,128)S(1)}, u32[]{:S(2)}, u32[]{:S(2)}) collective-permute-start(f32[264,64]{1,0:T(8,128)S(1)} %get-tuple-element.75), channel_id=1, source_target_pairs={{0,1},{1,2},{2,3},{3,0},{4,5},{5,6},{6,7},{7,4},{8,9},{9,10},{10,1... | collective-permute-start | bytes 202760 | tf_op jit(solution)/shard_map/ppermute | solution.py:894
  8.7 2.1 %collective-permute-start.1 = (f32[264,64]{1,0:T(8,128)S(1)}, f32[264,64]{1,0:T(8,128)S(1)}, u32[]{:S(2)}, u32[]{:S(2)}) collective-permute-start(f32[264,64]{1,0:T(8,128)S(1)} %get-tuple-element.76), channel_id=1, source_target_pairs={{0,3},{1,0},{2,1},{3,2},{4,7},{5,4},{6,5},{7,6},{8,11},{9,8},{10,9... | collective-permute-start | bytes 202760 | tf_op jit(solution)/shard_map/ppermute | solution.py:894
  10.9 3.5 %collective-permute-done.from_lower = f32[264,64]{1,0:T(8,128)S(1)} collective-permute-done((f32[264,64]{1,0:T(8,128)S(1)}, f32[264,64]{1,0:T(8,128)S(1)}, u32[]{:S(2)}, u32[]{:S(2)}) %collective-permute-start) | collective-permute-done | bytes 67616 | tf_op jit(solution)/shard_map/ppermute | solution.py:894
  14.4 0.1 collective-permute-done.1.from_upper
  14.5 0.4 shard_map.96.whole
  14.8 1.8 %collective-permute-start.3 = (f32[33,3,8,128]{3,2,1,0:T(8,128)S(1)}, f32[33,3,8,128]{3,2,1,0:T(8,128)S(1)}, u32[]{:S(2)}, u32[]{:S(2)}) collective-permute-start(f32[33,3,8,128]{3,2,1,0:T(8,128)S(1)} %shard_map.96.whole), channel_id=1, source_target_pairs={{0,4},{1,5},{2,6},{3,7},{4,0},{5,1},{6,2},{7,3},{8,16},{9,17},{10,... | collective-permute-start | bytes 1216520 | tf_op jit(solution)/shard_map/ppermute | solution.py:912
  16.7 0.1 pad_add_fusion.place
  16.8 0.3 collective-permute-done.4.near0
  17.0 1.1 %shard_map.97 = (f32[33,8,128]{2,1,0:T(8,128)S(1)}, f32[33,8,128]{2,1,0:T(8,128)S(1)}) custom-call(s32[2]{0:T(128)S(1)} %pad_add_fusion.place, f32[33,2,8,128]{3,2,1,0:T(8,128)S(1)} %collective-permute-done.4.near0, f32[33,2,8,128]{3,2,1,0:T(8,128)S(1)} %collective-permute-done.5.near1), custom_call_target="tpu_custom_call" | custom-call | tf_op jit(solution)/shard_map/pallas_call | solution.py:881
  18.1 1.7 %collective-permute-start.6 = (f32[33,8,128]{2,1,0:T(8,128)S(1)}, f32[33,8,128]{2,1,0:T(8,128)S(1)}, u32[]{:S(2)}, u32[]{:S(2)}) collective-permute-start(f32[33,8,128]{2,1,0:T(8,128)S(1)} %get-tuple-element.77), channel_id=1, source_target_pairs={{0,1},{1,2},{2,3},{3,0},{4,5},{5,6},{6,7},{7,4},{8,9},{9,10},{10,1... | collective-permute-start | bytes 405512 | tf_op jit(solution)/shard_map/ppermute | solution.py:894
  19.8 2.2 %collective-permute-start.7 = (f32[33,8,128]{2,1,0:T(8,128)S(1)}, f32[33,8,128]{2,1,0:T(8,128)S(1)}, u32[]{:S(2)}, u32[]{:S(2)}) collective-permute-start(f32[33,8,128]{2,1,0:T(8,128)S(1)} %get-tuple-element.78), channel_id=1, source_target_pairs={{0,3},{1,0},{2,1},{3,2},{4,7},{5,4},{6,5},{7,6},{8,11},{9,8},{10,9... | collective-permute-start | bytes 405512 | tf_op jit(solution)/shard_map/ppermute | solution.py:894
  22.0 0.9 %convolution_bitcast_fusion.mixed_table = f32[16,5]{1,0:T(8,128)S(1)} fusion(f32[5,5]{1,0:T(8,128)} %constant.17.clone, f32[16,5]{0,1:T(8,128)S(1)} %copy-done), kind=kOutput, calls=%fused_computation | convolution fusion | flops 4800 | bytes 740 | tf_op jit(solution)/shard_map/tk,jk->tj/dot_general | solution.py:956
  22.9 1.8 %shard_map.98 = (f32[40,4,8,128]{3,2,1,0:T(8,128)S(1)}, f32[40,5,8,128]{3,2,1,0:T(8,128)S(1)}, f32[40,4,8,128]{3,2,1,0:T(8,128)S(1)}, f32[40,4,8,128]{3,2,1,0:T(...) custom-call(s32[2]{0:T(128)S(1)} %pad_add_fusion.place, ...), custom_call_target="tpu_custom_call" | custom-call | tf_op jit(solution)/shard_map/pallas_call | solution.py:881
  24.8 5.1 %shard_map.99 = (f32[40,4,8,128]{3,2,1,0:T(8,128)S(1)}, f32[40,5,8,128]{3,2,1,0:T(8,128)S(1)}, f32[40,4,8,128]{3,2,1,0:T(8,128)S(1)}, f32[40,4,8,128]{3,2,1,0:T(...) custom-call(s32[2]{0:T(128)S(1)} %pad_add_fusion.place, ...), custom_call_target="tpu_custom_call", output_to_operand_aliasing={{0}: (6, {}), {1}: (7, {}), {2}: (8, {}), {3}: (9, {}), {4}... | custom-call | tf_op jit(solution)/shard_map/pallas_call | solution.py:881
  29.9 6.4 %shard_map.100 = (f32[40,4,8,128]{3,2,1,0:T(8,128)S(1)}, f32[40,5,8,128]{3,2,1,0:T(8,128)S(1)}, f32[40,4,8,128]{3,2,1,0:T(8,128)S(1)}, f32[40,4,8,128]{3,2,1,0:T...) custom-call(s32[2]{0:T(128)S(1)} %pad_add_fusion.place, ...), custom_call_target="tpu_custom_call", output_to_operand_aliasing={{0}: (4, {}), {1}: (5, {}), {2}: (6, {}), {3}: (7, {}), {4}... | custom-call | tf_op jit(solution)/shard_map/pallas_call | solution.py:881
  36.2 1.4 %collective-permute-start.8 = (f32[29,8,128]{2,1,0:T(8,128)S(1)}, f32[29,8,128]{2,1,0:T(8,128)S(1)}, u32[]{:S(2)}, u32[]{:S(2)}) collective-permute-start(f32[29,8,128]{2,1,0:T(8,128)S(1)} %get-tuple-element.131), channel_id=1, source_target_pairs={{0,8},{1,9},{2,10},{3,11},{4,12},{5,13},{6,14},{7,15},{8,0},{9,1},... | collective-permute-start | bytes 356360 | tf_op jit(solution)/shard_map/ppermute | solution.py:912
  37.6 4.6 %collective-permute-start.9 = (f32[29,8,128]{2,1,0:T(8,128)S(1)}, f32[29,8,128]{2,1,0:T(8,128)S(1)}, u32[]{:S(2)}, u32[]{:S(2)}) collective-permute-start(f32[29,8,128]{2,1,0:T(8,128)S(1)} %get-tuple-element.132), channel_id=1, source_target_pairs={{0,4},{1,5},{2,6},{3,7},{4,0},{5,1},{6,2},{7,3},{8,16},{9,17},{10,... | collective-permute-start | bytes 356360 | tf_op jit(solution)/shard_map/ppermute | solution.py:912
  42.2 2.5 %collective-permute-done.9.refs_24_ = f32[29,8,128]{2,1,0:T(8,128)S(1)} collective-permute-done((f32[29,8,128]{2,1,0:T(8,128)S(1)}, f32[29,8,128]{2,1,0:T(8,128)S(1)}, u32[]{:S(2)}, u32[]{:S(2)}) %collective-permute-start.9) | collective-permute-done | bytes 118816 | tf_op jit(solution)/shard_map/ppermute | solution.py:912
  44.7 6.7 %shard_map.101 = (f32[40,20,8,128]{3,2,1,0:T(8,128)S(1)}, f32[40,8,128]{2,1,0:T(8,128)S(1)}, f32[30,8,128]{2,1,0:T(8,128)S(1)}, f32[15,1,8,128]{3,2,1,0:T(8,128)...) custom-call(s32[2]{0:T(128)S(1)} %pad_add_fusion.place, ...), custom_call_target="tpu_custom_call" | custom-call | tf_op jit(solution)/shard_map/pallas_call | solution.py:881
  51.4 3.4 %collective-permute-start.11 = (f32[30,8,128]{2,1,0:T(8,128)S(1)}, f32[30,8,128]{2,1,0:T(8,128)S(1)}, u32[]{:S(2)}, u32[]{:S(2)}) collective-permute-start(f32[30,8,128]{2,1,0:T(8,128)S(1)} %get-tuple-element.135), channel_id=1, source_target_pairs={{0,1},{1,0},{2,3},{3,2},{4,8},{5,9},{6,10},{7,11},{8,4},{9,5},{10,... | collective-permute-start | bytes 368648 | tf_op jit(solution)/shard_map/ppermute | solution.py:912
  54.8 3.1 %collective-permute-done.11.refs_9_ = f32[30,8,128]{2,1,0:T(8,128)S(1)} collective-permute-done((f32[30,8,128]{2,1,0:T(8,128)S(1)}, f32[30,8,128]{2,1,0:T(8,128)S(1)}, u32[]{:S(2)}, u32[]{:S(2)}) %collective-permute-start.11) | collective-permute-done | bytes 122912 | tf_op jit(solution)/shard_map/ppermute | solution.py:912
  57.9 0.9 %collective-permute-done.10.refs_8_ = f32[30,8,128]{2,1,0:T(8,128)S(1)} collective-permute-done((f32[30,8,128]{2,1,0:T(8,128)S(1)}, f32[30,8,128]{2,1,0:T(8,128)S(1)}, u32[]{:S(2)}, u32[]{:S(2)}) %collective-permute-start.10) | collective-permute-done | bytes 122912 | tf_op jit(solution)/shard_map/ppermute | solution.py:912
  58.8 1.4 %shard_map.102 = (f32[20,10,8,128]{3,2,1,0:T(8,128)S(1)}, f32[20,10,8,128]{3,2,1,0:T(8,128)S(1)}, f32[4,5,8,128]{3,2,1,0:T(8,128)S(1)}) custom-call(s32[2]{0:T(128)S(1)} %pad_add_fusion.place, f32[20,2,8,128]{3,2,1,0:T(8,128)S(1)} %get-tuple-element.117.refs_9_.refs_0_.refs_7_, f32[20,3,8,128]{3,2,1,0:T(8,128)S(1)} %get-tuple-element.118.refs_10_.refs_1_.refs_8_, ...), custom_call_target="tpu_custom_call" | custom-call | tf_op jit(solution)/shard_map/pallas_call | solution.py:881
  60.2 2.1 %collective-permute-start.13 = (f32[4,5,8,128]{3,2,1,0:T(8,128)S(1)}, f32[4,5,8,128]{3,2,1,0:T(8,128)S(1)}, u32[]{:S(2)}, u32[]{:S(2)}) collective-permute-start(f32[4,5,8,128]{3,2,1,0:T(8,128)S(1)} %get-tuple-element.143.refs_19_), channel_id=1, source_target_pairs={{0,4},{1,5},{2,6},{3,7},{4,0},{5,1},{6,2},{7,3},{8,16},{9,17},{10,... | collective-permute-start | bytes 245768 | tf_op jit(solution)/shard_map/ppermute | solution.py:912
  62.3 2.4 %collective-permute-start.12 = (f32[4,5,8,128]{3,2,1,0:T(8,128)S(1)}, f32[4,5,8,128]{3,2,1,0:T(8,128)S(1)}, u32[]{:S(2)}, u32[]{:S(2)}) collective-permute-start(f32[4,5,8,128]{3,2,1,0:T(8,128)S(1)} %get-tuple-element.143.refs_19_), channel_id=1, source_target_pairs={{0,8},{1,9},{2,10},{3,11},{4,12},{5,13},{6,14},{7,15},{8,0},{9,1},... | collective-permute-start | bytes 245768 | tf_op jit(solution)/shard_map/ppermute | solution.py:912
  64.8 0.6 collective-permute-done.13.refs_21_
  65.3 2.0 %collective-permute-done.12.refs_20_ = f32[4,5,8,128]{3,2,1,0:T(8,128)S(1)} collective-permute-done((f32[4,5,8,128]{3,2,1,0:T(8,128)S(1)}, f32[4,5,8,128]{3,2,1,0:T(8,128)S(1)}, u32[]{:S(2)}, u32[]{:S(2)}) %collective-permute-start.12) | collective-permute-done | bytes 81952 | tf_op jit(solution)/shard_map/ppermute | solution.py:912
  67.4 4.4 %shard_map.103 = (f32[5,64,256]{2,1,0:T(8,128)}, f32[64,256]{1,0:T(8,128)}) custom-call(s32[2]{0:T(128)S(1)} %pad_add_fusion.place, f32[40,4,8,128]{3,2,1,0:T(8,128)S(1)} %get-tuple-element.108.refs_0_, f32[40,5,8,128]{3,2,1,0:T(8,128)S(1)} %get-tuple-element.109.refs_1_, f32[40,4,8,128]{3,2,1,0:T(8,128)S(1)} %get-tuple-element.110.refs_2_, ...), custom_call_target="tpu_custom_call" | custom-call | tf_op jit(solution)/shard_map/pallas_call | solution.py:881
  (11 shorter events, 0.0 us)
Async XLA Ops:
  0.6 21.4 %copy-start = (f32[16,5]{0,1:T(8,128)S(1)}, f32[16,5]{0,1:T(8,128)}, u32[]{:S(2)}) copy-start(f32[16,5]{0,1:T(8,128)} %param.14) | copy-start | bytes 964
  2.0 14.8 %collective-permute-start.5 = (f32[33,2,8,128]{3,2,1,0:T(8,128)S(1)}, f32[33,2,8,128]{3,2,1,0:T(8,128)S(1)}, u32[]{:S(2)}, u32[]{:S(2)}) collective-permute-start(f32[33,2,8,128]{3,2,1,0:T(8,128)S(1)} %get-tuple-element.74.own), channel_id=1, source_target_pairs={{0,1},{1,0},{2,3},{3,2},{4,8},{5,9},{6,10},{7,11},{8,4},{9,5},{10,... | collective-permute-start | bytes 811016 | tf_op jit(solution)/shard_map/ppermute | solution.py:912
  7.1 9.9 %collective-permute-start.4 = (f32[33,2,8,128]{3,2,1,0:T(8,128)S(1)}, f32[33,2,8,128]{3,2,1,0:T(8,128)S(1)}, u32[]{:S(2)}, u32[]{:S(2)}) collective-permute-start(f32[33,2,8,128]{3,2,1,0:T(8,128)S(1)} %get-tuple-element.74.own), channel_id=1, source_target_pairs={{0,4},{1,5},{2,6},{3,7},{4,0},{5,1},{6,2},{7,3},{8,12},{9,13},{10,... | collective-permute-start | bytes 811016 | tf_op jit(solution)/shard_map/ppermute | solution.py:912
  7.1 7.3 %collective-permute-start = (f32[264,64]{1,0:T(8,128)S(1)}, f32[264,64]{1,0:T(8,128)S(1)}, u32[]{:S(2)}, u32[]{:S(2)}) collective-permute-start(f32[264,64]{1,0:T(8,128)S(1)} %get-tuple-element.75), channel_id=1, source_target_pairs={{0,1},{1,2},{2,3},{3,0},{4,5},{5,6},{6,7},{7,4},{8,9},{9,10},{10,1... | collective-permute-start | bytes 202760 | tf_op jit(solution)/shard_map/ppermute | solution.py:894
  8.7 5.7 %collective-permute-start.1 = (f32[264,64]{1,0:T(8,128)S(1)}, f32[264,64]{1,0:T(8,128)S(1)}, u32[]{:S(2)}, u32[]{:S(2)}) collective-permute-start(f32[264,64]{1,0:T(8,128)S(1)} %get-tuple-element.76), channel_id=1, source_target_pairs={{0,3},{1,0},{2,1},{3,2},{4,7},{5,4},{6,5},{7,6},{8,11},{9,8},{10,9... | collective-permute-start | bytes 202760 | tf_op jit(solution)/shard_map/ppermute | solution.py:894
  14.8 15.0 %collective-permute-start.3 = (f32[33,3,8,128]{3,2,1,0:T(8,128)S(1)}, f32[33,3,8,128]{3,2,1,0:T(8,128)S(1)}, u32[]{:S(2)}, u32[]{:S(2)}) collective-permute-start(f32[33,3,8,128]{3,2,1,0:T(8,128)S(1)} %shard_map.96.whole), channel_id=1, source_target_pairs={{0,4},{1,5},{2,6},{3,7},{4,0},{5,1},{6,2},{7,3},{8,16},{9,17},{10,... | collective-permute-start | bytes 1216520 | tf_op jit(solution)/shard_map/ppermute | solution.py:912
  16.7 13.2 %collective-permute-start.2 = (f32[33,3,8,128]{3,2,1,0:T(8,128)S(1)}, f32[33,3,8,128]{3,2,1,0:T(8,128)S(1)}, u32[]{:S(2)}, u32[]{:S(2)}) collective-permute-start(f32[33,3,8,128]{3,2,1,0:T(8,128)S(1)} %shard_map.96.whole), channel_id=1, source_target_pairs={{0,8},{1,9},{2,10},{3,11},{4,12},{5,13},{6,14},{7,15},{8,0},{9,1},... | collective-permute-start | bytes 1216520 | tf_op jit(solution)/shard_map/ppermute | solution.py:912
  18.1 6.6 %collective-permute-start.6 = (f32[33,8,128]{2,1,0:T(8,128)S(1)}, f32[33,8,128]{2,1,0:T(8,128)S(1)}, u32[]{:S(2)}, u32[]{:S(2)}) collective-permute-start(f32[33,8,128]{2,1,0:T(8,128)S(1)} %get-tuple-element.77), channel_id=1, source_target_pairs={{0,1},{1,2},{2,3},{3,0},{4,5},{5,6},{6,7},{7,4},{8,9},{9,10},{10,1... | collective-permute-start | bytes 405512 | tf_op jit(solution)/shard_map/ppermute | solution.py:894
  19.8 4.9 %collective-permute-start.7 = (f32[33,8,128]{2,1,0:T(8,128)S(1)}, f32[33,8,128]{2,1,0:T(8,128)S(1)}, u32[]{:S(2)}, u32[]{:S(2)}) collective-permute-start(f32[33,8,128]{2,1,0:T(8,128)S(1)} %get-tuple-element.78), channel_id=1, source_target_pairs={{0,3},{1,0},{2,1},{3,2},{4,7},{5,4},{6,5},{7,6},{8,11},{9,8},{10,9... | collective-permute-start | bytes 405512 | tf_op jit(solution)/shard_map/ppermute | solution.py:894
  36.2 6.0 %collective-permute-start.8 = (f32[29,8,128]{2,1,0:T(8,128)S(1)}, f32[29,8,128]{2,1,0:T(8,128)S(1)}, u32[]{:S(2)}, u32[]{:S(2)}) collective-permute-start(f32[29,8,128]{2,1,0:T(8,128)S(1)} %get-tuple-element.131), channel_id=1, source_target_pairs={{0,8},{1,9},{2,10},{3,11},{4,12},{5,13},{6,14},{7,15},{8,0},{9,1},... | collective-permute-start | bytes 356360 | tf_op jit(solution)/shard_map/ppermute | solution.py:912
  37.6 7.1 %collective-permute-start.9 = (f32[29,8,128]{2,1,0:T(8,128)S(1)}, f32[29,8,128]{2,1,0:T(8,128)S(1)}, u32[]{:S(2)}, u32[]{:S(2)}) collective-permute-start(f32[29,8,128]{2,1,0:T(8,128)S(1)} %get-tuple-element.132), channel_id=1, source_target_pairs={{0,4},{1,5},{2,6},{3,7},{4,0},{5,1},{6,2},{7,3},{8,16},{9,17},{10,... | collective-permute-start | bytes 356360 | tf_op jit(solution)/shard_map/ppermute | solution.py:912
  44.7 22.7 %copy-start.1 = (f32[8,8,256]{2,1,0:T(8,128)S(1)}, f32[8,8,256]{2,1,0:T(8,128)}, u32[]{:S(2)}) copy-start(f32[8,8,256]{2,1,0:T(8,128)} %param.8) | copy-start | bytes 196612
  51.4 6.5 %collective-permute-start.11 = (f32[30,8,128]{2,1,0:T(8,128)S(1)}, f32[30,8,128]{2,1,0:T(8,128)S(1)}, u32[]{:S(2)}, u32[]{:S(2)}) collective-permute-start(f32[30,8,128]{2,1,0:T(8,128)S(1)} %get-tuple-element.135), channel_id=1, source_target_pairs={{0,1},{1,0},{2,3},{3,2},{4,8},{5,9},{6,10},{7,11},{8,4},{9,5},{10,... | collective-permute-start | bytes 368648 | tf_op jit(solution)/shard_map/ppermute | solution.py:912
  54.8 4.0 %collective-permute-start.10 = (f32[30,8,128]{2,1,0:T(8,128)S(1)}, f32[30,8,128]{2,1,0:T(8,128)S(1)}, u32[]{:S(2)}, u32[]{:S(2)}) collective-permute-start(f32[30,8,128]{2,1,0:T(8,128)S(1)} %get-tuple-element.135), channel_id=1, source_target_pairs={{0,4},{1,5},{2,6},{3,7},{4,0},{5,1},{6,2},{7,3},{8,12},{9,13},{10,... | collective-permute-start | bytes 368648 | tf_op jit(solution)/shard_map/ppermute | solution.py:912
  60.2 5.2 %collective-permute-start.13 = (f32[4,5,8,128]{3,2,1,0:T(8,128)S(1)}, f32[4,5,8,128]{3,2,1,0:T(8,128)S(1)}, u32[]{:S(2)}, u32[]{:S(2)}) collective-permute-start(f32[4,5,8,128]{3,2,1,0:T(8,128)S(1)} %get-tuple-element.143.refs_19_), channel_id=1, source_target_pairs={{0,4},{1,5},{2,6},{3,7},{4,0},{5,1},{6,2},{7,3},{8,16},{9,17},{10,... | collective-permute-start | bytes 245768 | tf_op jit(solution)/shard_map/ppermute | solution.py:912
  62.3 5.0 %collective-permute-start.12 = (f32[4,5,8,128]{3,2,1,0:T(8,128)S(1)}, f32[4,5,8,128]{3,2,1,0:T(8,128)S(1)}, u32[]{:S(2)}, u32[]{:S(2)}) collective-permute-start(f32[4,5,8,128]{3,2,1,0:T(8,128)S(1)} %get-tuple-element.143.refs_19_), channel_id=1, source_target_pairs={{0,8},{1,9},{2,10},{3,11},{4,12},{5,13},{6,14},{7,15},{8,0},{9,1},... | collective-permute-start | bytes 245768 | tf_op jit(solution)/shard_map/ppermute | solution.py:912

commit v5 on v4

--- a/solution.py
+++ b/solution.py
@@ -13,6 +13,7 @@
 EXT1 = 20
 EXT2 = 10
 WIDE2 = 14
+TILES = 160
 
 node_table = (0.35, 0.55, 0.8, 1.1, 1.5, 2.0, 2.7, 3.6)
 via_conductance = 2.5
@@ -266,8 +267,7 @@
 
 class Sides:
     def __init__(self, place, distance, first, second):
-        block = jnp.full((LAYERS, LANES), place[0], jnp.int32)
-        self.odd = (block & distance) != 0
+        self.odd = (place[0] & distance) != 0
         self.first, self.second = first, second
 
     def lower(self, *at):
@@ -598,19 +598,21 @@
             for t in range(LOADS):
                 chosen = loads[p] == float(t)
                 values = [
-                    jnp.where(chosen, mixed_table[t, k], values[k]) for k in range(SECTIONS)
+                    jnp.where(chosen, mixed_table[SECTIONS * t + k], values[k]) for k in range(SECTIONS)
                 ]
             for k in range(SECTIONS):
-                surface[4 * k + p, 8 * b : 8 * b + 8] = values[k]
+                at = 8 * b * TILES + (4 * k + p) * LAYERS + LAYERS - 1
+                surface[pl.ds(at, 8, stride=TILES), :] = values[k]
         rows_loop(8 * b, 8 * b + 8, set_gy, 8)
         rows_loop(8 * b, 8 * b + 8, turn_gy, 8)
         sum_below(below0, below1, 2, 4 * b, 4 * b + 4)
 
     def set_gx(i):
         row = 8 * row_block - 16 + i
-        inside = jnp.where((row == 0) | (row == 256), 0.0, 1.0).astype(jnp.float32)
+        twice = jnp.where((row == 0) | (row == 256), 0.0, 2.0)
         for p in range(4):
-            gx0[i, p] = inside * series(conduct[i - 1, p], conduct[i, p])
+            near, far = conduct[i - 1, p], conduct[i, p]
+            gx0[i, p] = twice * near * far / (near + far)
 
     def set_source(i):
         centre = [volt[i, p] for p in range(4)]
@@ -620,17 +622,21 @@
             )
             values = []
             for k in range(SECTIONS):
-                drawn = jnp.broadcast_to(surface[4 * k + p, pl.ds(i, 1), :], (LAYERS, LANES))
+                at = pl.multiple_of(i * TILES + (4 * k + p) * LAYERS, LAYERS)
+                drawn = surface[pl.ds(at, LAYERS), :]
                 values.append(jnp.where(top, drawn, 0.0) - ROW_SUMS[k] * leak)
                 f0[i, 4 * k + p] = values[k]
             for k, value in enumerate(fine.weighted(i, p, values)):
                 spare[i, 4 * k + p] = value
 
+    def set_row(i):
+        fine.set_total(i)
+        set_source(i)
+
     for low, high in gx_rows:
         rows_loop(low, high, set_gx, 4)
     for low, high in total_rows:
-        rows_loop(low, high, fine.set_total)
-        rows_loop(low, high, set_source)
+        rows_loop(low, high, set_row)
     for low, high in relax_rows:
         fine.relax(x0, spare, f0, low, high)
     for low, high in sum_rows:
@@ -696,9 +702,9 @@
             (0, far.lower, lambda n: far.lower(n, 2)),
             (4, far.upper, lambda n: far.upper(n, 2)),
         ),
-        ((1, 9), (32, 40)),
-        ((1, 9), (31, 39)),
-        ((2, 10), (30, 38)),
+        ((2, 9), (32, 39)),
+        ((2, 9), (31, 38)),
+        ((3, 10), (30, 37)),
         ((2, 6), (14, 18)),
     )
     fine = Level(4, *state[:7])
@@ -707,7 +713,7 @@
     coarsen(fine, middle, EXT1)
     coarsen(middle, coarse, EXT2)
     sum_below(below1, below2, 1, 0, EXT2)
-    rows_loop(1, EXT1 - 1, middle.set_total)
+    rows_loop(2, EXT1 - 2, middle.set_total, 4)
     middle.first_relax(spare1, f1, 2, 18)
     middle.relax(x1, spare1, f1, 3, 17)
     middle.restrict(f2, x1, f1, 2, 8)
@@ -816,7 +822,7 @@
             fw[1 + j, k] = got.lower(j, k)
             fw[5 + j, k] = own[j, k]
             fw[9 + j, k] = got.upper(j, k)
-    block = jnp.full((LAYERS, LANES), place[0], jnp.int32)
+    block = place[0]
     for k in range(SECTIONS):
         fw[4, k] = jnp.where(block == 1, got.lower(1, k), fw[4, k])
         fw[9, k] = jnp.where(block == 30, got.upper(2, k), fw[9, k])
@@ -861,7 +867,6 @@
 
 
 VMEM = pltpu.MemorySpace.VMEM
-SMEM = pltpu.MemorySpace.SMEM
 
 
 def vregs(*shape):
@@ -872,17 +877,13 @@
     return pltpu.VMEM(shape + (LAYERS, LANES), jnp.float32)
 
 
-def call(kernel, inputs, outs, scratches=(), scalars=0, outside=False, aliases=()):
+def call(kernel, inputs, outs, scratches=(), outside=False, aliases=()):
     space = pltpu.MemorySpace.HBM if outside else VMEM
-    inputs = [
-        value if n < scalars else pltpu.with_memory_space_constraint(value, space)
-        for n, value in enumerate(inputs)
-    ]
+    inputs = [pltpu.with_memory_space_constraint(value, space) for value in inputs]
     return pl.pallas_call(
         kernel,
         out_shape=outs,
-        in_specs=[pl.BlockSpec(memory_space=SMEM)] * scalars
-        + [pl.BlockSpec(memory_space=space)] * (len(inputs) - scalars),
+        in_specs=[pl.BlockSpec(memory_space=space)] * len(inputs),
         out_specs=[pl.BlockSpec(memory_space=VMEM)] * len(outs),
         scratch_shapes=list(scratches),
         input_output_aliases=dict(aliases),
@@ -898,8 +899,8 @@
     rows = lax.axis_size("section") * lax.axis_size("gx")
     columns = lax.axis_size("gy")
     values = value if isinstance(value, tuple) else (value, value)
-    result = []
-    for which in range(2):
+    result = [None, None]
+    for which in (1, 0):
         pairs = []
         for row in range(rows):
             up = (row // distance) % 2 == which
@@ -909,7 +910,7 @@
                 if not 0 <= other < rows:
                     target = (row, column ^ 1) if distance == 1 else (row ^ 1, column)
                 pairs.append((row * columns + column, target[0] * columns + target[1]))
-        result.append(lax.ppermute(values[which], ("section", "gx", "gy"), pairs))
+        result[which] = lax.ppermute(values[which], ("section", "gx", "gy"), pairs)
     return result
 
 
@@ -944,21 +945,25 @@
         ],
         outside=True,
     )
+    mixed_table = jnp.einsum(
+        "tk,jk->tj", load_table, jnp.asarray(INVERSE, jnp.float32), precision=lax.Precision.HIGHEST
+    )
+    row_block = lax.axis_index("section") * lax.axis_size("gx") + lax.axis_index("gx")
     place = jnp.stack(
         [
-            lax.axis_index("section") * lax.axis_size("gx") + lax.axis_index("gx"),
-            lax.axis_index("gy"),
+            jnp.full((LAYERS, LANES), number, jnp.int32)
+            for number in (row_block, lax.axis_index("gy"))
         ]
-    ).astype(jnp.int32)
+    )
+    mixed_table = jnp.broadcast_to(
+        mixed_table.reshape(LOADS * SECTIONS, 1, 1), (LOADS * SECTIONS, LAYERS, LANES)
+    )
     near = paired(own, 1)
     from_lower = turned(right, "gy", columns, 1)
     from_upper = turned(left, "gy", columns, -1)
-    mixed_table = jnp.einsum(
-        "tk,jk->tj", load_table, jnp.asarray(INVERSE, jnp.float32), precision=lax.Precision.HIGHEST
-    )
     (whole,) = call(rim_kernel, (own, from_lower, from_upper), [vregs(33, 3)])
     far = paired(whole, 2)
-    go_right, go_left = call(edge_kernel, (place, *near), [vregs(33), vregs(33)], (), 1)
+    go_right, go_left = call(edge_kernel, (place, *near), [vregs(33), vregs(33)])
     edge_left = turned(go_right, "gy", columns, 1)
     edge_right = turned(go_left, "gy", columns, -1)
     state_shapes = [
@@ -974,16 +979,14 @@
         vregs(EXT1, 2),
         vregs(EXT0, 4),
         vregs(EXT0, 4),
-        pltpu.VMEM((20, EXT0, LANES), jnp.float32),
+        pltpu.VMEM((EXT0 * TILES, LANES), jnp.float32),
         vregs(EXT0, 20),
     ]
-    state = call(own_kernel, (place, mixed_table, whole), state_shapes, (), 2)
+    state = call(own_kernel, (place, mixed_table, whole), state_shapes)
     state = call(
         near_kernel,
         (place, mixed_table, *near, edge_left, edge_right, *state),
         [*state_shapes, vregs(EXT1, 10)],
-        (),
-        2,
         aliases=[(6 + n, n) for n in range(STATE)],
     )
     state = call(
@@ -1008,7 +1011,6 @@
             vregs(29),
         ],
         [scratch(EXT1, 10)],
-        2,
         aliases=[(4 + n, n) for n in range(STATE + 1)],
     )
     fine, below1, f1 = state[:9], state[9], state[STATE]
@@ -1040,7 +1042,6 @@
             scratch(EXT0, 20),
             scratch(4, 10),
         ],
-        1,
     )
     got = paired(go_side, 1)
     f1, x1, f2_own = call(
@@ -1048,7 +1049,6 @@
         (place, *middle[:7], f1_own, *got),
         [vregs(EXT1, 10), vregs(EXT1, 10), vregs(4, 5)],
         [scratch(EXT1, 10)],
-        1,
     )
     got = paired(f2_own, 2)
     sections, next_voltage = call(
@@ -1086,7 +1086,6 @@
             scratch(4, 40),
             pltpu.VMEM((SECTIONS, 2, 64, LANES), jnp.float32),
         ],
-        1,
     )
     return sections.reshape((SECTIONS,) + voltage.shape), next_voltage.reshape(voltage.shape)
 

time: 73 us -> 68.4 us (0.937)
  Pallas kernels: 28.5 us -> 23.1 us
    pallas_call x9, Pallas kernels: 28.5 us -> 23.1 us  [call(): pl.pallas_call(kernel, out_shape=outs, in_specs=[pl.BlockSpec(memory_spac...]
  transfers between devices with their start and end apart: 14 -> 14, of which waited for: 8 -> 9; matrix products, arithmetic and copies ran while one was open for 1% -> 2% of each run, Pallas kernels for 12% -> 9%
where the time goes in v5:
time: 68.4 us; the launch traced here: 67.1 us
  starting transfers between devices  28.9 us (42%)
  Pallas kernels  23.1 us (34%)
  waiting for transfers between devices  13.1 us (19%)
  matrix products  0.81 us (1%)
  between operations  0.73 us (1%)
    pallas_call x9, Pallas kernels, call(): pl.pallas_call(kernel, out_shape=outs, in_specs=[pl.BlockSpec(memory_spac...  23.1 us
    ppermute x10, starting transfers between devices, paired(): result[which] = lax.ppermute(values[which], ('section', 'gx', 'gy'), pairs)  21.3 us
    ppermute x10, waiting for transfers between devices, paired(): result[which] = lax.ppermute(values[which], ('section', 'gx', 'gy'), pairs)  9.4 us
    ppermute x4, starting transfers between devices, turned(): lax.ppermute(value, axis, [(i, (i + shift) % count) for i in range(count)])  7.67 us
    ppermute x4, waiting for transfers between devices, turned(): lax.ppermute(value, axis, [(i, (i + shift) % count) for i in range(count)])  3.69 us
  transfers between devices with their start and end apart: 14, of which 9 were waited for; matrix products, arithmetic and copies ran while one was open for 2% of the time, Pallas kernels for 9%

profile of v5, /device:TPU:1, one launch (start us, length us, event | category | flops | bytes accessed | tf_op | source)
XLA Modules:
  0.0 67.1 jit_solution(4198427567654425117)
XLA Ops:
  0.6 1.3 %shard_map.95 = (f32[33,2,8,128]{3,2,1,0:T(8,128)S(1)}, f32[264,64]{1,0:T(8,128)S(1)}, f32[264,64]{1,0:T(8,128)S(1)}) custom-call(f32[64,256]{1,0:T(8,128)} %bitcast.11, f32[64,256]{1,0:T(8,128)} %bitcast.13, s32[64,256]{1,0:T(8,128)} %bitcast.14, s32[56,256]{1,0:T(8,128)} %bitcast.15, s32[8,256]{1,0:T(8,128)} %refs_4_.1, s32[8,256]{1,0:T(8,128)} %refs_5_.1), custom_call_target="tpu_custom_call" | custom-call | tf_op jit(solution)/shard_map/pallas_call | solution.py:883
  2.0 5.1 %collective-permute-start.5 = (f32[33,2,8,128]{3,2,1,0:T(8,128)S(1)}, f32[33,2,8,128]{3,2,1,0:T(8,128)S(1)}, u32[]{:S(2)}, u32[]{:S(2)}) collective-permute-start(f32[33,2,8,128]{3,2,1,0:T(8,128)S(1)} %get-tuple-element.74.own), channel_id=1, source_target_pairs={{0,1},{1,0},{2,3},{3,2},{4,8},{5,9},{6,10},{7,11},{8,4},{9,5},{10,... | collective-permute-start | bytes 811016 | tf_op jit(solution)/shard_map/ppermute | solution.py:913
  7.1 1.6 %collective-permute-start = (f32[264,64]{1,0:T(8,128)S(1)}, f32[264,64]{1,0:T(8,128)S(1)}, u32[]{:S(2)}, u32[]{:S(2)}) collective-permute-start(f32[264,64]{1,0:T(8,128)S(1)} %get-tuple-element.75), channel_id=1, source_target_pairs={{0,1},{1,2},{2,3},{3,0},{4,5},{5,6},{6,7},{7,4},{8,9},{9,10},{10,1... | collective-permute-start | bytes 202760 | tf_op jit(solution)/shard_map/ppermute | solution.py:895
  8.7 2.1 %collective-permute-start.1 = (f32[264,64]{1,0:T(8,128)S(1)}, f32[264,64]{1,0:T(8,128)S(1)}, u32[]{:S(2)}, u32[]{:S(2)}) collective-permute-start(f32[264,64]{1,0:T(8,128)S(1)} %get-tuple-element.76), channel_id=1, source_target_pairs={{0,3},{1,0},{2,1},{3,2},{4,7},{5,4},{6,5},{7,6},{8,11},{9,8},{10,9... | collective-permute-start | bytes 202760 | tf_op jit(solution)/shard_map/ppermute | solution.py:895
  10.9 3.5 %collective-permute-done.from_lower = f32[264,64]{1,0:T(8,128)S(1)} collective-permute-done((f32[264,64]{1,0:T(8,128)S(1)}, f32[264,64]{1,0:T(8,128)S(1)}, u32[]{:S(2)}, u32[]{:S(2)}) %collective-permute-start) | collective-permute-done | bytes 67616 | tf_op jit(solution)/shard_map/ppermute | solution.py:895
  14.5 0.4 shard_map.96.whole
  14.8 1.8 %collective-permute-start.3 = (f32[33,3,8,128]{3,2,1,0:T(8,128)S(1)}, f32[33,3,8,128]{3,2,1,0:T(8,128)S(1)}, u32[]{:S(2)}, u32[]{:S(2)}) collective-permute-start(f32[33,3,8,128]{3,2,1,0:T(8,128)S(1)} %shard_map.96.whole), channel_id=1, source_target_pairs={{0,4},{1,5},{2,6},{3,7},{4,0},{5,1},{6,2},{7,3},{8,16},{9,17},{10,... | collective-permute-start | bytes 1216520 | tf_op jit(solution)/shard_map/ppermute | solution.py:913
  16.7 0.3 collective-permute-done.4.near0
  17.1 0.5 shard_map.97
  17.7 1.7 %collective-permute-start.6 = (f32[33,8,128]{2,1,0:T(8,128)S(1)}, f32[33,8,128]{2,1,0:T(8,128)S(1)}, u32[]{:S(2)}, u32[]{:S(2)}) collective-permute-start(f32[33,8,128]{2,1,0:T(8,128)S(1)} %get-tuple-element.77), channel_id=1, source_target_pairs={{0,1},{1,2},{2,3},{3,0},{4,5},{5,6},{6,7},{7,4},{8,9},{9,10},{10,1... | collective-permute-start | bytes 405512 | tf_op jit(solution)/shard_map/ppermute | solution.py:895
  19.4 2.2 %collective-permute-start.7 = (f32[33,8,128]{2,1,0:T(8,128)S(1)}, f32[33,8,128]{2,1,0:T(8,128)S(1)}, u32[]{:S(2)}, u32[]{:S(2)}) collective-permute-start(f32[33,8,128]{2,1,0:T(8,128)S(1)} %get-tuple-element.78), channel_id=1, source_target_pairs={{0,3},{1,0},{2,1},{3,2},{4,7},{5,4},{6,5},{7,6},{8,11},{9,8},{10,9... | collective-permute-start | bytes 405512 | tf_op jit(solution)/shard_map/ppermute | solution.py:895
  21.6 0.8 %convolution_bitcast_fusion = f32[16,5]{0,1:T(8,128)S(1)} fusion(f32[5,5]{1,0:T(8,128)} %constant.17.clone, f32[16,5]{0,1:T(8,128)S(1)} %copy-done), kind=kOutput, calls=%fused_computation | convolution fusion | flops 4800 | bytes 740 | tf_op jit(solution)/shard_map/tk,jk->tj/dot_general | solution.py:948
  22.4 0.1 copy.40
  22.5 0.1 broadcast_in_dim.7
  22.6 0.1 broadcast_in_dim.8.mixed_table
  22.7 1.1 %shard_map.98 = (f32[40,4,8,128]{3,2,1,0:T(8,128)S(1)}, f32[40,5,8,128]{3,2,1,0:T(8,128)S(1)}, f32[40,4,8,128]{3,2,1,0:T(8,128)S(1)}, f32[40,4,8,128]{3,2,1,0:T(...) custom-call(s32[2,8,128]{2,1,0:T(8,128)S(1)} %stack.6.place, ...), custom_call_target="tpu_custom_call" | custom-call | tf_op jit(solution)/shard_map/pallas_call | solution.py:883
  23.8 0.1 collective-permute-done.6.edge_left
  23.9 4.0 %shard_map.99 = (f32[40,4,8,128]{3,2,1,0:T(8,128)S(1)}, f32[40,5,8,128]{3,2,1,0:T(8,128)S(1)}, f32[40,4,8,128]{3,2,1,0:T(8,128)S(1)}, f32[40,4,8,128]{3,2,1,0:T(...) custom-call(s32[2,8,128]{2,1,0:T(8,128)S(1)} %stack.6.place, ...), custom_call_target="tpu_custom_call", output_to_operand_aliasing={{0}: (6, {}), {1}: (7, {}), {2}: (8, {}), {3}: (9, {}), {4}... | custom-call | tf_op jit(solution)/shard_map/pallas_call | solution.py:883
  27.9 5.1 %shard_map.100 = (f32[40,4,8,128]{3,2,1,0:T(8,128)S(1)}, f32[40,5,8,128]{3,2,1,0:T(8,128)S(1)}, f32[40,4,8,128]{3,2,1,0:T(8,128)S(1)}, f32[40,4,8,128]{3,2,1,0:T...) custom-call(s32[2,8,128]{2,1,0:T(8,128)S(1)} %stack.6.place, ...), custom_call_target="tpu_custom_call", output_to_operand_aliasing={{0}: (4, {}), {1}: (5, {}), {2}: (6, {}), {3}: (7, {}), {4}... | custom-call | tf_op jit(solution)/shard_map/pallas_call | solution.py:883
  33.1 1.4 %collective-permute-start.8 = (f32[29,8,128]{2,1,0:T(8,128)S(1)}, f32[29,8,128]{2,1,0:T(8,128)S(1)}, u32[]{:S(2)}, u32[]{:S(2)}) collective-permute-start(f32[29,8,128]{2,1,0:T(8,128)S(1)} %get-tuple-element.131), channel_id=1, source_target_pairs={{0,8},{1,9},{2,10},{3,11},{4,12},{5,13},{6,14},{7,15},{8,0},{9,1},... | collective-permute-start | bytes 356360 | tf_op jit(solution)/shard_map/ppermute | solution.py:913
  34.5 5.0 %collective-permute-start.9 = (f32[29,8,128]{2,1,0:T(8,128)S(1)}, f32[29,8,128]{2,1,0:T(8,128)S(1)}, u32[]{:S(2)}, u32[]{:S(2)}) collective-permute-start(f32[29,8,128]{2,1,0:T(8,128)S(1)} %get-tuple-element.132), channel_id=1, source_target_pairs={{0,4},{1,5},{2,6},{3,7},{4,0},{5,1},{6,2},{7,3},{8,16},{9,17},{10,... | collective-permute-start | bytes 356360 | tf_op jit(solution)/shard_map/ppermute | solution.py:913
  39.4 2.5 %collective-permute-done.9.refs_24_ = f32[29,8,128]{2,1,0:T(8,128)S(1)} collective-permute-done((f32[29,8,128]{2,1,0:T(8,128)S(1)}, f32[29,8,128]{2,1,0:T(8,128)S(1)}, u32[]{:S(2)}, u32[]{:S(2)}) %collective-permute-start.9) | collective-permute-done | bytes 118816 | tf_op jit(solution)/shard_map/ppermute | solution.py:913
  41.9 6.0 %shard_map.101 = (f32[40,20,8,128]{3,2,1,0:T(8,128)S(1)}, f32[40,8,128]{2,1,0:T(8,128)S(1)}, f32[30,8,128]{2,1,0:T(8,128)S(1)}, f32[15,1,8,128]{3,2,1,0:T(8,128)...) custom-call(s32[2,8,128]{2,1,0:T(8,128)S(1)} %stack.6.place, ...), custom_call_target="tpu_custom_call" | custom-call | tf_op jit(solution)/shard_map/pallas_call | solution.py:883
  48.0 3.4 %collective-permute-start.11 = (f32[30,8,128]{2,1,0:T(8,128)S(1)}, f32[30,8,128]{2,1,0:T(8,128)S(1)}, u32[]{:S(2)}, u32[]{:S(2)}) collective-permute-start(f32[30,8,128]{2,1,0:T(8,128)S(1)} %get-tuple-element.135), channel_id=1, source_target_pairs={{0,1},{1,0},{2,3},{3,2},{4,8},{5,9},{6,10},{7,11},{8,4},{9,5},{10,... | collective-permute-start | bytes 368648 | tf_op jit(solution)/shard_map/ppermute | solution.py:913
  51.4 3.1 %collective-permute-done.11.refs_9_ = f32[30,8,128]{2,1,0:T(8,128)S(1)} collective-permute-done((f32[30,8,128]{2,1,0:T(8,128)S(1)}, f32[30,8,128]{2,1,0:T(8,128)S(1)}, u32[]{:S(2)}, u32[]{:S(2)}) %collective-permute-start.11) | collective-permute-done | bytes 122912 | tf_op jit(solution)/shard_map/ppermute | solution.py:913
  54.5 1.0 %collective-permute-done.10.refs_8_ = f32[30,8,128]{2,1,0:T(8,128)S(1)} collective-permute-done((f32[30,8,128]{2,1,0:T(8,128)S(1)}, f32[30,8,128]{2,1,0:T(8,128)S(1)}, u32[]{:S(2)}, u32[]{:S(2)}) %collective-permute-start.10) | collective-permute-done | bytes 122912 | tf_op jit(solution)/shard_map/ppermute | solution.py:913
  55.4 0.9 %shard_map.102 = (f32[20,10,8,128]{3,2,1,0:T(8,128)S(1)}, f32[20,10,8,128]{3,2,1,0:T(8,128)S(1)}, f32[4,5,8,128]{3,2,1,0:T(8,128)S(1)}) custom-call(s32[2,8,128]{2,1,0:T(8,128)S(1)} %stack.6.place, f32[20,2,8,128]{3,2,1,0:T(8,128)S(1)} %get-tuple-element.117.refs_9_.refs_0_.refs_7_, f32[20,3,8,128]{3,2,1,0:T(8,128)S(1)} %get-tuple-element.118.refs_10_.refs_1_.refs_8_, ...), custom_call_target="tpu_custom_call" | custom-call | tf_op jit(solution)/shard_map/pallas_call | solution.py:883
  56.3 2.2 %collective-permute-start.13 = (f32[4,5,8,128]{3,2,1,0:T(8,128)S(1)}, f32[4,5,8,128]{3,2,1,0:T(8,128)S(1)}, u32[]{:S(2)}, u32[]{:S(2)}) collective-permute-start(f32[4,5,8,128]{3,2,1,0:T(8,128)S(1)} %get-tuple-element.143.refs_19_), channel_id=1, source_target_pairs={{0,4},{1,5},{2,6},{3,7},{4,0},{5,1},{6,2},{7,3},{8,16},{9,17},{10,... | collective-permute-start | bytes 245768 | tf_op jit(solution)/shard_map/ppermute | solution.py:913
  58.5 2.3 %collective-permute-start.12 = (f32[4,5,8,128]{3,2,1,0:T(8,128)S(1)}, f32[4,5,8,128]{3,2,1,0:T(8,128)S(1)}, u32[]{:S(2)}, u32[]{:S(2)}) collective-permute-start(f32[4,5,8,128]{3,2,1,0:T(8,128)S(1)} %get-tuple-element.143.refs_19_), channel_id=1, source_target_pairs={{0,8},{1,9},{2,10},{3,11},{4,12},{5,13},{6,14},{7,15},{8,0},{9,1},... | collective-permute-start | bytes 245768 | tf_op jit(solution)/shard_map/ppermute | solution.py:913
  60.8 0.6 collective-permute-done.13.refs_21_
  61.5 1.9 %collective-permute-done.12.refs_20_ = f32[4,5,8,128]{3,2,1,0:T(8,128)S(1)} collective-permute-done((f32[4,5,8,128]{3,2,1,0:T(8,128)S(1)}, f32[4,5,8,128]{3,2,1,0:T(8,128)S(1)}, u32[]{:S(2)}, u32[]{:S(2)}) %collective-permute-start.12) | collective-permute-done | bytes 81952 | tf_op jit(solution)/shard_map/ppermute | solution.py:913
  63.4 3.7 %shard_map.103 = (f32[5,64,256]{2,1,0:T(8,128)}, f32[64,256]{1,0:T(8,128)}) custom-call(s32[2,8,128]{2,1,0:T(8,128)S(1)} %stack.6.place, f32[40,4,8,128]{3,2,1,0:T(8,128)S(1)} %get-tuple-element.108.refs_0_, f32[40,5,8,128]{3,2,1,0:T(8,128)S(1)} %get-tuple-element.109.refs_1_, f32[40,4,8,128]{3,2,1,0:T(8,128)S(1)} %get-tuple-element.110.refs_2_, ...), custom_call_target="tpu_custom_call" | custom-call | tf_op jit(solution)/shard_map/pallas_call | solution.py:883
  (15 shorter events, 0.2 us)
Async XLA Ops:
  0.6 20.9 %copy-start = (f32[16,5]{0,1:T(8,128)S(1)}, f32[16,5]{0,1:T(8,128)}, u32[]{:S(2)}) copy-start(f32[16,5]{0,1:T(8,128)} %param.14) | copy-start | bytes 964
  2.0 14.7 %collective-permute-start.5 = (f32[33,2,8,128]{3,2,1,0:T(8,128)S(1)}, f32[33,2,8,128]{3,2,1,0:T(8,128)S(1)}, u32[]{:S(2)}, u32[]{:S(2)}) collective-permute-start(f32[33,2,8,128]{3,2,1,0:T(8,128)S(1)} %get-tuple-element.74.own), channel_id=1, source_target_pairs={{0,1},{1,0},{2,3},{3,2},{4,8},{5,9},{6,10},{7,11},{8,4},{9,5},{10,... | collective-permute-start | bytes 811016 | tf_op jit(solution)/shard_map/ppermute | solution.py:913
  7.1 9.9 %collective-permute-start.4 = (f32[33,2,8,128]{3,2,1,0:T(8,128)S(1)}, f32[33,2,8,128]{3,2,1,0:T(8,128)S(1)}, u32[]{:S(2)}, u32[]{:S(2)}) collective-permute-start(f32[33,2,8,128]{3,2,1,0:T(8,128)S(1)} %get-tuple-element.74.own), channel_id=1, source_target_pairs={{0,4},{1,5},{2,6},{3,7},{4,0},{5,1},{6,2},{7,3},{8,12},{9,13},{10,... | collective-permute-start | bytes 811016 | tf_op jit(solution)/shard_map/ppermute | solution.py:913
  7.1 7.3 %collective-permute-start = (f32[264,64]{1,0:T(8,128)S(1)}, f32[264,64]{1,0:T(8,128)S(1)}, u32[]{:S(2)}, u32[]{:S(2)}) collective-permute-start(f32[264,64]{1,0:T(8,128)S(1)} %get-tuple-element.75), channel_id=1, source_target_pairs={{0,1},{1,2},{2,3},{3,0},{4,5},{5,6},{6,7},{7,4},{8,9},{9,10},{10,1... | collective-permute-start | bytes 202760 | tf_op jit(solution)/shard_map/ppermute | solution.py:895
  8.7 5.7 %collective-permute-start.1 = (f32[264,64]{1,0:T(8,128)S(1)}, f32[264,64]{1,0:T(8,128)S(1)}, u32[]{:S(2)}, u32[]{:S(2)}) collective-permute-start(f32[264,64]{1,0:T(8,128)S(1)} %get-tuple-element.76), channel_id=1, source_target_pairs={{0,3},{1,0},{2,1},{3,2},{4,7},{5,4},{6,5},{7,6},{8,11},{9,8},{10,9... | collective-permute-start | bytes 202760 | tf_op jit(solution)/shard_map/ppermute | solution.py:895
  14.8 13.1 %collective-permute-start.3 = (f32[33,3,8,128]{3,2,1,0:T(8,128)S(1)}, f32[33,3,8,128]{3,2,1,0:T(8,128)S(1)}, u32[]{:S(2)}, u32[]{:S(2)}) collective-permute-start(f32[33,3,8,128]{3,2,1,0:T(8,128)S(1)} %shard_map.96.whole), channel_id=1, source_target_pairs={{0,4},{1,5},{2,6},{3,7},{4,0},{5,1},{6,2},{7,3},{8,16},{9,17},{10,... | collective-permute-start | bytes 1216520 | tf_op jit(solution)/shard_map/ppermute | solution.py:913
  16.7 11.2 %collective-permute-start.2 = (f32[33,3,8,128]{3,2,1,0:T(8,128)S(1)}, f32[33,3,8,128]{3,2,1,0:T(8,128)S(1)}, u32[]{:S(2)}, u32[]{:S(2)}) collective-permute-start(f32[33,3,8,128]{3,2,1,0:T(8,128)S(1)} %shard_map.96.whole), channel_id=1, source_target_pairs={{0,8},{1,9},{2,10},{3,11},{4,12},{5,13},{6,14},{7,15},{8,0},{9,1},... | collective-permute-start | bytes 1216520 | tf_op jit(solution)/shard_map/ppermute | solution.py:913
  17.7 6.2 %collective-permute-start.6 = (f32[33,8,128]{2,1,0:T(8,128)S(1)}, f32[33,8,128]{2,1,0:T(8,128)S(1)}, u32[]{:S(2)}, u32[]{:S(2)}) collective-permute-start(f32[33,8,128]{2,1,0:T(8,128)S(1)} %get-tuple-element.77), channel_id=1, source_target_pairs={{0,1},{1,2},{2,3},{3,0},{4,5},{5,6},{6,7},{7,4},{8,9},{9,10},{10,1... | collective-permute-start | bytes 405512 | tf_op jit(solution)/shard_map/ppermute | solution.py:895
  19.4 4.5 %collective-permute-start.7 = (f32[33,8,128]{2,1,0:T(8,128)S(1)}, f32[33,8,128]{2,1,0:T(8,128)S(1)}, u32[]{:S(2)}, u32[]{:S(2)}) collective-permute-start(f32[33,8,128]{2,1,0:T(8,128)S(1)} %get-tuple-element.78), channel_id=1, source_target_pairs={{0,3},{1,0},{2,1},{3,2},{4,7},{5,4},{6,5},{7,6},{8,11},{9,8},{10,9... | collective-permute-start | bytes 405512 | tf_op jit(solution)/shard_map/ppermute | solution.py:895
  33.1 6.3 %collective-permute-start.8 = (f32[29,8,128]{2,1,0:T(8,128)S(1)}, f32[29,8,128]{2,1,0:T(8,128)S(1)}, u32[]{:S(2)}, u32[]{:S(2)}) collective-permute-start(f32[29,8,128]{2,1,0:T(8,128)S(1)} %get-tuple-element.131), channel_id=1, source_target_pairs={{0,8},{1,9},{2,10},{3,11},{4,12},{5,13},{6,14},{7,15},{8,0},{9,1},... | collective-permute-start | bytes 356360 | tf_op jit(solution)/shard_map/ppermute | solution.py:913
  34.5 7.5 %collective-permute-start.9 = (f32[29,8,128]{2,1,0:T(8,128)S(1)}, f32[29,8,128]{2,1,0:T(8,128)S(1)}, u32[]{:S(2)}, u32[]{:S(2)}) collective-permute-start(f32[29,8,128]{2,1,0:T(8,128)S(1)} %get-tuple-element.132), channel_id=1, source_target_pairs={{0,4},{1,5},{2,6},{3,7},{4,0},{5,1},{6,2},{7,3},{8,16},{9,17},{10,... | collective-permute-start | bytes 356360 | tf_op jit(solution)/shard_map/ppermute | solution.py:913
  41.9 21.4 %copy-start.1 = (f32[8,8,256]{2,1,0:T(8,128)S(1)}, f32[8,8,256]{2,1,0:T(8,128)}, u32[]{:S(2)}) copy-start(f32[8,8,256]{2,1,0:T(8,128)} %param.8) | copy-start | bytes 196612
  48.0 6.5 %collective-permute-start.11 = (f32[30,8,128]{2,1,0:T(8,128)S(1)}, f32[30,8,128]{2,1,0:T(8,128)S(1)}, u32[]{:S(2)}, u32[]{:S(2)}) collective-permute-start(f32[30,8,128]{2,1,0:T(8,128)S(1)} %get-tuple-element.135), channel_id=1, source_target_pairs={{0,1},{1,0},{2,3},{3,2},{4,8},{5,9},{6,10},{7,11},{8,4},{9,5},{10,... | collective-permute-start | bytes 368648 | tf_op jit(solution)/shard_map/ppermute | solution.py:913
  51.4 4.0 %collective-permute-start.10 = (f32[30,8,128]{2,1,0:T(8,128)S(1)}, f32[30,8,128]{2,1,0:T(8,128)S(1)}, u32[]{:S(2)}, u32[]{:S(2)}) collective-permute-start(f32[30,8,128]{2,1,0:T(8,128)S(1)} %get-tuple-element.135), channel_id=1, source_target_pairs={{0,4},{1,5},{2,6},{3,7},{4,0},{5,1},{6,2},{7,3},{8,12},{9,13},{10,... | collective-permute-start | bytes 368648 | tf_op jit(solution)/shard_map/ppermute | solution.py:913
  56.3 5.2 %collective-permute-start.13 = (f32[4,5,8,128]{3,2,1,0:T(8,128)S(1)}, f32[4,5,8,128]{3,2,1,0:T(8,128)S(1)}, u32[]{:S(2)}, u32[]{:S(2)}) collective-permute-start(f32[4,5,8,128]{3,2,1,0:T(8,128)S(1)} %get-tuple-element.143.refs_19_), channel_id=1, source_target_pairs={{0,4},{1,5},{2,6},{3,7},{4,0},{5,1},{6,2},{7,3},{8,16},{9,17},{10,... | collective-permute-start | bytes 245768 | tf_op jit(solution)/shard_map/ppermute | solution.py:913
  58.5 4.9 %collective-permute-start.12 = (f32[4,5,8,128]{3,2,1,0:T(8,128)S(1)}, f32[4,5,8,128]{3,2,1,0:T(8,128)S(1)}, u32[]{:S(2)}, u32[]{:S(2)}) collective-permute-start(f32[4,5,8,128]{3,2,1,0:T(8,128)S(1)} %get-tuple-element.143.refs_19_), channel_id=1, source_target_pairs={{0,8},{1,9},{2,10},{3,11},{4,12},{5,13},{6,14},{7,15},{8,0},{9,1},... | collective-permute-start | bytes 245768 | tf_op jit(solution)/shard_map/ppermute | solution.py:913

commit v6 on v5

--- a/solution.py
+++ b/solution.py
@@ -228,25 +228,39 @@
 
 def packed(values):
     lane = lane_index()
-    dead = (lane >= 80) & (lane < 112)
-    one, two, three, last = values
-    tail = jnp.where(lane < 96, pltpu.roll(last, 96, 1), pltpu.roll(last, 32, 1))
-    return [
-        jnp.where(dead, pltpu.roll(last, 80, 1), one),
-        jnp.where(dead, pltpu.roll(last, 48, 1), two),
-        jnp.where(dead, tail, three),
-    ]
+    result = []
+    for q in range(5):
+        carrier = values[q]
+        for e in range(3):
+            spare, at = values[5 + e], 72 + 16 * e
+            if q < 4:
+                part = pltpu.roll(spare, at - 16 * q, 1)
+            else:
+                part = jnp.where(
+                    lane < at + 8,
+                    pltpu.roll(spare, at - 64, 1),
+                    pltpu.roll(spare, (at + 8 - 120) % LANES, 1),
+                )
+            carrier = jnp.where((lane >= at) & (lane < at + 16), part, carrier)
+        result.append(carrier)
+    return result
 
 
 def unpacked(packs):
     lane = lane_index()
-    one, two, three = packs
-    last = jnp.where(
-        lane < 64,
-        jnp.where(lane < 32, pltpu.roll(one, 48, 1), pltpu.roll(two, 80, 1)),
-        jnp.where(lane < 96, pltpu.roll(three, 96, 1), pltpu.roll(three, 32, 1)),
-    )
-    return [one, two, three, last]
+    result = list(packs)
+    for e in range(3):
+        at = 72 + 16 * e
+        value = jnp.where(
+            lane < 96,
+            pltpu.roll(packs[4], (64 - at) % LANES, 1),
+            pltpu.roll(packs[4], (120 - at - 8) % LANES, 1),
+        )
+        for q in range(4):
+            part = pltpu.roll(packs[q], (16 * q - at) % LANES, 1)
+            value = jnp.where((lane >= 16 * q) & (lane < 16 * q + 16), part, value)
+        result.append(value)
+    return result
 
 
 def rows_loop(low, high, body, unroll=2):
@@ -690,7 +704,7 @@
     refs = refs[STATE + 1 :]
     state, f1 = refs[:STATE], refs[STATE]
     gx1, gy1, via1, cap1, total1, weights1, x1 = refs[STATE + 1 : STATE + 8]
-    gx2, gy2, below2, cap2, f2, go0, go1, spare1 = refs[STATE + 8 :]
+    gx2, gy2, below2, cap2, f2, go1, go0, spare1 = refs[STATE + 8 :]
     far = Sides(place, 2, far0, far1)
     below1 = state[9]
     prepare(
@@ -734,7 +748,7 @@
 def middle_kernel(place, *refs):
     (gx0, gy0, via0, below0, cap0, total0, weights0, f0, x0) = refs[0:9]
     (gx1, gy1, via1, below1, cap1, total1, weights1, f1, x1) = refs[9:18]
-    (gx2, gy2, below2, cap2, f2, got0, got1) = refs[18:25]
+    (gx2, gy2, below2, cap2, f2, got1, got0) = refs[18:25]
     got = Sides(place, 2, got0, got1)
     (x0_out, f1_out, go_side, gxw, gyw, viaw, beloww, weightsw) = refs[25:33]
     (capw, totalw, fw, xa, xb, ya, yb, za, f1_own) = refs[33:42]
@@ -764,7 +778,7 @@
         capw[2 + j, 0] = cap2[j, 0]
     for j in range(1, 10):
         gxw[2 + j, 0] = gx2[j, 0]
-    rows_loop(0, WIDE2, coarse.set_total)
+    rows_loop(0, WIDE2, coarse.set_total, 7)
     coarse.first_relax(xa, fw, 0, 14)
     coarse.relax(xb, xa, fw, 1, 13)
     coarse.relax(xa, xb, fw, 2, 12)
@@ -781,10 +795,10 @@
     for j in range(4):
         for n in range(10):
             f1_out[10 * j + n] = f1_own[j, n]
-    for j in range(10):
-        packs = packed([f1_own[n // 10, n % 10] for n in range(4 * j, 4 * j + 4)])
-        for t in range(3):
-            go_side[3 * j + t] = packs[t]
+    for j in range(5):
+        packs = packed([f1_own[n // 10, n % 10] for n in range(8 * j, 8 * j + 8)])
+        for t in range(5):
+            go_side[5 * j + t] = packs[t]
 
 
 def lower_kernel(place, *refs):
@@ -794,13 +808,13 @@
     f1, x1, f2_out = refs[10:13]
     (xa,) = refs[13:14]
     middle = Level(2, gx1, gy1, via1, below1, cap1, total1, weights1)
-    for j in range(10):
+    for j in range(5):
         for first, source in ((4, got.lower), (12, got.upper)):
-            values = unpacked([source(3 * j + t) for t in range(3)])
-            for t in range(4):
-                n = 4 * j + t
+            values = unpacked([source(5 * j + t) for t in range(5)])
+            for t in range(8):
+                n = 8 * j + t
                 f1[first + n // 10, n % 10] = values[t]
-        for n in range(4 * j, 4 * j + 4):
+        for n in range(8 * j, 8 * j + 8):
             f1[8 + n // 10, n % 10] = own[n]
     middle.first_relax(xa, f1, 4, 16)
     middle.relax(x1, xa, f1, 5, 15)
@@ -813,7 +827,7 @@
     (gxw, gyw, viaw, beloww, weightsw, own, got0, got1, voltage) = refs[14:23]
     got = Sides(place, 2, got0, got1)
     sections, next_voltage = refs[23:25]
-    fw, xa, xb, ya, yb, za, zb, mixed, turn = refs[25:34]
+    fw, xa, xb, ya, yb, za, zb, mixed, turn, after, done = refs[25:36]
     fine = Level(4, gx0, gy0, via0, below0, None, None, weights0)
     middle = Level(2, gx1, gy1, via1, below1, None, None, weights1)
     coarse = Level(1, gxw, gyw, viaw, beloww, None, None, weightsw)
@@ -837,33 +851,50 @@
     fine.relax(zb, za, f0, 15, 25)
     fine.relax(za, zb, f0, 16, 24)
 
+    half = lane_index() < 64
+
     def mix(row):
+        phases = []
         for p in range(4):
             values = [za[16 + row, 4 * k + p] for k in range(SECTIONS)]
+            sums = []
             for j in range(SECTIONS):
                 total = TRANSFORM[j][0] * values[0]
                 for k in range(1, SECTIONS):
                     total = total + TRANSFORM[j][k] * values[k]
-                mixed[p, 8 * j + row] = total
+                sums.append(total)
+            phases.append(sums)
+        for h in range(2):
+            for j in range(SECTIONS):
+                mixed[h, 8 * j + row] = jnp.where(
+                    half, phases[2 * h][j], pltpu.roll(phases[2 * h + 1][j], 64, 1)
+                )
 
     rows_loop(0, 8, mix)
-    result = None
-    for p in range(4):
-        lane = lax.broadcasted_iota(jnp.int32, (LANES, 256), 0)
-        column = lax.broadcasted_iota(jnp.int32, (LANES, 256), 1)
-        chooser = jnp.where((lane < 64) & (column == 4 * lane + p), 1.0, 0.0).astype(jnp.bfloat16)
-        part = selected(mixed[p].reshape(320, LANES), chooser)
-        result = part if result is None else result + part
-    for j in range(SECTIONS):
-        for row in range(8):
-            at = (8 * j + row) * 8
-            for h in range(2):
-                turn[j, h, pl.ds(row, 8, stride=8), :] = result[
-                    at : at + 8, h * 128 : h * 128 + 128
-                ]
+    slot = lax.broadcasted_iota(jnp.int32, (256, 256), 0)
+    column = lax.broadcasted_iota(jnp.int32, (256, 256), 1)
+    chooser = jnp.where(column == 4 * (slot % 64) + slot // 64, 1.0, 0.0).astype(jnp.bfloat16)
+    result = selected(
+        jnp.concatenate([mixed[h].reshape(320, LANES) for h in range(2)], axis=1), chooser
+    )
+    started = []
+
+    def send(source, target):
+        started.append(pltpu.make_async_copy(source, target, done.at[len(started)]))
+        started[-1].start()
+
+    for j in (4, 0, 1, 2, 3):
         for h in range(2):
-            sections[j, :, h * 128 : h * 128 + 128] = turn[j, h]
-    next_voltage[...] = voltage[...] + sections[SECTIONS - 1]
+            cut = slice(h * 128, h * 128 + 128)
+            for row in range(8):
+                at = (8 * j + row) * 8
+                turn[j, h, pl.ds(row, 8, stride=8), :] = result[at : at + 8, cut]
+            if j == 4:
+                after[h] = voltage[:, cut] + turn[j, h]
+                send(after.at[h], next_voltage.at[:, cut])
+            send(turn.at[j, h], sections.at[j, :, cut])
+    for copy in started:
+        copy.wait()
 
 
 VMEM = pltpu.MemorySpace.VMEM
@@ -877,14 +908,14 @@
     return pltpu.VMEM(shape + (LAYERS, LANES), jnp.float32)
 
 
-def call(kernel, inputs, outs, scratches=(), outside=False, aliases=()):
+def call(kernel, inputs, outs, scratches=(), outside=False, aliases=(), out_space=None):
     space = pltpu.MemorySpace.HBM if outside else VMEM
     inputs = [pltpu.with_memory_space_constraint(value, space) for value in inputs]
     return pl.pallas_call(
         kernel,
         out_shape=outs,
         in_specs=[pl.BlockSpec(memory_space=space)] * len(inputs),
-        out_specs=[pl.BlockSpec(memory_space=VMEM)] * len(outs),
+        out_specs=[pl.BlockSpec(memory_space=out_space or VMEM)] * len(outs),
         scratch_shapes=list(scratches),
         input_output_aliases=dict(aliases),
         compiler_params=pltpu.CompilerParams(vmem_limit_bytes=12 * 2**20),
@@ -1017,14 +1048,14 @@
     gx1, gy1, via1, cap1, total1, weights1, x1 = state[STATE + 1 : STATE + 8]
     middle = (gx1, gy1, via1, below1, cap1, total1, weights1, f1, x1)
     coarse = state[STATE + 8 : STATE + 13]
-    got = paired(tuple(state[STATE + 13 :]), 2)
+    got = paired(tuple(reversed(state[STATE + 13 :])), 2)
     x0, f1_own, go_side, gxw, gyw, viaw, beloww, weightsw = call(
         middle_kernel,
-        (place, *fine, *middle, *coarse, *got),
+        (place, *fine, *middle, *coarse, *reversed(got)),
         [
             vregs(EXT0, 20),
             vregs(40),
-            vregs(30),
+            vregs(25),
             vregs(WIDE2 + 1, 1),
             vregs(WIDE2, 2),
             vregs(WIDE2, 1),
@@ -1083,9 +1114,12 @@
             scratch(EXT1, 10),
             scratch(EXT0, 20),
             scratch(EXT0, 20),
-            scratch(4, 40),
+            scratch(2, 40),
             pltpu.VMEM((SECTIONS, 2, 64, LANES), jnp.float32),
+            pltpu.VMEM((2, 64, LANES), jnp.float32),
+            pltpu.SemaphoreType.DMA((12,)),
         ],
+        out_space=pltpu.MemorySpace.HBM,
     )
     return sections.reshape((SECTIONS,) + voltage.shape), next_voltage.reshape(voltage.shape)
 

time: 68.4 us -> 67.3 us (0.984)
  starting transfers between devices: 28.9 us -> 23.8 us
  waiting for transfers between devices: 13.1 us -> 17.8 us
    ppermute x10, starting transfers between devices: 21.3 us -> 16.1 us  [paired(): result[which] = lax.ppermute(values[which], ('section', 'gx', 'gy'), pairs)]
    ppermute x10, waiting for transfers between devices: 9.4 us -> 14.1 us  [paired(): result[which] = lax.ppermute(values[which], ('section', 'gx', 'gy'), pairs)]
  transfers between devices with their start and end apart: 14 -> 14, of which waited for: 9 -> 10; matrix products, arithmetic and copies ran while one was open for 2% -> 2% of each run, Pallas kernels for 9% -> 9%
where the time goes in v6:
time: 67.3 us; the launch traced here: 66.6 us
  starting transfers between devices  23.8 us (35%)
  Pallas kernels  23 us (34%)
  waiting for transfers between devices  17.8 us (26%)
  matrix products  0.81 us (1%)
  between operations  0.74 us (1%)
    pallas_call x9, Pallas kernels, call(): pl.pallas_call(kernel, out_shape=outs, in_specs=[pl.BlockSpec(memory_spac...  23 us
    ppermute x10, starting transfers between devices, paired(): result[which] = lax.ppermute(values[which], ('section', 'gx', 'gy'), pairs)  16.1 us
    ppermute x10, waiting for transfers between devices, paired(): result[which] = lax.ppermute(values[which], ('section', 'gx', 'gy'), pairs)  14.1 us
    ppermute x4, starting transfers between devices, turned(): lax.ppermute(value, axis, [(i, (i + shift) % count) for i in range(count)])  7.67 us
    ppermute x4, waiting for transfers between devices, turned(): lax.ppermute(value, axis, [(i, (i + shift) % count) for i in range(count)])  3.69 us
  transfers between devices with their start and end apart: 14, of which 10 were waited for; matrix products, arithmetic and copies ran while one was open for 2% of the time, Pallas kernels for 9%

profile of v6, /device:TPU:1, one launch (start us, length us, event | category | flops | bytes accessed | tf_op | source)
XLA Modules:
  0.0 66.6 jit_solution(11207717054236520765)
XLA Ops:
  0.6 1.3 %shard_map.95 = (f32[33,2,8,128]{3,2,1,0:T(8,128)S(1)}, f32[264,64]{1,0:T(8,128)S(1)}, f32[264,64]{1,0:T(8,128)S(1)}) custom-call(f32[64,256]{1,0:T(8,128)} %bitcast.11, f32[64,256]{1,0:T(8,128)} %bitcast.13, s32[64,256]{1,0:T(8,128)} %bitcast.14, s32[56,256]{1,0:T(8,128)} %bitcast.15, s32[8,256]{1,0:T(8,128)} %refs_4_.1, s32[8,256]{1,0:T(8,128)} %refs_5_.1), custom_call_target="tpu_custom_call" | custom-call | tf_op jit(solution)/shard_map/pallas_call | solution.py:914
  2.0 5.1 %collective-permute-start.5 = (f32[33,2,8,128]{3,2,1,0:T(8,128)S(1)}, f32[33,2,8,128]{3,2,1,0:T(8,128)S(1)}, u32[]{:S(2)}, u32[]{:S(2)}) collective-permute-start(f32[33,2,8,128]{3,2,1,0:T(8,128)S(1)} %get-tuple-element.74.own), channel_id=1, source_target_pairs={{0,1},{1,0},{2,3},{3,2},{4,8},{5,9},{6,10},{7,11},{8,4},{9,5},{10,... | collective-permute-start | bytes 811016 | tf_op jit(solution)/shard_map/ppermute | solution.py:944
  7.1 1.6 %collective-permute-start = (f32[264,64]{1,0:T(8,128)S(1)}, f32[264,64]{1,0:T(8,128)S(1)}, u32[]{:S(2)}, u32[]{:S(2)}) collective-permute-start(f32[264,64]{1,0:T(8,128)S(1)} %get-tuple-element.75), channel_id=1, source_target_pairs={{0,1},{1,2},{2,3},{3,0},{4,5},{5,6},{6,7},{7,4},{8,9},{9,10},{10,1... | collective-permute-start | bytes 202760 | tf_op jit(solution)/shard_map/ppermute | solution.py:926
  8.7 2.1 %collective-permute-start.1 = (f32[264,64]{1,0:T(8,128)S(1)}, f32[264,64]{1,0:T(8,128)S(1)}, u32[]{:S(2)}, u32[]{:S(2)}) collective-permute-start(f32[264,64]{1,0:T(8,128)S(1)} %get-tuple-element.76), channel_id=1, source_target_pairs={{0,3},{1,0},{2,1},{3,2},{4,7},{5,4},{6,5},{7,6},{8,11},{9,8},{10,9... | collective-permute-start | bytes 202760 | tf_op jit(solution)/shard_map/ppermute | solution.py:926
  10.9 3.5 %collective-permute-done.from_lower = f32[264,64]{1,0:T(8,128)S(1)} collective-permute-done((f32[264,64]{1,0:T(8,128)S(1)}, f32[264,64]{1,0:T(8,128)S(1)}, u32[]{:S(2)}, u32[]{:S(2)}) %collective-permute-start) | collective-permute-done | bytes 67616 | tf_op jit(solution)/shard_map/ppermute | solution.py:926
  14.4 0.1 collective-permute-done.1.from_upper
  14.5 0.4 shard_map.96.whole
  14.8 1.8 %collective-permute-start.3 = (f32[33,3,8,128]{3,2,1,0:T(8,128)S(1)}, f32[33,3,8,128]{3,2,1,0:T(8,128)S(1)}, u32[]{:S(2)}, u32[]{:S(2)}) collective-permute-start(f32[33,3,8,128]{3,2,1,0:T(8,128)S(1)} %shard_map.96.whole), channel_id=1, source_target_pairs={{0,4},{1,5},{2,6},{3,7},{4,0},{5,1},{6,2},{7,3},{8,16},{9,17},{10,... | collective-permute-start | bytes 1216520 | tf_op jit(solution)/shard_map/ppermute | solution.py:944
  16.7 0.3 collective-permute-done.4.near0
  17.1 0.5 shard_map.97
  17.7 1.7 %collective-permute-start.6 = (f32[33,8,128]{2,1,0:T(8,128)S(1)}, f32[33,8,128]{2,1,0:T(8,128)S(1)}, u32[]{:S(2)}, u32[]{:S(2)}) collective-permute-start(f32[33,8,128]{2,1,0:T(8,128)S(1)} %get-tuple-element.77), channel_id=1, source_target_pairs={{0,1},{1,2},{2,3},{3,0},{4,5},{5,6},{6,7},{7,4},{8,9},{9,10},{10,1... | collective-permute-start | bytes 405512 | tf_op jit(solution)/shard_map/ppermute | solution.py:926
  19.4 2.2 %collective-permute-start.7 = (f32[33,8,128]{2,1,0:T(8,128)S(1)}, f32[33,8,128]{2,1,0:T(8,128)S(1)}, u32[]{:S(2)}, u32[]{:S(2)}) collective-permute-start(f32[33,8,128]{2,1,0:T(8,128)S(1)} %get-tuple-element.78), channel_id=1, source_target_pairs={{0,3},{1,0},{2,1},{3,2},{4,7},{5,4},{6,5},{7,6},{8,11},{9,8},{10,9... | collective-permute-start | bytes 405512 | tf_op jit(solution)/shard_map/ppermute | solution.py:926
  21.6 0.8 %convolution_bitcast_fusion = f32[16,5]{0,1:T(8,128)S(1)} fusion(f32[5,5]{1,0:T(8,128)} %constant.17.clone, f32[16,5]{0,1:T(8,128)S(1)} %copy-done), kind=kOutput, calls=%fused_computation | convolution fusion | flops 4800 | bytes 740 | tf_op jit(solution)/shard_map/tk,jk->tj/dot_general | solution.py:979
  22.4 0.1 copy.40
  22.5 0.1 broadcast_in_dim.7
  22.6 0.1 broadcast_in_dim.8.mixed_table
  22.7 1.1 %shard_map.98 = (f32[40,4,8,128]{3,2,1,0:T(8,128)S(1)}, f32[40,5,8,128]{3,2,1,0:T(8,128)S(1)}, f32[40,4,8,128]{3,2,1,0:T(8,128)S(1)}, f32[40,4,8,128]{3,2,1,0:T(...) custom-call(s32[2,8,128]{2,1,0:T(8,128)S(1)} %stack.6.place, ...), custom_call_target="tpu_custom_call" | custom-call | tf_op jit(solution)/shard_map/pallas_call | solution.py:914
  23.8 0.1 collective-permute-done.6.edge_left
  23.9 4.0 %shard_map.99 = (f32[40,4,8,128]{3,2,1,0:T(8,128)S(1)}, f32[40,5,8,128]{3,2,1,0:T(8,128)S(1)}, f32[40,4,8,128]{3,2,1,0:T(8,128)S(1)}, f32[40,4,8,128]{3,2,1,0:T(...) custom-call(s32[2,8,128]{2,1,0:T(8,128)S(1)} %stack.6.place, ...), custom_call_target="tpu_custom_call", output_to_operand_aliasing={{0}: (6, {}), {1}: (7, {}), {2}: (8, {}), {3}: (9, {}), {4}... | custom-call | tf_op jit(solution)/shard_map/pallas_call | solution.py:914
  27.9 5.1 %shard_map.100 = (f32[40,4,8,128]{3,2,1,0:T(8,128)S(1)}, f32[40,5,8,128]{3,2,1,0:T(8,128)S(1)}, f32[40,4,8,128]{3,2,1,0:T(8,128)S(1)}, f32[40,4,8,128]{3,2,1,0:T...) custom-call(s32[2,8,128]{2,1,0:T(8,128)S(1)} %stack.6.place, ...), custom_call_target="tpu_custom_call", output_to_operand_aliasing={{0}: (4, {}), {1}: (5, {}), {2}: (6, {}), {3}: (7, {}), {4}... | custom-call | tf_op jit(solution)/shard_map/pallas_call | solution.py:914
  33.0 4.6 %collective-permute-start.8 = (f32[29,8,128]{2,1,0:T(8,128)S(1)}, f32[29,8,128]{2,1,0:T(8,128)S(1)}, u32[]{:S(2)}, u32[]{:S(2)}) collective-permute-start(f32[29,8,128]{2,1,0:T(8,128)S(1)} %get-tuple-element.131), channel_id=1, source_target_pairs={{0,4},{1,5},{2,6},{3,7},{4,0},{5,1},{6,2},{7,3},{8,16},{9,17},{10,... | collective-permute-start | bytes 356360 | tf_op jit(solution)/shard_map/ppermute | solution.py:944
  37.6 2.5 %collective-permute-done.8.refs_23_ = f32[29,8,128]{2,1,0:T(8,128)S(1)} collective-permute-done((f32[29,8,128]{2,1,0:T(8,128)S(1)}, f32[29,8,128]{2,1,0:T(8,128)S(1)}, u32[]{:S(2)}, u32[]{:S(2)}) %collective-permute-start.8) | collective-permute-done | bytes 118816 | tf_op jit(solution)/shard_map/ppermute | solution.py:944
  40.1 2.7 %collective-permute-done.9.refs_24_ = f32[29,8,128]{2,1,0:T(8,128)S(1)} collective-permute-done((f32[29,8,128]{2,1,0:T(8,128)S(1)}, f32[29,8,128]{2,1,0:T(8,128)S(1)}, u32[]{:S(2)}, u32[]{:S(2)}) %collective-permute-start.9) | collective-permute-done | bytes 118816 | tf_op jit(solution)/shard_map/ppermute | solution.py:944
  42.8 6.0 %shard_map.101 = (f32[40,20,8,128]{3,2,1,0:T(8,128)S(1)}, f32[40,8,128]{2,1,0:T(8,128)S(1)}, f32[25,8,128]{2,1,0:T(8,128)S(1)}, f32[15,1,8,128]{3,2,1,0:T(8,128)...) custom-call(s32[2,8,128]{2,1,0:T(8,128)S(1)} %stack.6.place, ...), custom_call_target="tpu_custom_call" | custom-call | tf_op jit(solution)/shard_map/pallas_call | solution.py:914
  48.8 2.3 %collective-permute-start.11 = (f32[25,8,128]{2,1,0:T(8,128)S(1)}, f32[25,8,128]{2,1,0:T(8,128)S(1)}, u32[]{:S(2)}, u32[]{:S(2)}) collective-permute-start(f32[25,8,128]{2,1,0:T(8,128)S(1)} %get-tuple-element.135), channel_id=1, source_target_pairs={{0,1},{1,0},{2,3},{3,2},{4,8},{5,9},{6,10},{7,11},{8,4},{9,5},{10,... | collective-permute-start | bytes 307208 | tf_op jit(solution)/shard_map/ppermute | solution.py:944
  51.0 4.3 %collective-permute-done.11.refs_9_ = f32[25,8,128]{2,1,0:T(8,128)S(1)} collective-permute-done((f32[25,8,128]{2,1,0:T(8,128)S(1)}, f32[25,8,128]{2,1,0:T(8,128)S(1)}, u32[]{:S(2)}, u32[]{:S(2)}) %collective-permute-start.11) | collective-permute-done | bytes 102432 | tf_op jit(solution)/shard_map/ppermute | solution.py:944
  55.3 0.6 collective-permute-done.10.refs_8_
  55.9 1.0 %shard_map.102 = (f32[20,10,8,128]{3,2,1,0:T(8,128)S(1)}, f32[20,10,8,128]{3,2,1,0:T(8,128)S(1)}, f32[4,5,8,128]{3,2,1,0:T(8,128)S(1)}) custom-call(s32[2,8,128]{2,1,0:T(8,128)S(1)} %stack.6.place, f32[20,2,8,128]{3,2,1,0:T(8,128)S(1)} %get-tuple-element.117.refs_9_.refs_0_.refs_7_, f32[20,3,8,128]{3,2,1,0:T(8,128)S(1)} %get-tuple-element.118.refs_10_.refs_1_.refs_8_, ...), custom_call_target="tpu_custom_call" | custom-call | tf_op jit(solution)/shard_map/pallas_call | solution.py:914
  56.9 2.3 %collective-permute-start.13 = (f32[4,5,8,128]{3,2,1,0:T(8,128)S(1)}, f32[4,5,8,128]{3,2,1,0:T(8,128)S(1)}, u32[]{:S(2)}, u32[]{:S(2)}) collective-permute-start(f32[4,5,8,128]{3,2,1,0:T(8,128)S(1)} %get-tuple-element.143.refs_19_), channel_id=1, source_target_pairs={{0,4},{1,5},{2,6},{3,7},{4,0},{5,1},{6,2},{7,3},{8,16},{9,17},{10,... | collective-permute-start | bytes 245768 | tf_op jit(solution)/shard_map/ppermute | solution.py:944
  59.2 2.9 %collective-permute-done.13.refs_21_ = f32[4,5,8,128]{3,2,1,0:T(8,128)S(1)} collective-permute-done((f32[4,5,8,128]{3,2,1,0:T(8,128)S(1)}, f32[4,5,8,128]{3,2,1,0:T(8,128)S(1)}, u32[]{:S(2)}, u32[]{:S(2)}) %collective-permute-start.13) | collective-permute-done | bytes 81952 | tf_op jit(solution)/shard_map/ppermute | solution.py:944
  62.0 0.9 %collective-permute-done.12.refs_20_ = f32[4,5,8,128]{3,2,1,0:T(8,128)S(1)} collective-permute-done((f32[4,5,8,128]{3,2,1,0:T(8,128)S(1)}, f32[4,5,8,128]{3,2,1,0:T(8,128)S(1)}, u32[]{:S(2)}, u32[]{:S(2)}) %collective-permute-start.12) | collective-permute-done | bytes 81952 | tf_op jit(solution)/shard_map/ppermute | solution.py:944
  62.9 3.6 %shard_map.103 = (f32[5,64,256]{2,1,0:T(8,128)}, f32[64,256]{1,0:T(8,128)}) custom-call(s32[2,8,128]{2,1,0:T(8,128)S(1)} %stack.6.place, f32[40,4,8,128]{3,2,1,0:T(8,128)S(1)} %get-tuple-element.108.refs_0_, f32[40,5,8,128]{3,2,1,0:T(8,128)S(1)} %get-tuple-element.109.refs_1_, f32[40,4,8,128]{3,2,1,0:T(8,128)S(1)} %get-tuple-element.110.refs_2_, ...), custom_call_target="tpu_custom_call" | custom-call | tf_op jit(solution)/shard_map/pallas_call | solution.py:914
  (15 shorter events, 0.1 us)
Async XLA Ops:
  0.6 20.9 %copy-start = (f32[16,5]{0,1:T(8,128)S(1)}, f32[16,5]{0,1:T(8,128)}, u32[]{:S(2)}) copy-start(f32[16,5]{0,1:T(8,128)} %param.14) | copy-start | bytes 964
  2.0 14.7 %collective-permute-start.5 = (f32[33,2,8,128]{3,2,1,0:T(8,128)S(1)}, f32[33,2,8,128]{3,2,1,0:T(8,128)S(1)}, u32[]{:S(2)}, u32[]{:S(2)}) collective-permute-start(f32[33,2,8,128]{3,2,1,0:T(8,128)S(1)} %get-tuple-element.74.own), channel_id=1, source_target_pairs={{0,1},{1,0},{2,3},{3,2},{4,8},{5,9},{6,10},{7,11},{8,4},{9,5},{10,... | collective-permute-start | bytes 811016 | tf_op jit(solution)/shard_map/ppermute | solution.py:944
  7.1 9.9 %collective-permute-start.4 = (f32[33,2,8,128]{3,2,1,0:T(8,128)S(1)}, f32[33,2,8,128]{3,2,1,0:T(8,128)S(1)}, u32[]{:S(2)}, u32[]{:S(2)}) collective-permute-start(f32[33,2,8,128]{3,2,1,0:T(8,128)S(1)} %get-tuple-element.74.own), channel_id=1, source_target_pairs={{0,4},{1,5},{2,6},{3,7},{4,0},{5,1},{6,2},{7,3},{8,12},{9,13},{10,... | collective-permute-start | bytes 811016 | tf_op jit(solution)/shard_map/ppermute | solution.py:944
  7.1 7.3 %collective-permute-start = (f32[264,64]{1,0:T(8,128)S(1)}, f32[264,64]{1,0:T(8,128)S(1)}, u32[]{:S(2)}, u32[]{:S(2)}) collective-permute-start(f32[264,64]{1,0:T(8,128)S(1)} %get-tuple-element.75), channel_id=1, source_target_pairs={{0,1},{1,2},{2,3},{3,0},{4,5},{5,6},{6,7},{7,4},{8,9},{9,10},{10,1... | collective-permute-start | bytes 202760 | tf_op jit(solution)/shard_map/ppermute | solution.py:926
  8.7 5.7 %collective-permute-start.1 = (f32[264,64]{1,0:T(8,128)S(1)}, f32[264,64]{1,0:T(8,128)S(1)}, u32[]{:S(2)}, u32[]{:S(2)}) collective-permute-start(f32[264,64]{1,0:T(8,128)S(1)} %get-tuple-element.76), channel_id=1, source_target_pairs={{0,3},{1,0},{2,1},{3,2},{4,7},{5,4},{6,5},{7,6},{8,11},{9,8},{10,9... | collective-permute-start | bytes 202760 | tf_op jit(solution)/shard_map/ppermute | solution.py:926
  14.8 13.1 %collective-permute-start.3 = (f32[33,3,8,128]{3,2,1,0:T(8,128)S(1)}, f32[33,3,8,128]{3,2,1,0:T(8,128)S(1)}, u32[]{:S(2)}, u32[]{:S(2)}) collective-permute-start(f32[33,3,8,128]{3,2,1,0:T(8,128)S(1)} %shard_map.96.whole), channel_id=1, source_target_pairs={{0,4},{1,5},{2,6},{3,7},{4,0},{5,1},{6,2},{7,3},{8,16},{9,17},{10,... | collective-permute-start | bytes 1216520 | tf_op jit(solution)/shard_map/ppermute | solution.py:944
  16.7 11.2 %collective-permute-start.2 = (f32[33,3,8,128]{3,2,1,0:T(8,128)S(1)}, f32[33,3,8,128]{3,2,1,0:T(8,128)S(1)}, u32[]{:S(2)}, u32[]{:S(2)}) collective-permute-start(f32[33,3,8,128]{3,2,1,0:T(8,128)S(1)} %shard_map.96.whole), channel_id=1, source_target_pairs={{0,8},{1,9},{2,10},{3,11},{4,12},{5,13},{6,14},{7,15},{8,0},{9,1},... | collective-permute-start | bytes 1216520 | tf_op jit(solution)/shard_map/ppermute | solution.py:944
  17.7 6.2 %collective-permute-start.6 = (f32[33,8,128]{2,1,0:T(8,128)S(1)}, f32[33,8,128]{2,1,0:T(8,128)S(1)}, u32[]{:S(2)}, u32[]{:S(2)}) collective-permute-start(f32[33,8,128]{2,1,0:T(8,128)S(1)} %get-tuple-element.77), channel_id=1, source_target_pairs={{0,1},{1,2},{2,3},{3,0},{4,5},{5,6},{6,7},{7,4},{8,9},{9,10},{10,1... | collective-permute-start | bytes 405512 | tf_op jit(solution)/shard_map/ppermute | solution.py:926
  19.4 4.5 %collective-permute-start.7 = (f32[33,8,128]{2,1,0:T(8,128)S(1)}, f32[33,8,128]{2,1,0:T(8,128)S(1)}, u32[]{:S(2)}, u32[]{:S(2)}) collective-permute-start(f32[33,8,128]{2,1,0:T(8,128)S(1)} %get-tuple-element.78), channel_id=1, source_target_pairs={{0,3},{1,0},{2,1},{3,2},{4,7},{5,4},{6,5},{7,6},{8,11},{9,8},{10,9... | collective-permute-start | bytes 405512 | tf_op jit(solution)/shard_map/ppermute | solution.py:926
  33.0 7.1 %collective-permute-start.8 = (f32[29,8,128]{2,1,0:T(8,128)S(1)}, f32[29,8,128]{2,1,0:T(8,128)S(1)}, u32[]{:S(2)}, u32[]{:S(2)}) collective-permute-start(f32[29,8,128]{2,1,0:T(8,128)S(1)} %get-tuple-element.131), channel_id=1, source_target_pairs={{0,4},{1,5},{2,6},{3,7},{4,0},{5,1},{6,2},{7,3},{8,16},{9,17},{10,... | collective-permute-start | bytes 356360 | tf_op jit(solution)/shard_map/ppermute | solution.py:944
  37.6 5.2 %collective-permute-start.9 = (f32[29,8,128]{2,1,0:T(8,128)S(1)}, f32[29,8,128]{2,1,0:T(8,128)S(1)}, u32[]{:S(2)}, u32[]{:S(2)}) collective-permute-start(f32[29,8,128]{2,1,0:T(8,128)S(1)} %get-tuple-element.132), channel_id=1, source_target_pairs={{0,8},{1,9},{2,10},{3,11},{4,12},{5,13},{6,14},{7,15},{8,0},{9,1},... | collective-permute-start | bytes 356360 | tf_op jit(solution)/shard_map/ppermute | solution.py:944
  42.8 20.1 %copy-start.1 = (f32[8,8,256]{2,1,0:T(8,128)S(1)}, f32[8,8,256]{2,1,0:T(8,128)}, u32[]{:S(2)}) copy-start(f32[8,8,256]{2,1,0:T(8,128)} %param.8) | copy-start | bytes 196612
  48.8 6.5 %collective-permute-start.11 = (f32[25,8,128]{2,1,0:T(8,128)S(1)}, f32[25,8,128]{2,1,0:T(8,128)S(1)}, u32[]{:S(2)}, u32[]{:S(2)}) collective-permute-start(f32[25,8,128]{2,1,0:T(8,128)S(1)} %get-tuple-element.135), channel_id=1, source_target_pairs={{0,1},{1,0},{2,3},{3,2},{4,8},{5,9},{6,10},{7,11},{8,4},{9,5},{10,... | collective-permute-start | bytes 307208 | tf_op jit(solution)/shard_map/ppermute | solution.py:944
  51.0 4.9 %collective-permute-start.10 = (f32[25,8,128]{2,1,0:T(8,128)S(1)}, f32[25,8,128]{2,1,0:T(8,128)S(1)}, u32[]{:S(2)}, u32[]{:S(2)}) collective-permute-start(f32[25,8,128]{2,1,0:T(8,128)S(1)} %get-tuple-element.135), channel_id=1, source_target_pairs={{0,4},{1,5},{2,6},{3,7},{4,0},{5,1},{6,2},{7,3},{8,12},{9,13},{10,... | collective-permute-start | bytes 307208 | tf_op jit(solution)/shard_map/ppermute | solution.py:944
  56.9 5.2 %collective-permute-start.13 = (f32[4,5,8,128]{3,2,1,0:T(8,128)S(1)}, f32[4,5,8,128]{3,2,1,0:T(8,128)S(1)}, u32[]{:S(2)}, u32[]{:S(2)}) collective-permute-start(f32[4,5,8,128]{3,2,1,0:T(8,128)S(1)} %get-tuple-element.143.refs_19_), channel_id=1, source_target_pairs={{0,4},{1,5},{2,6},{3,7},{4,0},{5,1},{6,2},{7,3},{8,16},{9,17},{10,... | collective-permute-start | bytes 245768 | tf_op jit(solution)/shard_map/ppermute | solution.py:944
  59.2 3.7 %collective-permute-start.12 = (f32[4,5,8,128]{3,2,1,0:T(8,128)S(1)}, f32[4,5,8,128]{3,2,1,0:T(8,128)S(1)}, u32[]{:S(2)}, u32[]{:S(2)}) collective-permute-start(f32[4,5,8,128]{3,2,1,0:T(8,128)S(1)} %get-tuple-element.143.refs_19_), channel_id=1, source_target_pairs={{0,8},{1,9},{2,10},{3,11},{4,12},{5,13},{6,14},{7,15},{8,0},{9,1},... | collective-permute-start | bytes 245768 | tf_op jit(solution)/shard_map/ppermute | solution.py:944

commit v7 on v6

--- a/solution.py
+++ b/solution.py
@@ -572,7 +572,9 @@
     rows_loop(0, 33, body, 11)
 
 
-def prepare(place, mixed_table, state, f1, blocks, gx_rows, total_rows, relax_rows, sum_rows):
+def prepare(
+    place, mixed_table, state, f1, blocks, gx_rows, total_rows, relax_rows, sum_rows, unroll=8
+):
     (gx0, gy0, via0, below0, cap0, total0, weights0, f0, x0) = state[:9]
     below1, volt, conduct, surface, spare = state[9:14]
     fine = Level(4, gx0, gy0, via0, below0, cap0, total0, weights0)
@@ -605,7 +607,7 @@
                 for p in range(4):
                     ref[8 * b + s, p] = phases[p]
 
-        rows_loop(0, 8, place_row, 4)
+        rows_loop(0, 8, place_row, unroll)
         loads = spread(block(32, 0), block(32, 1), rim(32))
         for p in range(4):
             values = [jnp.zeros((8, LANES), jnp.float32) for _ in range(SECTIONS)]
@@ -648,9 +650,9 @@
         set_source(i)
 
     for low, high in gx_rows:
-        rows_loop(low, high, set_gx, 4)
+        rows_loop(low, high, set_gx, 8)
     for low, high in total_rows:
-        rows_loop(low, high, set_row)
+        rows_loop(low, high, set_row, 4)
     for low, high in relax_rows:
         fine.relax(x0, spare, f0, low, high)
     for low, high in sum_rows:
@@ -697,6 +699,7 @@
         ((9, 17), (23, 31)),
         ((10, 18), (22, 30)),
         ((6, 14),),
+        4,
     )
 
 

time: 67.3 us -> 66.6 us (0.990)
  Pallas kernels: 23 us -> 22.1 us
    pallas_call x9, Pallas kernels: 23 us -> 22.1 us  [call(): pl.pallas_call(kernel, out_shape=outs, in_specs=[pl.BlockSpec(memory_spac...]
where the time goes in v7:
time: 66.6 us; the launch traced here: 65.9 us
  starting transfers between devices  23.8 us (36%)
  Pallas kernels  22.1 us (33%)
  waiting for transfers between devices  18 us (27%)
  matrix products  0.81 us (1%)
  between operations  0.74 us (1%)
    pallas_call x9, Pallas kernels, call(): pl.pallas_call(kernel, out_shape=outs, in_specs=[pl.BlockSpec(memory_spac...  22.1 us
    ppermute x10, starting transfers between devices, paired(): result[which] = lax.ppermute(values[which], ('section', 'gx', 'gy'), pairs)  16.1 us
    ppermute x10, waiting for transfers between devices, paired(): result[which] = lax.ppermute(values[which], ('section', 'gx', 'gy'), pairs)  14.1 us
    ppermute x4, starting transfers between devices, turned(): lax.ppermute(value, axis, [(i, (i + shift) % count) for i in range(count)])  7.67 us
    ppermute x4, waiting for transfers between devices, turned(): lax.ppermute(value, axis, [(i, (i + shift) % count) for i in range(count)])  3.9 us
  transfers between devices with their start and end apart: 14, of which 10 were waited for; matrix products, arithmetic and copies ran while one was open for 2% of the time, Pallas kernels for 9%

profile of v7, /device:TPU:1, one launch (start us, length us, event | category | flops | bytes accessed | tf_op | source)
XLA Modules:
  0.0 65.9 jit_solution(14013908806314534857)
XLA Ops:
  0.6 1.3 %shard_map.95 = (f32[33,2,8,128]{3,2,1,0:T(8,128)S(1)}, f32[264,64]{1,0:T(8,128)S(1)}, f32[264,64]{1,0:T(8,128)S(1)}) custom-call(f32[64,256]{1,0:T(8,128)} %bitcast.11, f32[64,256]{1,0:T(8,128)} %bitcast.13, s32[64,256]{1,0:T(8,128)} %bitcast.14, s32[56,256]{1,0:T(8,128)} %bitcast.15, s32[8,256]{1,0:T(8,128)} %refs_4_.1, s32[8,256]{1,0:T(8,128)} %refs_5_.1), custom_call_target="tpu_custom_call" | custom-call | tf_op jit(solution)/shard_map/pallas_call | solution.py:917
  2.0 5.1 %collective-permute-start.5 = (f32[33,2,8,128]{3,2,1,0:T(8,128)S(1)}, f32[33,2,8,128]{3,2,1,0:T(8,128)S(1)}, u32[]{:S(2)}, u32[]{:S(2)}) collective-permute-start(f32[33,2,8,128]{3,2,1,0:T(8,128)S(1)} %get-tuple-element.74.own), channel_id=1, source_target_pairs={{0,1},{1,0},{2,3},{3,2},{4,8},{5,9},{6,10},{7,11},{8,4},{9,5},{10,... | collective-permute-start | bytes 811016 | tf_op jit(solution)/shard_map/ppermute | solution.py:947
  7.1 1.6 %collective-permute-start = (f32[264,64]{1,0:T(8,128)S(1)}, f32[264,64]{1,0:T(8,128)S(1)}, u32[]{:S(2)}, u32[]{:S(2)}) collective-permute-start(f32[264,64]{1,0:T(8,128)S(1)} %get-tuple-element.75), channel_id=1, source_target_pairs={{0,1},{1,2},{2,3},{3,0},{4,5},{5,6},{6,7},{7,4},{8,9},{9,10},{10,1... | collective-permute-start | bytes 202760 | tf_op jit(solution)/shard_map/ppermute | solution.py:929
  8.7 2.1 %collective-permute-start.1 = (f32[264,64]{1,0:T(8,128)S(1)}, f32[264,64]{1,0:T(8,128)S(1)}, u32[]{:S(2)}, u32[]{:S(2)}) collective-permute-start(f32[264,64]{1,0:T(8,128)S(1)} %get-tuple-element.76), channel_id=1, source_target_pairs={{0,3},{1,0},{2,1},{3,2},{4,7},{5,4},{6,5},{7,6},{8,11},{9,8},{10,9... | collective-permute-start | bytes 202760 | tf_op jit(solution)/shard_map/ppermute | solution.py:929
  10.9 3.5 %collective-permute-done.from_lower = f32[264,64]{1,0:T(8,128)S(1)} collective-permute-done((f32[264,64]{1,0:T(8,128)S(1)}, f32[264,64]{1,0:T(8,128)S(1)}, u32[]{:S(2)}, u32[]{:S(2)}) %collective-permute-start) | collective-permute-done | bytes 67616 | tf_op jit(solution)/shard_map/ppermute | solution.py:929
  14.4 0.1 collective-permute-done.1.from_upper
  14.5 0.4 shard_map.96.whole
  14.8 1.8 %collective-permute-start.3 = (f32[33,3,8,128]{3,2,1,0:T(8,128)S(1)}, f32[33,3,8,128]{3,2,1,0:T(8,128)S(1)}, u32[]{:S(2)}, u32[]{:S(2)}) collective-permute-start(f32[33,3,8,128]{3,2,1,0:T(8,128)S(1)} %shard_map.96.whole), channel_id=1, source_target_pairs={{0,4},{1,5},{2,6},{3,7},{4,0},{5,1},{6,2},{7,3},{8,16},{9,17},{10,... | collective-permute-start | bytes 1216520 | tf_op jit(solution)/shard_map/ppermute | solution.py:947
  16.7 0.3 collective-permute-done.4.near0
  17.1 0.5 shard_map.97
  17.7 1.7 %collective-permute-start.6 = (f32[33,8,128]{2,1,0:T(8,128)S(1)}, f32[33,8,128]{2,1,0:T(8,128)S(1)}, u32[]{:S(2)}, u32[]{:S(2)}) collective-permute-start(f32[33,8,128]{2,1,0:T(8,128)S(1)} %get-tuple-element.77), channel_id=1, source_target_pairs={{0,1},{1,2},{2,3},{3,0},{4,5},{5,6},{6,7},{7,4},{8,9},{9,10},{10,1... | collective-permute-start | bytes 405512 | tf_op jit(solution)/shard_map/ppermute | solution.py:929
  19.4 2.2 %collective-permute-start.7 = (f32[33,8,128]{2,1,0:T(8,128)S(1)}, f32[33,8,128]{2,1,0:T(8,128)S(1)}, u32[]{:S(2)}, u32[]{:S(2)}) collective-permute-start(f32[33,8,128]{2,1,0:T(8,128)S(1)} %get-tuple-element.78), channel_id=1, source_target_pairs={{0,3},{1,0},{2,1},{3,2},{4,7},{5,4},{6,5},{7,6},{8,11},{9,8},{10,9... | collective-permute-start | bytes 405512 | tf_op jit(solution)/shard_map/ppermute | solution.py:929
  21.6 0.8 %convolution_bitcast_fusion = f32[16,5]{0,1:T(8,128)S(1)} fusion(f32[5,5]{1,0:T(8,128)} %constant.17.clone, f32[16,5]{0,1:T(8,128)S(1)} %copy-done), kind=kOutput, calls=%fused_computation | convolution fusion | flops 4800 | bytes 740 | tf_op jit(solution)/shard_map/tk,jk->tj/dot_general | solution.py:982
  22.4 0.1 copy.40
  22.5 0.1 broadcast_in_dim.7
  22.6 0.1 broadcast_in_dim.8.mixed_table
  22.7 0.9 %shard_map.98 = (f32[40,4,8,128]{3,2,1,0:T(8,128)S(1)}, f32[40,5,8,128]{3,2,1,0:T(8,128)S(1)}, f32[40,4,8,128]{3,2,1,0:T(8,128)S(1)}, f32[40,4,8,128]{3,2,1,0:T(...) custom-call(s32[2,8,128]{2,1,0:T(8,128)S(1)} %stack.6.place, ...), custom_call_target="tpu_custom_call" | custom-call | tf_op jit(solution)/shard_map/pallas_call | solution.py:917
  23.6 0.3 collective-permute-done.6.edge_left
  23.9 3.9 %shard_map.99 = (f32[40,4,8,128]{3,2,1,0:T(8,128)S(1)}, f32[40,5,8,128]{3,2,1,0:T(8,128)S(1)}, f32[40,4,8,128]{3,2,1,0:T(8,128)S(1)}, f32[40,4,8,128]{3,2,1,0:T(...) custom-call(s32[2,8,128]{2,1,0:T(8,128)S(1)} %stack.6.place, ...), custom_call_target="tpu_custom_call", output_to_operand_aliasing={{0}: (6, {}), {1}: (7, {}), {2}: (8, {}), {3}: (9, {}), {4}... | custom-call | tf_op jit(solution)/shard_map/pallas_call | solution.py:917
  27.9 4.5 %shard_map.100 = (f32[40,4,8,128]{3,2,1,0:T(8,128)S(1)}, f32[40,5,8,128]{3,2,1,0:T(8,128)S(1)}, f32[40,4,8,128]{3,2,1,0:T(8,128)S(1)}, f32[40,4,8,128]{3,2,1,0:T...) custom-call(s32[2,8,128]{2,1,0:T(8,128)S(1)} %stack.6.place, ...), custom_call_target="tpu_custom_call", output_to_operand_aliasing={{0}: (4, {}), {1}: (5, {}), {2}: (6, {}), {3}: (7, {}), {4}... | custom-call | tf_op jit(solution)/shard_map/pallas_call | solution.py:917
  32.3 4.6 %collective-permute-start.8 = (f32[29,8,128]{2,1,0:T(8,128)S(1)}, f32[29,8,128]{2,1,0:T(8,128)S(1)}, u32[]{:S(2)}, u32[]{:S(2)}) collective-permute-start(f32[29,8,128]{2,1,0:T(8,128)S(1)} %get-tuple-element.131), channel_id=1, source_target_pairs={{0,4},{1,5},{2,6},{3,7},{4,0},{5,1},{6,2},{7,3},{8,16},{9,17},{10,... | collective-permute-start | bytes 356360 | tf_op jit(solution)/shard_map/ppermute | solution.py:947
  37.0 2.5 %collective-permute-done.8.refs_23_ = f32[29,8,128]{2,1,0:T(8,128)S(1)} collective-permute-done((f32[29,8,128]{2,1,0:T(8,128)S(1)}, f32[29,8,128]{2,1,0:T(8,128)S(1)}, u32[]{:S(2)}, u32[]{:S(2)}) %collective-permute-start.8) | collective-permute-done | bytes 118816 | tf_op jit(solution)/shard_map/ppermute | solution.py:947
  39.5 2.7 %collective-permute-done.9.refs_24_ = f32[29,8,128]{2,1,0:T(8,128)S(1)} collective-permute-done((f32[29,8,128]{2,1,0:T(8,128)S(1)}, f32[29,8,128]{2,1,0:T(8,128)S(1)}, u32[]{:S(2)}, u32[]{:S(2)}) %collective-permute-start.9) | collective-permute-done | bytes 118816 | tf_op jit(solution)/shard_map/ppermute | solution.py:947
  42.1 6.0 %shard_map.101 = (f32[40,20,8,128]{3,2,1,0:T(8,128)S(1)}, f32[40,8,128]{2,1,0:T(8,128)S(1)}, f32[25,8,128]{2,1,0:T(8,128)S(1)}, f32[15,1,8,128]{3,2,1,0:T(8,128)...) custom-call(s32[2,8,128]{2,1,0:T(8,128)S(1)} %stack.6.place, ...), custom_call_target="tpu_custom_call" | custom-call | tf_op jit(solution)/shard_map/pallas_call | solution.py:917
  48.1 2.3 %collective-permute-start.11 = (f32[25,8,128]{2,1,0:T(8,128)S(1)}, f32[25,8,128]{2,1,0:T(8,128)S(1)}, u32[]{:S(2)}, u32[]{:S(2)}) collective-permute-start(f32[25,8,128]{2,1,0:T(8,128)S(1)} %get-tuple-element.135), channel_id=1, source_target_pairs={{0,1},{1,0},{2,3},{3,2},{4,8},{5,9},{6,10},{7,11},{8,4},{9,5},{10,... | collective-permute-start | bytes 307208 | tf_op jit(solution)/shard_map/ppermute | solution.py:947
  50.4 4.3 %collective-permute-done.11.refs_9_ = f32[25,8,128]{2,1,0:T(8,128)S(1)} collective-permute-done((f32[25,8,128]{2,1,0:T(8,128)S(1)}, f32[25,8,128]{2,1,0:T(8,128)S(1)}, u32[]{:S(2)}, u32[]{:S(2)}) %collective-permute-start.11) | collective-permute-done | bytes 102432 | tf_op jit(solution)/shard_map/ppermute | solution.py:947
  54.6 0.6 collective-permute-done.10.refs_8_
  55.2 1.0 %shard_map.102 = (f32[20,10,8,128]{3,2,1,0:T(8,128)S(1)}, f32[20,10,8,128]{3,2,1,0:T(8,128)S(1)}, f32[4,5,8,128]{3,2,1,0:T(8,128)S(1)}) custom-call(s32[2,8,128]{2,1,0:T(8,128)S(1)} %stack.6.place, f32[20,2,8,128]{3,2,1,0:T(8,128)S(1)} %get-tuple-element.117.refs_9_.refs_0_.refs_7_, f32[20,3,8,128]{3,2,1,0:T(8,128)S(1)} %get-tuple-element.118.refs_10_.refs_1_.refs_8_, ...), custom_call_target="tpu_custom_call" | custom-call | tf_op jit(solution)/shard_map/pallas_call | solution.py:917
  56.2 2.3 %collective-permute-start.13 = (f32[4,5,8,128]{3,2,1,0:T(8,128)S(1)}, f32[4,5,8,128]{3,2,1,0:T(8,128)S(1)}, u32[]{:S(2)}, u32[]{:S(2)}) collective-permute-start(f32[4,5,8,128]{3,2,1,0:T(8,128)S(1)} %get-tuple-element.143.refs_19_), channel_id=1, source_target_pairs={{0,4},{1,5},{2,6},{3,7},{4,0},{5,1},{6,2},{7,3},{8,16},{9,17},{10,... | collective-permute-start | bytes 245768 | tf_op jit(solution)/shard_map/ppermute | solution.py:947
  58.5 2.9 %collective-permute-done.13.refs_21_ = f32[4,5,8,128]{3,2,1,0:T(8,128)S(1)} collective-permute-done((f32[4,5,8,128]{3,2,1,0:T(8,128)S(1)}, f32[4,5,8,128]{3,2,1,0:T(8,128)S(1)}, u32[]{:S(2)}, u32[]{:S(2)}) %collective-permute-start.13) | collective-permute-done | bytes 81952 | tf_op jit(solution)/shard_map/ppermute | solution.py:947
  61.4 0.9 %collective-permute-done.12.refs_20_ = f32[4,5,8,128]{3,2,1,0:T(8,128)S(1)} collective-permute-done((f32[4,5,8,128]{3,2,1,0:T(8,128)S(1)}, f32[4,5,8,128]{3,2,1,0:T(8,128)S(1)}, u32[]{:S(2)}, u32[]{:S(2)}) %collective-permute-start.12) | collective-permute-done | bytes 81952 | tf_op jit(solution)/shard_map/ppermute | solution.py:947
  62.2 3.6 %shard_map.103 = (f32[5,64,256]{2,1,0:T(8,128)}, f32[64,256]{1,0:T(8,128)}) custom-call(s32[2,8,128]{2,1,0:T(8,128)S(1)} %stack.6.place, f32[40,4,8,128]{3,2,1,0:T(8,128)S(1)} %get-tuple-element.108.refs_0_, f32[40,5,8,128]{3,2,1,0:T(8,128)S(1)} %get-tuple-element.109.refs_1_, f32[40,4,8,128]{3,2,1,0:T(8,128)S(1)} %get-tuple-element.110.refs_2_, ...), custom_call_target="tpu_custom_call" | custom-call | tf_op jit(solution)/shard_map/pallas_call | solution.py:917
  (15 shorter events, 0.1 us)
Async XLA Ops:
  0.6 20.9 %copy-start = (f32[16,5]{0,1:T(8,128)S(1)}, f32[16,5]{0,1:T(8,128)}, u32[]{:S(2)}) copy-start(f32[16,5]{0,1:T(8,128)} %param.14) | copy-start | bytes 964
  2.0 14.7 %collective-permute-start.5 = (f32[33,2,8,128]{3,2,1,0:T(8,128)S(1)}, f32[33,2,8,128]{3,2,1,0:T(8,128)S(1)}, u32[]{:S(2)}, u32[]{:S(2)}) collective-permute-start(f32[33,2,8,128]{3,2,1,0:T(8,128)S(1)} %get-tuple-element.74.own), channel_id=1, source_target_pairs={{0,1},{1,0},{2,3},{3,2},{4,8},{5,9},{6,10},{7,11},{8,4},{9,5},{10,... | collective-permute-start | bytes 811016 | tf_op jit(solution)/shard_map/ppermute | solution.py:947
  7.1 9.9 %collective-permute-start.4 = (f32[33,2,8,128]{3,2,1,0:T(8,128)S(1)}, f32[33,2,8,128]{3,2,1,0:T(8,128)S(1)}, u32[]{:S(2)}, u32[]{:S(2)}) collective-permute-start(f32[33,2,8,128]{3,2,1,0:T(8,128)S(1)} %get-tuple-element.74.own), channel_id=1, source_target_pairs={{0,4},{1,5},{2,6},{3,7},{4,0},{5,1},{6,2},{7,3},{8,12},{9,13},{10,... | collective-permute-start | bytes 811016 | tf_op jit(solution)/shard_map/ppermute | solution.py:947
  7.1 7.3 %collective-permute-start = (f32[264,64]{1,0:T(8,128)S(1)}, f32[264,64]{1,0:T(8,128)S(1)}, u32[]{:S(2)}, u32[]{:S(2)}) collective-permute-start(f32[264,64]{1,0:T(8,128)S(1)} %get-tuple-element.75), channel_id=1, source_target_pairs={{0,1},{1,2},{2,3},{3,0},{4,5},{5,6},{6,7},{7,4},{8,9},{9,10},{10,1... | collective-permute-start | bytes 202760 | tf_op jit(solution)/shard_map/ppermute | solution.py:929
  8.7 5.7 %collective-permute-start.1 = (f32[264,64]{1,0:T(8,128)S(1)}, f32[264,64]{1,0:T(8,128)S(1)}, u32[]{:S(2)}, u32[]{:S(2)}) collective-permute-start(f32[264,64]{1,0:T(8,128)S(1)} %get-tuple-element.76), channel_id=1, source_target_pairs={{0,3},{1,0},{2,1},{3,2},{4,7},{5,4},{6,5},{7,6},{8,11},{9,8},{10,9... | collective-permute-start | bytes 202760 | tf_op jit(solution)/shard_map/ppermute | solution.py:929
  14.8 13.0 %collective-permute-start.3 = (f32[33,3,8,128]{3,2,1,0:T(8,128)S(1)}, f32[33,3,8,128]{3,2,1,0:T(8,128)S(1)}, u32[]{:S(2)}, u32[]{:S(2)}) collective-permute-start(f32[33,3,8,128]{3,2,1,0:T(8,128)S(1)} %shard_map.96.whole), channel_id=1, source_target_pairs={{0,4},{1,5},{2,6},{3,7},{4,0},{5,1},{6,2},{7,3},{8,16},{9,17},{10,... | collective-permute-start | bytes 1216520 | tf_op jit(solution)/shard_map/ppermute | solution.py:947
  16.7 11.2 %collective-permute-start.2 = (f32[33,3,8,128]{3,2,1,0:T(8,128)S(1)}, f32[33,3,8,128]{3,2,1,0:T(8,128)S(1)}, u32[]{:S(2)}, u32[]{:S(2)}) collective-permute-start(f32[33,3,8,128]{3,2,1,0:T(8,128)S(1)} %shard_map.96.whole), channel_id=1, source_target_pairs={{0,8},{1,9},{2,10},{3,11},{4,12},{5,13},{6,14},{7,15},{8,0},{9,1},... | collective-permute-start | bytes 1216520 | tf_op jit(solution)/shard_map/ppermute | solution.py:947
  17.7 6.2 %collective-permute-start.6 = (f32[33,8,128]{2,1,0:T(8,128)S(1)}, f32[33,8,128]{2,1,0:T(8,128)S(1)}, u32[]{:S(2)}, u32[]{:S(2)}) collective-permute-start(f32[33,8,128]{2,1,0:T(8,128)S(1)} %get-tuple-element.77), channel_id=1, source_target_pairs={{0,1},{1,2},{2,3},{3,0},{4,5},{5,6},{6,7},{7,4},{8,9},{9,10},{10,1... | collective-permute-start | bytes 405512 | tf_op jit(solution)/shard_map/ppermute | solution.py:929
  19.4 4.5 %collective-permute-start.7 = (f32[33,8,128]{2,1,0:T(8,128)S(1)}, f32[33,8,128]{2,1,0:T(8,128)S(1)}, u32[]{:S(2)}, u32[]{:S(2)}) collective-permute-start(f32[33,8,128]{2,1,0:T(8,128)S(1)} %get-tuple-element.78), channel_id=1, source_target_pairs={{0,3},{1,0},{2,1},{3,2},{4,7},{5,4},{6,5},{7,6},{8,11},{9,8},{10,9... | collective-permute-start | bytes 405512 | tf_op jit(solution)/shard_map/ppermute | solution.py:929
  32.3 7.1 %collective-permute-start.8 = (f32[29,8,128]{2,1,0:T(8,128)S(1)}, f32[29,8,128]{2,1,0:T(8,128)S(1)}, u32[]{:S(2)}, u32[]{:S(2)}) collective-permute-start(f32[29,8,128]{2,1,0:T(8,128)S(1)} %get-tuple-element.131), channel_id=1, source_target_pairs={{0,4},{1,5},{2,6},{3,7},{4,0},{5,1},{6,2},{7,3},{8,16},{9,17},{10,... | collective-permute-start | bytes 356360 | tf_op jit(solution)/shard_map/ppermute | solution.py:947
  37.0 5.2 %collective-permute-start.9 = (f32[29,8,128]{2,1,0:T(8,128)S(1)}, f32[29,8,128]{2,1,0:T(8,128)S(1)}, u32[]{:S(2)}, u32[]{:S(2)}) collective-permute-start(f32[29,8,128]{2,1,0:T(8,128)S(1)} %get-tuple-element.132), channel_id=1, source_target_pairs={{0,8},{1,9},{2,10},{3,11},{4,12},{5,13},{6,14},{7,15},{8,0},{9,1},... | collective-permute-start | bytes 356360 | tf_op jit(solution)/shard_map/ppermute | solution.py:947
  42.1 20.1 %copy-start.1 = (f32[8,8,256]{2,1,0:T(8,128)S(1)}, f32[8,8,256]{2,1,0:T(8,128)}, u32[]{:S(2)}) copy-start(f32[8,8,256]{2,1,0:T(8,128)} %param.8) | copy-start | bytes 196612
  48.1 6.5 %collective-permute-start.11 = (f32[25,8,128]{2,1,0:T(8,128)S(1)}, f32[25,8,128]{2,1,0:T(8,128)S(1)}, u32[]{:S(2)}, u32[]{:S(2)}) collective-permute-start(f32[25,8,128]{2,1,0:T(8,128)S(1)} %get-tuple-element.135), channel_id=1, source_target_pairs={{0,1},{1,0},{2,3},{3,2},{4,8},{5,9},{6,10},{7,11},{8,4},{9,5},{10,... | collective-permute-start | bytes 307208 | tf_op jit(solution)/shard_map/ppermute | solution.py:947
  50.4 4.9 %collective-permute-start.10 = (f32[25,8,128]{2,1,0:T(8,128)S(1)}, f32[25,8,128]{2,1,0:T(8,128)S(1)}, u32[]{:S(2)}, u32[]{:S(2)}) collective-permute-start(f32[25,8,128]{2,1,0:T(8,128)S(1)} %get-tuple-element.135), channel_id=1, source_target_pairs={{0,4},{1,5},{2,6},{3,7},{4,0},{5,1},{6,2},{7,3},{8,12},{9,13},{10,... | collective-permute-start | bytes 307208 | tf_op jit(solution)/shard_map/ppermute | solution.py:947
  56.2 5.2 %collective-permute-start.13 = (f32[4,5,8,128]{3,2,1,0:T(8,128)S(1)}, f32[4,5,8,128]{3,2,1,0:T(8,128)S(1)}, u32[]{:S(2)}, u32[]{:S(2)}) collective-permute-start(f32[4,5,8,128]{3,2,1,0:T(8,128)S(1)} %get-tuple-element.143.refs_19_), channel_id=1, source_target_pairs={{0,4},{1,5},{2,6},{3,7},{4,0},{5,1},{6,2},{7,3},{8,16},{9,17},{10,... | collective-permute-start | bytes 245768 | tf_op jit(solution)/shard_map/ppermute | solution.py:947
  58.5 3.7 %collective-permute-start.12 = (f32[4,5,8,128]{3,2,1,0:T(8,128)S(1)}, f32[4,5,8,128]{3,2,1,0:T(8,128)S(1)}, u32[]{:S(2)}, u32[]{:S(2)}) collective-permute-start(f32[4,5,8,128]{3,2,1,0:T(8,128)S(1)} %get-tuple-element.143.refs_19_), channel_id=1, source_target_pairs={{0,8},{1,9},{2,10},{3,11},{4,12},{5,13},{6,14},{7,15},{8,0},{9,1},... | collective-permute-start | bytes 245768 | tf_op jit(solution)/shard_map/ppermute | solution.py:947

commit v8 on v7

--- a/solution.py
+++ b/solution.py
@@ -425,7 +425,7 @@
                         two[2 * q][k] + two[2 * q + 1][k]
                     )
 
-        rows_loop(low, high, body, self.unroll // 2)
+        rows_loop(low, high, body, 2)
 
     def correct(self, target, iterate, coarse, low, high, shift=0):
         count, half = self.phases, self.phases // 2

time: 66.6 us -> 66.5 us (level)
  no operation moved by 1% of the time
where the time goes in v8:
time: 66.5 us; the launch traced here: 65.8 us
  starting transfers between devices  23.8 us (36%)
  Pallas kernels  22 us (33%)
  waiting for transfers between devices  18 us (27%)
  matrix products  0.81 us (1%)
  between operations  0.74 us (1%)
    pallas_call x9, Pallas kernels, call(): pl.pallas_call(kernel, out_shape=outs, in_specs=[pl.BlockSpec(memory_spac...  22 us
    ppermute x10, starting transfers between devices, paired(): result[which] = lax.ppermute(values[which], ('section', 'gx', 'gy'), pairs)  16.1 us
    ppermute x10, waiting for transfers between devices, paired(): result[which] = lax.ppermute(values[which], ('section', 'gx', 'gy'), pairs)  14.1 us
    ppermute x4, starting transfers between devices, turned(): lax.ppermute(value, axis, [(i, (i + shift) % count) for i in range(count)])  7.67 us
    ppermute x4, waiting for transfers between devices, turned(): lax.ppermute(value, axis, [(i, (i + shift) % count) for i in range(count)])  3.9 us
  transfers between devices with their start and end apart: 14, of which 10 were waited for; matrix products, arithmetic and copies ran while one was open for 2% of the time, Pallas kernels for 9%

profile of v8, /device:TPU:1, one launch (start us, length us, event | category | flops | bytes accessed | tf_op | source)
XLA Modules:
  0.0 65.8 jit_solution(478462331216407138)
XLA Ops:
  0.6 1.3 %shard_map.95 = (f32[33,2,8,128]{3,2,1,0:T(8,128)S(1)}, f32[264,64]{1,0:T(8,128)S(1)}, f32[264,64]{1,0:T(8,128)S(1)}) custom-call(f32[64,256]{1,0:T(8,128)} %bitcast.11, f32[64,256]{1,0:T(8,128)} %bitcast.13, s32[64,256]{1,0:T(8,128)} %bitcast.14, s32[56,256]{1,0:T(8,128)} %bitcast.15, s32[8,256]{1,0:T(8,128)} %refs_4_.1, s32[8,256]{1,0:T(8,128)} %refs_5_.1), custom_call_target="tpu_custom_call" | custom-call | tf_op jit(solution)/shard_map/pallas_call | solution.py:917
  2.0 5.1 %collective-permute-start.5 = (f32[33,2,8,128]{3,2,1,0:T(8,128)S(1)}, f32[33,2,8,128]{3,2,1,0:T(8,128)S(1)}, u32[]{:S(2)}, u32[]{:S(2)}) collective-permute-start(f32[33,2,8,128]{3,2,1,0:T(8,128)S(1)} %get-tuple-element.74.own), channel_id=1, source_target_pairs={{0,1},{1,0},{2,3},{3,2},{4,8},{5,9},{6,10},{7,11},{8,4},{9,5},{10,... | collective-permute-start | bytes 811016 | tf_op jit(solution)/shard_map/ppermute | solution.py:947
  7.1 1.6 %collective-permute-start = (f32[264,64]{1,0:T(8,128)S(1)}, f32[264,64]{1,0:T(8,128)S(1)}, u32[]{:S(2)}, u32[]{:S(2)}) collective-permute-start(f32[264,64]{1,0:T(8,128)S(1)} %get-tuple-element.75), channel_id=1, source_target_pairs={{0,1},{1,2},{2,3},{3,0},{4,5},{5,6},{6,7},{7,4},{8,9},{9,10},{10,1... | collective-permute-start | bytes 202760 | tf_op jit(solution)/shard_map/ppermute | solution.py:929
  8.7 2.1 %collective-permute-start.1 = (f32[264,64]{1,0:T(8,128)S(1)}, f32[264,64]{1,0:T(8,128)S(1)}, u32[]{:S(2)}, u32[]{:S(2)}) collective-permute-start(f32[264,64]{1,0:T(8,128)S(1)} %get-tuple-element.76), channel_id=1, source_target_pairs={{0,3},{1,0},{2,1},{3,2},{4,7},{5,4},{6,5},{7,6},{8,11},{9,8},{10,9... | collective-permute-start | bytes 202760 | tf_op jit(solution)/shard_map/ppermute | solution.py:929
  10.9 3.5 %collective-permute-done.from_lower = f32[264,64]{1,0:T(8,128)S(1)} collective-permute-done((f32[264,64]{1,0:T(8,128)S(1)}, f32[264,64]{1,0:T(8,128)S(1)}, u32[]{:S(2)}, u32[]{:S(2)}) %collective-permute-start) | collective-permute-done | bytes 67616 | tf_op jit(solution)/shard_map/ppermute | solution.py:929
  14.4 0.1 collective-permute-done.1.from_upper
  14.5 0.4 shard_map.96.whole
  14.8 1.8 %collective-permute-start.3 = (f32[33,3,8,128]{3,2,1,0:T(8,128)S(1)}, f32[33,3,8,128]{3,2,1,0:T(8,128)S(1)}, u32[]{:S(2)}, u32[]{:S(2)}) collective-permute-start(f32[33,3,8,128]{3,2,1,0:T(8,128)S(1)} %shard_map.96.whole), channel_id=1, source_target_pairs={{0,4},{1,5},{2,6},{3,7},{4,0},{5,1},{6,2},{7,3},{8,16},{9,17},{10,... | collective-permute-start | bytes 1216520 | tf_op jit(solution)/shard_map/ppermute | solution.py:947
  16.7 0.3 collective-permute-done.4.near0
  17.1 0.5 shard_map.97
  17.7 1.7 %collective-permute-start.6 = (f32[33,8,128]{2,1,0:T(8,128)S(1)}, f32[33,8,128]{2,1,0:T(8,128)S(1)}, u32[]{:S(2)}, u32[]{:S(2)}) collective-permute-start(f32[33,8,128]{2,1,0:T(8,128)S(1)} %get-tuple-element.77), channel_id=1, source_target_pairs={{0,1},{1,2},{2,3},{3,0},{4,5},{5,6},{6,7},{7,4},{8,9},{9,10},{10,1... | collective-permute-start | bytes 405512 | tf_op jit(solution)/shard_map/ppermute | solution.py:929
  19.4 2.2 %collective-permute-start.7 = (f32[33,8,128]{2,1,0:T(8,128)S(1)}, f32[33,8,128]{2,1,0:T(8,128)S(1)}, u32[]{:S(2)}, u32[]{:S(2)}) collective-permute-start(f32[33,8,128]{2,1,0:T(8,128)S(1)} %get-tuple-element.78), channel_id=1, source_target_pairs={{0,3},{1,0},{2,1},{3,2},{4,7},{5,4},{6,5},{7,6},{8,11},{9,8},{10,9... | collective-permute-start | bytes 405512 | tf_op jit(solution)/shard_map/ppermute | solution.py:929
  21.6 0.8 %convolution_bitcast_fusion = f32[16,5]{0,1:T(8,128)S(1)} fusion(f32[5,5]{1,0:T(8,128)} %constant.17.clone, f32[16,5]{0,1:T(8,128)S(1)} %copy-done), kind=kOutput, calls=%fused_computation | convolution fusion | flops 4800 | bytes 740 | tf_op jit(solution)/shard_map/tk,jk->tj/dot_general | solution.py:982
  22.4 0.1 copy.40
  22.5 0.1 broadcast_in_dim.7
  22.6 0.1 broadcast_in_dim.8.mixed_table
  22.7 0.9 %shard_map.98 = (f32[40,4,8,128]{3,2,1,0:T(8,128)S(1)}, f32[40,5,8,128]{3,2,1,0:T(8,128)S(1)}, f32[40,4,8,128]{3,2,1,0:T(8,128)S(1)}, f32[40,4,8,128]{3,2,1,0:T(...) custom-call(s32[2,8,128]{2,1,0:T(8,128)S(1)} %stack.6.place, ...), custom_call_target="tpu_custom_call" | custom-call | tf_op jit(solution)/shard_map/pallas_call | solution.py:917
  23.6 0.3 collective-permute-done.6.edge_left
  23.9 3.9 %shard_map.99 = (f32[40,4,8,128]{3,2,1,0:T(8,128)S(1)}, f32[40,5,8,128]{3,2,1,0:T(8,128)S(1)}, f32[40,4,8,128]{3,2,1,0:T(8,128)S(1)}, f32[40,4,8,128]{3,2,1,0:T(...) custom-call(s32[2,8,128]{2,1,0:T(8,128)S(1)} %stack.6.place, ...), custom_call_target="tpu_custom_call", output_to_operand_aliasing={{0}: (6, {}), {1}: (7, {}), {2}: (8, {}), {3}: (9, {}), {4}... | custom-call | tf_op jit(solution)/shard_map/pallas_call | solution.py:917
  27.8 4.4 %shard_map.100 = (f32[40,4,8,128]{3,2,1,0:T(8,128)S(1)}, f32[40,5,8,128]{3,2,1,0:T(8,128)S(1)}, f32[40,4,8,128]{3,2,1,0:T(8,128)S(1)}, f32[40,4,8,128]{3,2,1,0:T...) custom-call(s32[2,8,128]{2,1,0:T(8,128)S(1)} %stack.6.place, ...), custom_call_target="tpu_custom_call", output_to_operand_aliasing={{0}: (4, {}), {1}: (5, {}), {2}: (6, {}), {3}: (7, {}), {4}... | custom-call | tf_op jit(solution)/shard_map/pallas_call | solution.py:917
  32.3 4.6 %collective-permute-start.8 = (f32[29,8,128]{2,1,0:T(8,128)S(1)}, f32[29,8,128]{2,1,0:T(8,128)S(1)}, u32[]{:S(2)}, u32[]{:S(2)}) collective-permute-start(f32[29,8,128]{2,1,0:T(8,128)S(1)} %get-tuple-element.131), channel_id=1, source_target_pairs={{0,4},{1,5},{2,6},{3,7},{4,0},{5,1},{6,2},{7,3},{8,16},{9,17},{10,... | collective-permute-start | bytes 356360 | tf_op jit(solution)/shard_map/ppermute | solution.py:947
  36.9 2.5 %collective-permute-done.8.refs_23_ = f32[29,8,128]{2,1,0:T(8,128)S(1)} collective-permute-done((f32[29,8,128]{2,1,0:T(8,128)S(1)}, f32[29,8,128]{2,1,0:T(8,128)S(1)}, u32[]{:S(2)}, u32[]{:S(2)}) %collective-permute-start.8) | collective-permute-done | bytes 118816 | tf_op jit(solution)/shard_map/ppermute | solution.py:947
  39.4 2.7 %collective-permute-done.9.refs_24_ = f32[29,8,128]{2,1,0:T(8,128)S(1)} collective-permute-done((f32[29,8,128]{2,1,0:T(8,128)S(1)}, f32[29,8,128]{2,1,0:T(8,128)S(1)}, u32[]{:S(2)}, u32[]{:S(2)}) %collective-permute-start.9) | collective-permute-done | bytes 118816 | tf_op jit(solution)/shard_map/ppermute | solution.py:947
  42.1 6.0 %shard_map.101 = (f32[40,20,8,128]{3,2,1,0:T(8,128)S(1)}, f32[40,8,128]{2,1,0:T(8,128)S(1)}, f32[25,8,128]{2,1,0:T(8,128)S(1)}, f32[15,1,8,128]{3,2,1,0:T(8,128)...) custom-call(s32[2,8,128]{2,1,0:T(8,128)S(1)} %stack.6.place, ...), custom_call_target="tpu_custom_call" | custom-call | tf_op jit(solution)/shard_map/pallas_call | solution.py:917
  48.0 2.3 %collective-permute-start.11 = (f32[25,8,128]{2,1,0:T(8,128)S(1)}, f32[25,8,128]{2,1,0:T(8,128)S(1)}, u32[]{:S(2)}, u32[]{:S(2)}) collective-permute-start(f32[25,8,128]{2,1,0:T(8,128)S(1)} %get-tuple-element.135), channel_id=1, source_target_pairs={{0,1},{1,0},{2,3},{3,2},{4,8},{5,9},{6,10},{7,11},{8,4},{9,5},{10,... | collective-permute-start | bytes 307208 | tf_op jit(solution)/shard_map/ppermute | solution.py:947
  50.3 4.3 %collective-permute-done.11.refs_9_ = f32[25,8,128]{2,1,0:T(8,128)S(1)} collective-permute-done((f32[25,8,128]{2,1,0:T(8,128)S(1)}, f32[25,8,128]{2,1,0:T(8,128)S(1)}, u32[]{:S(2)}, u32[]{:S(2)}) %collective-permute-start.11) | collective-permute-done | bytes 102432 | tf_op jit(solution)/shard_map/ppermute | solution.py:947
  54.6 0.6 collective-permute-done.10.refs_8_
  55.2 1.0 %shard_map.102 = (f32[20,10,8,128]{3,2,1,0:T(8,128)S(1)}, f32[20,10,8,128]{3,2,1,0:T(8,128)S(1)}, f32[4,5,8,128]{3,2,1,0:T(8,128)S(1)}) custom-call(s32[2,8,128]{2,1,0:T(8,128)S(1)} %stack.6.place, f32[20,2,8,128]{3,2,1,0:T(8,128)S(1)} %get-tuple-element.117.refs_9_.refs_0_.refs_7_, f32[20,3,8,128]{3,2,1,0:T(8,128)S(1)} %get-tuple-element.118.refs_10_.refs_1_.refs_8_, ...), custom_call_target="tpu_custom_call" | custom-call | tf_op jit(solution)/shard_map/pallas_call | solution.py:917
  56.1 2.3 %collective-permute-start.13 = (f32[4,5,8,128]{3,2,1,0:T(8,128)S(1)}, f32[4,5,8,128]{3,2,1,0:T(8,128)S(1)}, u32[]{:S(2)}, u32[]{:S(2)}) collective-permute-start(f32[4,5,8,128]{3,2,1,0:T(8,128)S(1)} %get-tuple-element.143.refs_19_), channel_id=1, source_target_pairs={{0,4},{1,5},{2,6},{3,7},{4,0},{5,1},{6,2},{7,3},{8,16},{9,17},{10,... | collective-permute-start | bytes 245768 | tf_op jit(solution)/shard_map/ppermute | solution.py:947
  58.4 2.9 %collective-permute-done.13.refs_21_ = f32[4,5,8,128]{3,2,1,0:T(8,128)S(1)} collective-permute-done((f32[4,5,8,128]{3,2,1,0:T(8,128)S(1)}, f32[4,5,8,128]{3,2,1,0:T(8,128)S(1)}, u32[]{:S(2)}, u32[]{:S(2)}) %collective-permute-start.13) | collective-permute-done | bytes 81952 | tf_op jit(solution)/shard_map/ppermute | solution.py:947
  61.3 0.9 %collective-permute-done.12.refs_20_ = f32[4,5,8,128]{3,2,1,0:T(8,128)S(1)} collective-permute-done((f32[4,5,8,128]{3,2,1,0:T(8,128)S(1)}, f32[4,5,8,128]{3,2,1,0:T(8,128)S(1)}, u32[]{:S(2)}, u32[]{:S(2)}) %collective-permute-start.12) | collective-permute-done | bytes 81952 | tf_op jit(solution)/shard_map/ppermute | solution.py:947
  62.2 3.6 %shard_map.103 = (f32[5,64,256]{2,1,0:T(8,128)}, f32[64,256]{1,0:T(8,128)}) custom-call(s32[2,8,128]{2,1,0:T(8,128)S(1)} %stack.6.place, f32[40,4,8,128]{3,2,1,0:T(8,128)S(1)} %get-tuple-element.108.refs_0_, f32[40,5,8,128]{3,2,1,0:T(8,128)S(1)} %get-tuple-element.109.refs_1_, f32[40,4,8,128]{3,2,1,0:T(8,128)S(1)} %get-tuple-element.110.refs_2_, ...), custom_call_target="tpu_custom_call" | custom-call | tf_op jit(solution)/shard_map/pallas_call | solution.py:917
  (15 shorter events, 0.1 us)
Async XLA Ops:
  0.6 20.9 %copy-start = (f32[16,5]{0,1:T(8,128)S(1)}, f32[16,5]{0,1:T(8,128)}, u32[]{:S(2)}) copy-start(f32[16,5]{0,1:T(8,128)} %param.14) | copy-start | bytes 964
  2.0 14.7 %collective-permute-start.5 = (f32[33,2,8,128]{3,2,1,0:T(8,128)S(1)}, f32[33,2,8,128]{3,2,1,0:T(8,128)S(1)}, u32[]{:S(2)}, u32[]{:S(2)}) collective-permute-start(f32[33,2,8,128]{3,2,1,0:T(8,128)S(1)} %get-tuple-element.74.own), channel_id=1, source_target_pairs={{0,1},{1,0},{2,3},{3,2},{4,8},{5,9},{6,10},{7,11},{8,4},{9,5},{10,... | collective-permute-start | bytes 811016 | tf_op jit(solution)/shard_map/ppermute | solution.py:947
  7.1 9.9 %collective-permute-start.4 = (f32[33,2,8,128]{3,2,1,0:T(8,128)S(1)}, f32[33,2,8,128]{3,2,1,0:T(8,128)S(1)}, u32[]{:S(2)}, u32[]{:S(2)}) collective-permute-start(f32[33,2,8,128]{3,2,1,0:T(8,128)S(1)} %get-tuple-element.74.own), channel_id=1, source_target_pairs={{0,4},{1,5},{2,6},{3,7},{4,0},{5,1},{6,2},{7,3},{8,12},{9,13},{10,... | collective-permute-start | bytes 811016 | tf_op jit(solution)/shard_map/ppermute | solution.py:947
  7.1 7.3 %collective-permute-start = (f32[264,64]{1,0:T(8,128)S(1)}, f32[264,64]{1,0:T(8,128)S(1)}, u32[]{:S(2)}, u32[]{:S(2)}) collective-permute-start(f32[264,64]{1,0:T(8,128)S(1)} %get-tuple-element.75), channel_id=1, source_target_pairs={{0,1},{1,2},{2,3},{3,0},{4,5},{5,6},{6,7},{7,4},{8,9},{9,10},{10,1... | collective-permute-start | bytes 202760 | tf_op jit(solution)/shard_map/ppermute | solution.py:929
  8.7 5.7 %collective-permute-start.1 = (f32[264,64]{1,0:T(8,128)S(1)}, f32[264,64]{1,0:T(8,128)S(1)}, u32[]{:S(2)}, u32[]{:S(2)}) collective-permute-start(f32[264,64]{1,0:T(8,128)S(1)} %get-tuple-element.76), channel_id=1, source_target_pairs={{0,3},{1,0},{2,1},{3,2},{4,7},{5,4},{6,5},{7,6},{8,11},{9,8},{10,9... | collective-permute-start | bytes 202760 | tf_op jit(solution)/shard_map/ppermute | solution.py:929
  14.8 13.0 %collective-permute-start.3 = (f32[33,3,8,128]{3,2,1,0:T(8,128)S(1)}, f32[33,3,8,128]{3,2,1,0:T(8,128)S(1)}, u32[]{:S(2)}, u32[]{:S(2)}) collective-permute-start(f32[33,3,8,128]{3,2,1,0:T(8,128)S(1)} %shard_map.96.whole), channel_id=1, source_target_pairs={{0,4},{1,5},{2,6},{3,7},{4,0},{5,1},{6,2},{7,3},{8,16},{9,17},{10,... | collective-permute-start | bytes 1216520 | tf_op jit(solution)/shard_map/ppermute | solution.py:947
  16.7 11.1 %collective-permute-start.2 = (f32[33,3,8,128]{3,2,1,0:T(8,128)S(1)}, f32[33,3,8,128]{3,2,1,0:T(8,128)S(1)}, u32[]{:S(2)}, u32[]{:S(2)}) collective-permute-start(f32[33,3,8,128]{3,2,1,0:T(8,128)S(1)} %shard_map.96.whole), channel_id=1, source_target_pairs={{0,8},{1,9},{2,10},{3,11},{4,12},{5,13},{6,14},{7,15},{8,0},{9,1},... | collective-permute-start | bytes 1216520 | tf_op jit(solution)/shard_map/ppermute | solution.py:947
  17.7 6.2 %collective-permute-start.6 = (f32[33,8,128]{2,1,0:T(8,128)S(1)}, f32[33,8,128]{2,1,0:T(8,128)S(1)}, u32[]{:S(2)}, u32[]{:S(2)}) collective-permute-start(f32[33,8,128]{2,1,0:T(8,128)S(1)} %get-tuple-element.77), channel_id=1, source_target_pairs={{0,1},{1,2},{2,3},{3,0},{4,5},{5,6},{6,7},{7,4},{8,9},{9,10},{10,1... | collective-permute-start | bytes 405512 | tf_op jit(solution)/shard_map/ppermute | solution.py:929
  19.4 4.5 %collective-permute-start.7 = (f32[33,8,128]{2,1,0:T(8,128)S(1)}, f32[33,8,128]{2,1,0:T(8,128)S(1)}, u32[]{:S(2)}, u32[]{:S(2)}) collective-permute-start(f32[33,8,128]{2,1,0:T(8,128)S(1)} %get-tuple-element.78), channel_id=1, source_target_pairs={{0,3},{1,0},{2,1},{3,2},{4,7},{5,4},{6,5},{7,6},{8,11},{9,8},{10,9... | collective-permute-start | bytes 405512 | tf_op jit(solution)/shard_map/ppermute | solution.py:929
  32.3 7.1 %collective-permute-start.8 = (f32[29,8,128]{2,1,0:T(8,128)S(1)}, f32[29,8,128]{2,1,0:T(8,128)S(1)}, u32[]{:S(2)}, u32[]{:S(2)}) collective-permute-start(f32[29,8,128]{2,1,0:T(8,128)S(1)} %get-tuple-element.131), channel_id=1, source_target_pairs={{0,4},{1,5},{2,6},{3,7},{4,0},{5,1},{6,2},{7,3},{8,16},{9,17},{10,... | collective-permute-start | bytes 356360 | tf_op jit(solution)/shard_map/ppermute | solution.py:947
  36.9 5.2 %collective-permute-start.9 = (f32[29,8,128]{2,1,0:T(8,128)S(1)}, f32[29,8,128]{2,1,0:T(8,128)S(1)}, u32[]{:S(2)}, u32[]{:S(2)}) collective-permute-start(f32[29,8,128]{2,1,0:T(8,128)S(1)} %get-tuple-element.132), channel_id=1, source_target_pairs={{0,8},{1,9},{2,10},{3,11},{4,12},{5,13},{6,14},{7,15},{8,0},{9,1},... | collective-permute-start | bytes 356360 | tf_op jit(solution)/shard_map/ppermute | solution.py:947
  42.1 20.1 %copy-start.1 = (f32[8,8,256]{2,1,0:T(8,128)S(1)}, f32[8,8,256]{2,1,0:T(8,128)}, u32[]{:S(2)}) copy-start(f32[8,8,256]{2,1,0:T(8,128)} %param.8) | copy-start | bytes 196612
  48.0 6.5 %collective-permute-start.11 = (f32[25,8,128]{2,1,0:T(8,128)S(1)}, f32[25,8,128]{2,1,0:T(8,128)S(1)}, u32[]{:S(2)}, u32[]{:S(2)}) collective-permute-start(f32[25,8,128]{2,1,0:T(8,128)S(1)} %get-tuple-element.135), channel_id=1, source_target_pairs={{0,1},{1,0},{2,3},{3,2},{4,8},{5,9},{6,10},{7,11},{8,4},{9,5},{10,... | collective-permute-start | bytes 307208 | tf_op jit(solution)/shard_map/ppermute | solution.py:947
  50.3 4.9 %collective-permute-start.10 = (f32[25,8,128]{2,1,0:T(8,128)S(1)}, f32[25,8,128]{2,1,0:T(8,128)S(1)}, u32[]{:S(2)}, u32[]{:S(2)}) collective-permute-start(f32[25,8,128]{2,1,0:T(8,128)S(1)} %get-tuple-element.135), channel_id=1, source_target_pairs={{0,4},{1,5},{2,6},{3,7},{4,0},{5,1},{6,2},{7,3},{8,12},{9,13},{10,... | collective-permute-start | bytes 307208 | tf_op jit(solution)/shard_map/ppermute | solution.py:947
  56.1 5.2 %collective-permute-start.13 = (f32[4,5,8,128]{3,2,1,0:T(8,128)S(1)}, f32[4,5,8,128]{3,2,1,0:T(8,128)S(1)}, u32[]{:S(2)}, u32[]{:S(2)}) collective-permute-start(f32[4,5,8,128]{3,2,1,0:T(8,128)S(1)} %get-tuple-element.143.refs_19_), channel_id=1, source_target_pairs={{0,4},{1,5},{2,6},{3,7},{4,0},{5,1},{6,2},{7,3},{8,16},{9,17},{10,... | collective-permute-start | bytes 245768 | tf_op jit(solution)/shard_map/ppermute | solution.py:947
  58.4 3.7 %collective-permute-start.12 = (f32[4,5,8,128]{3,2,1,0:T(8,128)S(1)}, f32[4,5,8,128]{3,2,1,0:T(8,128)S(1)}, u32[]{:S(2)}, u32[]{:S(2)}) collective-permute-start(f32[4,5,8,128]{3,2,1,0:T(8,128)S(1)} %get-tuple-element.143.refs_19_), channel_id=1, source_target_pairs={{0,8},{1,9},{2,10},{3,11},{4,12},{5,13},{6,14},{7,15},{8,0},{9,1},... | collective-permute-start | bytes 245768 | tf_op jit(solution)/shard_map/ppermute | solution.py:947
